TPU v7x, 32 devices: a whole 2x2x4 slice. The times are simulated.
32 devices in a mesh: leaf: 8 (over z, y), row: 2 (over core), col: 2 (over x).
Axes of the slice: x: 2, y: 2, z: 4, core: 2. Of those that a mesh axis runs over, the one named last changes fastest.
Arguments:
- sigma_top: float32 [4096, 4096], P('row', ('leaf', 'col'))
- structure: int32 [8, 16], replicated, may hold values from 0 to 31, as said below
- lower: float32 [8, 2048, 2048], P('leaf', 'row', 'col'), may hold values from -0.25 to 0.25
- dinv: float32 [8, 2048, 2048], P('leaf', 'row', 'col'), may hold values from -6 to 6
Outputs:
- sigma_sj: float32 [8, 2048, 2048], P('leaf', 'row', 'col')
- sigma_jj: float32 [8, 2048, 2048], P('leaf', 'row', 'col')
Inputs may be any that keep to these rules, and one draw needn't show every extreme that they name: `structure`: each row lists 16 distinct tiles in increasing order and always holds tile 0 and tile 32 - 1.
All inputs are finite; a program needn't handle non-finite values.
Results may differ from a plain program's by a relative error of at most 0.0003.
Values sent between devices are 32-bit elements; how exact they have to be, the bound alone decides.
No kernel may reach another device: no remote copies, remote signals or barrier semaphores. Data moves between devices by JAX's collectives and lax.ppermute only.
A program may use at most 192 MiB of HBM per device.

v0:
```python
import jax
import jax.numpy as jnp
from jax import lax
from jax.sharding import PartitionSpec as P

TILE = 128


def body(sigma_top, structure, lower, dinv):
    factor_block = lower[0]
    diag_inverse = dinv[0]
    struct_rows = factor_block.shape[0]
    n_row = lax.axis_size("row")
    n_col = lax.axis_size("col")
    total_rows = struct_rows * n_row
    root_rows = sigma_top.shape[0]
    within = jnp.arange(TILE, dtype=jnp.int32)
    all_indices = (structure[:, :, None] * TILE + within[None, None, :]).reshape(
        structure.shape[0], -1
    )
    leaf_index = lax.axis_index("leaf")
    own_indices = lax.dynamic_index_in_dim(all_indices, leaf_index, 0, keepdims=False)
    first_root_row = lax.axis_index("row") * root_rows
    quarter = total_rows // n_col
    wanted_cols = lax.dynamic_slice_in_dim(own_indices, lax.axis_index("col") * quarter, quarter)
    empty_cols = jnp.zeros((root_rows, quarter), jnp.float32)
    shard_piece = lax.all_gather(sigma_top, ("leaf", "col"), axis=1, tiled=True)
    piece_width = shard_piece.shape[1]
    inside = (wanted_cols >= 0) & (wanted_cols < piece_width)
    values = jnp.take(shard_piece, jnp.clip(wanted_cols, 0, piece_width - 1), axis=1)
    picked_cols = jnp.where(inside[None, :], values, empty_cols)
    wanted = own_indices - first_root_row
    inside = (wanted >= 0) & (wanted < root_rows)
    values = jnp.take(picked_cols, jnp.clip(wanted, 0, root_rows - 1), axis=0)
    sigma_block = lax.psum_scatter(
        jnp.where(inside[:, None], values, 0.0), "row", scatter_dimension=0, tiled=True
    )
    row_panel = lax.all_gather(sigma_block, "col", axis=1, tiled=True)
    cross = -jnp.dot(
        row_panel,
        lax.all_gather(factor_block, "row", axis=0, tiled=True),
        precision=lax.Precision.HIGHEST,
        preferred_element_type=jnp.float32,
    )
    factor_rows = lax.all_gather(factor_block, "col", axis=1, tiled=True)
    front = diag_inverse + lax.psum_scatter(
        -lax.dot_general(
            factor_rows,
            cross,
            (((0,), (0,)), ((), ())),
            precision=lax.Precision.HIGHEST,
            preferred_element_type=jnp.float32,
        ),
        "row",
        scatter_dimension=0,
        tiled=True,
    )
    return (cross[None], front[None])


def solution(mesh):
    placed = (P("row", ("leaf", "col")), P(), P("leaf", "row", "col"), P("leaf", "row", "col"))
    return jax.shard_map(
        body,
        mesh=mesh,
        in_specs=placed,
        out_specs=(P("leaf", "row", "col"), P("leaf", "row", "col")),
        check_vma=False,
    )
```

profile of v0, /device:TPU:1, one launch (start us, length us, event | category | flops | bytes accessed | tf_op | source)
XLA Modules:
  0.0 738.1 jit_solution(9349008275643625200)
XLA Ops:
  7.2 0.0 all-gather.7.cloned.1.call-start
  7.2 2.9 copy.11
  10.1 0.0 all-gather.7.cloned.1.call-update
  10.1 0.0 reduce-scatter.3.cloned.1.call-start
  10.2 0.7 broadcast_multiply_fusion
  10.9 0.1 copy.10
  10.9 0.1 bitcast_add_fusion.1
  11.0 0.1 and_reduce_fusion.1
  11.1 0.1 and_reduce_fusion
  11.2 0.1 compare_select_fusion.1
  11.4 352.5 %all-gather.7.cloned.1.call-done = f32[2048,4096]{0,1:T(8,128)} async-done(((f32[2048,256]{0,1:T(8,128)}), f32[2048,4096]{0,1:T(8,128)}) %all-gather.7.cloned.1.call-update) | async-done | bytes 33554448 | tf_op jit(solution)/shard_map/all_gather | solution.py:27
  363.9 19.6 %gather_fusion = f32[1024,2048]{1,0:T(8,128)} fusion(f32[2048,4096]{0,1:T(8,128)} %all-gather.7.cloned.1.call-done, s32[1024]{0:T(1024)S(1)} %broadcast_clamp_fusion.2), kind=kCustom, calls=%fused_computation | custom fusion | bytes 16781312 | tf_op jit(solution)/shard_map/jit(_take)/gather | solution.py:30
  383.5 6.2 select_bitcast_fusion
  389.7 9.3 %copy.12 = f32[2048,1024]{1,0:T(8,128)} copy(f32[2048,1024]{0,1:T(8,128)} %select_bitcast_fusion) | data formatting | bytes 16777216 | tf_op jit(solution)/shard_map/jit(_where)/select_n | solution.py:31
  399.0 15.1 %gather_fusion.1 = f32[2048,1024]{1,0:T(8,128)} fusion(f32[2048,1024]{1,0:T(8,128)} %copy.12, s32[2048]{0:T(1024)S(1)} %broadcast_clamp_fusion), kind=kCustom, calls=%fused_computation.1 | custom fusion | bytes 16785408 | tf_op jit(solution)/shard_map/jit(_take)/gather | solution.py:34
  414.1 5.9 select_select_fusion
  420.0 0.0 reduce-scatter.3.cloned.1.call-update
  420.0 0.0 all-gather.11.cloned.1.call-start
  420.1 0.7 all-gather.11.cloned.1.call-update
  420.8 0.0 all-gather.9.cloned.1.call-start
  420.8 15.2 %reduce-scatter.3.cloned.1.call-done = f32[1024,1024]{1,0:T(8,128)} async-done(((f32[2048,1024]{1,0:T(8,128)}), f32[1024,1024]{1,0:T(8,128)}) %reduce-scatter.3.cloned.1.call-update) | async-done | bytes 4194320 | tf_op jit(solution)/shard_map/reduce_scatter | solution.py:35
  436.1 0.0 all-gather.9.cloned.1.call-update
  436.1 0.0 all-gather.13.cloned.1.call-start
  436.1 0.5 all-gather.13.cloned.1.call-update
  436.7 0.0 reduce-scatter.5.cloned.1.call-start
  436.7 22.0 %all-gather.11.cloned.1.call-done = f32[1,2048,1024]{2,1,0:T(8,128)} async-done(((f32[1,1024,1024]{2,1,0:T(8,128)}), f32[1,2048,1024]{2,1,0:T(8,128)}) %all-gather.11.cloned.1.call-update) | async-done | bytes 8388624 | tf_op jit(solution)/shard_map/all_gather | solution.py:41
  458.7 106.3 %all-gather.9.cloned.1.call-done = f32[1024,2048]{1,0:T(8,128)} async-done(((f32[1024,1024]{1,0:T(8,128)}), f32[1024,2048]{1,0:T(8,128)}) %all-gather.9.cloned.1.call-update) | async-done | bytes 8388624 | tf_op jit(solution)/shard_map/all_gather | solution.py:38
  565.0 31.8 %fusion.2 = f32[1024,1024]{1,0:T(8,128)} fusion(f32[1024,2048]{1,0:T(8,128)} %all-gather.9.cloned.1.call-done, f32[1,2048,1024]{2,1,0:T(8,128)} %all-gather.11.cloned.1.call-done), kind=kOutput, calls=%fused_computation.4 | convolution fusion | flops 25769803776 | bytes 20971520 | tf_op jit(solution)/shard_map/dot_general | solution.py:39
  596.9 73.7 %all-gather.13.cloned.1.call-done = f32[1,1024,2048]{2,1,0:T(8,128)} async-done(((f32[1,1024,1024]{2,1,0:T(8,128)}), f32[1,1024,2048]{2,1,0:T(8,128)}) %all-gather.13.cloned.1.call-update) | async-done | bytes 8388624 | tf_op jit(solution)/shard_map/all_gather | solution.py:45
  670.6 31.2 %negate_bitcast_fusion = f32[2048,1024]{0,1:T(8,128)} fusion(f32[1,1024,2048]{2,1,0:T(8,128)} %all-gather.13.cloned.1.call-done, f32[1024,1024]{1,0:T(8,128)} %fusion.2), kind=kOutput, calls=%fused_computation.7 | convolution fusion | flops 25772949504 | bytes 20971520 | tf_op jit(solution)/shard_map/dot_general | solution.py:47
  701.7 0.0 reduce-scatter.5.cloned.1.call-update
  701.7 5.4 copy.13
  707.1 6.2 negate_bitcast_fusion.1
  713.3 5.9 reduce-scatter.5.cloned.1.call-done
  719.2 6.8 fusion.6
  725.9 5.3 copy.14
  (6 shorter events, 0.1 us)
Async XLA Ops:
  7.2 356.7 %all-gather.7.cloned.1.call-start = ((), (), s32[]{:S(2)}) async-start(), calls=%async_computation.2 | async-start | bytes 35651584 | tf_op jit(solution)/shard_map/all_gather | solution.py:27
  10.1 425.9 %reduce-scatter.3.cloned.1.call-start = ((), (), s32[]{:S(2)}) async-start(), calls=%async_computation.3 | async-start | bytes 12582912 | tf_op jit(solution)/shard_map/reduce_scatter | solution.py:35
  420.0 38.7 %all-gather.11.cloned.1.call-start = ((), (), s32[]{:S(2)}) async-start(), calls=%async_computation.6 | async-start | bytes 12582912 | tf_op jit(solution)/shard_map/all_gather | solution.py:41
  420.8 144.3 %all-gather.9.cloned.1.call-start = ((), (), s32[]{:S(2)}) async-start(), calls=%async_computation.4 | async-start | bytes 12582912 | tf_op jit(solution)/shard_map/all_gather | solution.py:38
  436.1 234.5 %all-gather.13.cloned.1.call-start = ((), (), s32[]{:S(2)}) async-start(), calls=%async_computation.7 | async-start | bytes 12582912 | tf_op jit(solution)/shard_map/all_gather | solution.py:45
  436.7 282.5 %reduce-scatter.5.cloned.1.call-start = ((), (), s32[]{:S(2)}) async-start(), calls=%async_computation.5 | async-start | bytes 12582912 | tf_op jit(solution)/shard_map/reduce_scatter | solution.py:46
Sparse Core Ops, SparseCore 0:
  11.3 352.5 all-gather.6
  420.2 15.8 reduce-scatter.2
  437.7 21.0 all-gather.10
  460.2 104.7 all-gather.8
  566.5 103.9 all-gather.12
  701.9 17.2 reduce-scatter.4
where the time goes:
time: 739 us; the launch traced here: 738 us
  waiting for transfers between devices  577 us (78%)
  matrix products  63 us (9%)
  local copies, waits for them, and re-layouts  57.6 us (8%)
  other arithmetic  26.2 us (4%)
  between operations  14.2 us (2%)
    all_gather x1, waiting for transfers between devices, body(): shard_piece = lax.all_gather(sigma_top, ('leaf', 'col'), axis=1, tiled=True)  353 us
    all_gather x1, waiting for transfers between devices, body(): row_panel = lax.all_gather(sigma_block, 'col', axis=1, tiled=True)  106 us
    all_gather x1, waiting for transfers between devices, body(): factor_rows = lax.all_gather(factor_block, 'col', axis=1, tiled=True)  73.7 us
    dot_general x1, matrix products, body(): jnp.dot(row_panel, lax.all_gather(factor_block, 'row', axis=0, tiled=True...  31.8 us
    dot_general x1, matrix products, body(): lax.dot_general(factor_rows, cross, (((0,), (0,)), ((), ())), precision=l...  31.2 us
    all_gather x1, waiting for transfers between devices, body(): lax.all_gather(factor_block, 'row', axis=0, tiled=True)  22 us
    gather x1, local copies, waits for them, and re-layouts, body(): jnp.take(shard_piece, jnp.clip(wanted_cols, 0, piece_width - 1), axis=1)  19.6 us
    reduce_scatter x1, waiting for transfers between devices, body(): lax.psum_scatter(jnp.where(inside[:, None], values, 0.0), 'row', scatter_...  15.2 us
  transfers between devices with their start and end apart: 6, of which 6 were waited for; matrix products, arithmetic and copies ran while one was open for 6% of the time, Pallas kernels for 0%

commit v1 on v0

v1 whole, which is shorter than its diff:
```python
import jax
import jax.numpy as jnp
from jax import lax
from jax.experimental import pallas as pl
from jax.experimental.pallas import tpu as pltpu
from jax.sharding import Mesh
from jax.sharding import PartitionSpec as P

TILE = 128
HALF = "half"
LOW = "low"


def swap(x, axis, bit):
    size = lax.axis_size(axis)
    return lax.ppermute(x, axis, [(i, i ^ bit) for i in range(size)])


def select_kernel(n_out, per_src, row_core, row_tile, col_half, col_src, col_lane, *refs):
    pieces = refs[:4]
    outs = refs[4 : 4 + n_out]
    table, sems = refs[4 + n_out :]
    copies = [
        pltpu.make_async_copy(pieces[i], table.at[i // 2, i % 2], sems.at[i]) for i in range(4)
    ]
    for copy in copies:
        copy.start()
    for copy in copies:
        copy.wait()
    n_p = outs[0].shape[0]
    n_q = outs[0].shape[2] // TILE
    for child in range(n_out):

        @pl.loop(0, n_p)
        def _(p, child=child):
            core = row_core[child, p]
            tile = row_tile[child, p]
            for q in range(n_q):
                lane = pl.multiple_of(col_lane[child, q], TILE)
                outs[child][p, :, q * TILE : (q + 1) * TILE] = table[
                    core, col_half[child, q], col_src[child, q], tile, :, pl.ds(lane, TILE)
                ]


def select(pieces, rows, cols, row_id, half_id, n_row):
    n_src, rt, k, width = pieces[0].shape
    n_out, n_q = cols.shape
    per_src = width // TILE
    half_cols = n_src * per_src
    tables = (
        (rows // rt) ^ row_id,
        rows % rt,
        (cols // half_cols) ^ half_id,
        cols % half_cols // per_src,
        cols % per_src * TILE,
    )
    n_p = rows.shape[1]
    out = jax.ShapeDtypeStruct((n_p, k, n_q * TILE), jnp.float32)
    return pl.pallas_call(
        lambda *refs: select_kernel(n_out, per_src, *refs),
        out_shape=[out] * n_out,
        grid_spec=pltpu.PrefetchScalarGridSpec(
            num_scalar_prefetch=5,
            grid=(1,),
            in_specs=[pl.BlockSpec(memory_space=pl.ANY)] * 4,
            out_specs=[pl.BlockSpec((n_p, k, n_q * TILE), lambda i, *_: (0, 0, 0))] * n_out,
            scratch_shapes=[
                pltpu.VMEM((2, 2) + pieces[0].shape, jnp.float32),
                pltpu.SemaphoreType.DMA((4,)),
            ],
        ),
        compiler_params=pltpu.CompilerParams(vmem_limit_bytes=32 << 20),
        cost_estimate=pl.CostEstimate(
            flops=0, transcendentals=0, bytes_accessed=2 * 4 * n_out * n_p * k * n_q * TILE
        ),
    )(*tables, *pieces)


def dot(a, b):
    return jnp.dot(a, b, precision=lax.Precision.HIGH, preferred_element_type=jnp.float32)


def body(sigma_top, structure, lower, dinv):
    own = lower[0]
    half_id, low_id = lax.axis_index(HALF), lax.axis_index(LOW)
    row_id, col_id = lax.axis_index("row"), lax.axis_index("col")
    n_low, n_row, n_col = lax.axis_size(LOW), lax.axis_size("row"), lax.axis_size("col")
    groups = n_low * n_col
    per = TILE // groups
    n_ch = 2 if per % 16 == 0 else 1
    k = per // n_ch
    rt, width = sigma_top.shape[0] // TILE, sigma_top.shape[1]
    n_q = structure.shape[1]
    n_p = n_q // n_row
    s_rows, s_cols = own.shape

    near = half_id * n_low + (low_id ^ jnp.arange(n_low, dtype=jnp.int32))
    lists = jnp.take(structure, near, axis=0)
    mine = lax.dynamic_slice_in_dim(lists, row_id * n_p, n_p, axis=1)
    other = lax.dynamic_slice_in_dim(lists, (1 - row_id) * n_p, n_p, axis=1)
    cols = jnp.concatenate([mine, other], axis=1)

    parts = sigma_top.reshape(rt, groups, n_ch, k, width)
    got = []
    for ch in range(n_ch):
        send = parts[:, :, ch].transpose(1, 0, 2, 3)
        got.append(lax.all_to_all(send, (LOW, "col"), 0, 0, tiled=False))
    merge = max(1, TILE // width)
    if merge > 1:
        got = [
            g.reshape(groups // merge, merge, rt, k, width)
            .transpose(0, 2, 3, 1, 4)
            .reshape(groups // merge, rt, k, merge * width)
            for g in got
        ]

    own_x = swap(own, "col", 1)
    own_p = swap(own, "row", 1)

    s_mine, s_theirs = [], []
    panels = []
    for g in got:
        far = swap(g, HALF, 1)
        near_core = swap(g, "row", 1)
        far_core = swap(far, "row", 1)
        chosen = select((g, far, near_core, far_core), mine, cols, row_id, half_id, n_row)
        blocks = [chosen[0]] + [swap(chosen[s], LOW, s) for s in range(1, n_low)]
        panels.append(jnp.stack(blocks).reshape(-1, n_q * TILE))
    own_xp = swap(own_x, "row", 1)
    keep, sent = [], []
    for m in panels:
        a, b = m[:, :s_rows], m[:, s_rows:]
        out = -(dot(a, own_x) + dot(b, own_xp))
        sent.append(swap(out, "col", 1))
        keep.append(-(dot(a, own) + dot(b, own_p)))

    def place(blocks):
        full = [x.reshape(n_low, n_p, k, s_cols) for x in blocks]
        srcs = []
        for src in range(n_low):
            at = low_id ^ src
            srcs.append(
                jnp.stack(
                    [lax.dynamic_index_in_dim(x, at, 0, keepdims=False) for x in full], axis=1
                )
            )
        return jnp.stack(srcs, axis=1)

    kept, came = place(keep), place(sent)
    first = col_id == 0
    cross = jnp.stack([jnp.where(first, kept, came), jnp.where(first, came, kept)], axis=2)
    cross = cross.reshape(s_rows, s_cols)
    cross_p = swap(cross, "row", 1)
    same = row_id == col_id
    left = jnp.where(same, own, own_x)
    left_p = jnp.where(same, own_p, own_xp)
    dims = (((0,), (0,)), ((), ()))

    def tdot(a, b):
        return lax.dot_general(
            a, b, dims, precision=lax.Precision.HIGH, preferred_element_type=jnp.float32
        )

    front = dinv[0] - tdot(left, cross) - tdot(left_p, cross_p)
    return (cross[None], front[None])


def solution(mesh):
    n_leaf, n_row, n_col = (mesh.shape[a] for a in ("leaf", "row", "col"))
    fine = Mesh(
        mesh.devices.reshape(2, n_leaf // 2, n_row, n_col), (HALF, LOW, "row", "col")
    )
    leaf = (HALF, LOW)
    block = P(leaf, "row", "col")
    return jax.shard_map(
        body,
        mesh=fine,
        in_specs=(P("row", leaf + ("col",)), P(), block, block),
        out_specs=(block, block),
        check_vma=False,
    )
```

time: 739 us -> 326 us (0.44)
  waiting for transfers between devices: 577 us -> 221 us
  local copies, waits for them, and re-layouts: 57.6 us -> 6.44 us
  starting transfers between devices: 0.24 us -> 29.1 us
  other arithmetic: 26.2 us -> 5.48 us
  between operations: 14.2 us -> 0.96 us
  matrix products: 63 us -> 52.9 us
  Pallas kernels: 0 us -> 10 us
    all_gather x4 -> x0, waiting for transfers between devices: 555 us -> none  [the longest x1 353 us: body(): shard_piece = lax.all_gather(sigma_top, ('leaf', 'col'), axis=1, tiled=True)]
    ppermute x0 -> x18, waiting for transfers between devices: none -> 117 us  [swap(): return lax.ppermute(x, axis, [(i, i ^ bit) for i in range(size)])]
    all_to_all x0 -> x2, waiting for transfers between devices: none -> 103 us  [body(): got.append(lax.all_to_all(send, (LOW, 'col'), 0, 0, tiled=False))]
    gather x2 -> x1, local copies, waits for them, and re-layouts: 34.7 us -> 0.56 us  [body(): lists = jnp.take(structure, near, axis=0)]
    reduce_scatter x2 -> x0, waiting for transfers between devices: 21.1 us -> none  [the longest x1 15.2 us: body(): lax.psum_scatter(jnp.where(inside[:, None], values, 0.0), 'row', scatter_...]
    ppermute x0 -> x18, starting transfers between devices: none -> 19.4 us  [swap(): return lax.ppermute(x, axis, [(i, i ^ bit) for i in range(size)])]
    broadcast_in_dim x2 -> x0, other arithmetic: 12.9 us -> none  [body(): return (cross[None], front[None])]
    select_n x4, other arithmetic: 12.3 us -> 1.03 us  [the longest x1 0.87 us: body(): jnp.where(first, kept, came)]
  transfers between devices with their start and end apart: 6 -> 20, of which waited for: 6 -> 11; matrix products, arithmetic and copies ran while one was open for 6% -> 12% of each run, Pallas kernels for 0% -> 3%
where the time goes in v1:
time: 326 us
  waiting for transfers between devices  221 us (68%)
  matrix products  52.9 us (16%)
  starting transfers between devices  29.1 us (9%)
  Pallas kernels  10 us (3%)
  local copies, waits for them, and re-layouts  6.44 us (2%)
  other arithmetic  5.48 us (2%)
    ppermute x18, waiting for transfers between devices, swap(): return lax.ppermute(x, axis, [(i, i ^ bit) for i in range(size)])  117 us
    all_to_all x2, waiting for transfers between devices, body(): got.append(lax.all_to_all(send, (LOW, 'col'), 0, 0, tiled=False))  103 us
    dot_general x8, matrix products, dot(): jnp.dot(a, b, precision=lax.Precision.HIGH, preferred_element_type=jnp.fl...  30.1 us
    dot_general x2, matrix products, tdot(): lax.dot_general(a, b, dims, precision=lax.Precision.HIGH, preferred_eleme...  22.9 us
    ppermute x18, starting transfers between devices, swap(): return lax.ppermute(x, axis, [(i, i ^ bit) for i in range(size)])  19.4 us
    pallas_call x2, Pallas kernels, select(): pl.pallas_call(lambda *refs: select_kernel(n_out, per_src, *refs), out_sh...  10 us
    all_to_all x2, starting transfers between devices, body(): got.append(lax.all_to_all(send, (LOW, 'col'), 0, 0, tiled=False))  9.75 us
  transfers between devices with their start and end apart: 20, of which 11 were waited for; matrix products, arithmetic and copies ran while one was open for 12% of the time, Pallas kernels for 3%

profile of v1, /device:TPU:1, one launch (start us, length us, event | category | flops | bytes accessed | tf_op | source)
XLA Modules:
  0.0 325.8 jit_solution(15347422449352355616)
XLA Ops:
  0.6 1.7 fusion.44
  2.3 1.1 copy.12
  3.4 5.3 %all-to-all-start.1 = ((f32[8,16,8,256]{3,2,1,0:T(8,128)}), f32[8,16,8,256]{3,2,1,0:T(8,128)S(1)}, u32[]{:S(2)}, u32[]{:S(2)}) async-start(f32[8,16,8,256]{3,2,1,0:T(8,128)} %bitcast.100), calls=%async_computation.1 | async-start | bytes 2097152 | tf_op jit(solution)/shard_map/all_to_all | solution.py:107
  8.7 1.5 collective-permute-start.13
  10.2 1.1 copy.13
  11.2 11.1 %all-to-all-done.1.refs_5_ = f32[8,16,8,256]{3,2,1,0:T(8,128)S(1)} async-done(((f32[8,16,8,256]{3,2,1,0:T(8,128)}), f32[8,16,8,256]{3,2,1,0:T(8,128)S(1)}, u32[]{:S(2)}, u32[]{:S(2)}) %all-to-all-start.1) | async-done | bytes 1048608 | tf_op jit(solution)/shard_map/all_to_all | solution.py:107
  22.3 4.5 %all-to-all-start = ((f32[8,16,8,256]{3,2,1,0:T(8,128)}), f32[8,16,8,256]{3,2,1,0:T(8,128)S(1)}, u32[]{:S(2)}, u32[]{:S(2)}) async-start(f32[8,16,8,256]{3,2,1,0:T(8,128)} %bitcast.101), calls=%async_computation | async-start | bytes 2097152 | tf_op jit(solution)/shard_map/all_to_all | solution.py:107
  26.8 2.2 collective-permute-start.6
  29.0 2.3 collective-permute-start.7
  31.3 0.3 collective-permute-start.8
  31.6 92.3 %all-to-all-done.refs_5_ = f32[8,16,8,256]{3,2,1,0:T(8,128)S(1)} async-done(((f32[8,16,8,256]{3,2,1,0:T(8,128)}), f32[8,16,8,256]{3,2,1,0:T(8,128)S(1)}, u32[]{:S(2)}, u32[]{:S(2)}) %all-to-all-start) | async-done | bytes 1048608 | tf_op jit(solution)/shard_map/all_to_all | solution.py:107
  123.9 2.3 collective-permute-start
  126.3 1.7 collective-permute-start.9
  128.1 42.5 %collective-permute-done.refs_6_ = f32[8,16,8,256]{3,2,1,0:T(8,128)S(1)} collective-permute-done((f32[8,16,8,256]{3,2,1,0:T(8,128)S(1)}, f32[8,16,8,256]{3,2,1,0:T(8,128)S(1)}, u32[]{:S(2)}, u32[]{:S(2)}) %collective-permute-start) | collective-permute-done | bytes 1048608 | tf_op jit(solution)/shard_map/ppermute | solution.py:16
  170.6 2.3 collective-permute-start.2
  172.9 0.6 gather_fusion
  173.8 4.5 %shard_map.60 = (f32[8,8,2048]{2,1,0:T(8,128)S(1)}, f32[8,8,2048]{2,1,0:T(8,128)S(1)}, f32[8,8,2048]{2,1,0:T(8,128)S(1)}, f32[8,8,2048]{2,1,0:T(8,128)S(1)}) custom-call(s32[4,8]{1,0:T(4,128)S(1)} %fusion.32.refs_0_, s32[4,8]{1,0:T(4,128)S(1)} %get-tuple-element.18.refs_1_, s32[4,16]{1,0:T(4,128)S(1)} %get-tuple-element.42.refs_2_, ...), custom_call_target="tpu_custom_call" | custom-call | bytes 4194304 | tf_op jit(solution)/shard_map/pallas_call | solution.py:59
  178.3 0.8 copy-done.2
  179.1 0.4 collective-permute-start.12
  179.5 1.1 collective-permute-start.11
  180.5 1.2 collective-permute-start.10
  181.7 5.5 %shard_map.59 = (f32[8,8,2048]{2,1,0:T(8,128)S(1)}, f32[8,8,2048]{2,1,0:T(8,128)}, f32[8,8,2048]{2,1,0:T(8,128)}, f32[8,8,2048]{2,1,0:T(8,128)}) custom-call(s32[4,8]{1,0:T(4,128)S(1)} %fusion.32.refs_0_, s32[4,8]{1,0:T(4,128)S(1)} %get-tuple-element.18.refs_1_, s32[4,16]{1,0:T(4,128)S(1)} %get-tuple-element.42.refs_2_, ...), custom_call_target="tpu_custom_call" | custom-call | bytes 4194304 | tf_op jit(solution)/shard_map/pallas_call | solution.py:59
  187.3 5.7 %collective-permute-done.12 = f32[8,8,2048]{2,1,0:T(8,128)S(1)} collective-permute-done((f32[8,8,2048]{2,1,0:T(8,128)S(1)}, f32[8,8,2048]{2,1,0:T(8,128)S(1)}, u32[]{:S(2)}, u32[]{:S(2)}) %collective-permute-start.12) | collective-permute-done | bytes 524320 | tf_op jit(solution)/shard_map/ppermute | solution.py:16
  193.0 0.4 collective-permute-start.5
  193.4 9.9 %collective-permute-done.11 = f32[8,8,2048]{2,1,0:T(8,128)S(1)} collective-permute-done((f32[8,8,2048]{2,1,0:T(8,128)S(1)}, f32[8,8,2048]{2,1,0:T(8,128)S(1)}, u32[]{:S(2)}, u32[]{:S(2)}) %collective-permute-start.11) | collective-permute-done | bytes 524320 | tf_op jit(solution)/shard_map/ppermute | solution.py:16
  203.3 0.4 collective-permute-start.4
  203.7 2.1 collective-permute-done.10
  205.8 0.8 copy-done.8
  206.9 1.6 pad_maximum_fusion.2
  208.5 7.0 %collective-permute-done.5 = f32[8,8,2048]{2,1,0:T(8,128)S(1)} collective-permute-done((f32[8,8,2048]{2,1,0:T(8,128)}, f32[8,8,2048]{2,1,0:T(8,128)S(1)}, u32[]{:S(2)}, u32[]{:S(2)}) %collective-permute-start.5) | collective-permute-done | bytes 524320 | tf_op jit(solution)/shard_map/ppermute | solution.py:16
  215.5 10.3 %collective-permute-done.4 = f32[8,8,2048]{2,1,0:T(8,128)S(1)} collective-permute-done((f32[8,8,2048]{2,1,0:T(8,128)}, f32[8,8,2048]{2,1,0:T(8,128)S(1)}, u32[]{:S(2)}, u32[]{:S(2)}) %collective-permute-start.4) | collective-permute-done | bytes 524320 | tf_op jit(solution)/shard_map/ppermute | solution.py:16
  225.9 1.7 collective-permute-done.3
  227.7 4.2 %fusion.17 = f32[256,1024]{1,0:T(8,128)S(1)} fusion(f32[1024,1024]{1,0:T(8,128)} %collective-permute-done.13, f32[256,2048]{1,0:T(8,128)S(1)} %bitcast.106), kind=kOutput, calls=%fused_computation.28 | convolution fusion | flops 1610612736 | bytes 6291456 | tf_op jit(solution)/shard_map/dot_general | solution.py:80
  231.9 4.2 %fusion.26 = f32[256,1024]{1,0:T(8,128)S(1)} fusion(f32[1024,1024]{1,0:T(8,128)} %collective-permute-done.13, f32[256,2048]{1,0:T(8,128)S(1)} %bitcast.110), kind=kOutput, calls=%fused_computation.35 | convolution fusion | flops 1610612736 | bytes 6291456 | tf_op jit(solution)/shard_map/dot_general | solution.py:80
  236.2 4.2 %fusion.15 = f32[256,1024]{1,0:T(8,128)S(1)} fusion(f32[1024,1024]{1,0:T(8,128)} %collective-permute-done.6, f32[256,2048]{1,0:T(8,128)S(1)} %bitcast.107), kind=kOutput, calls=%fused_computation.26 | convolution fusion | flops 1610612736 | bytes 6291456 | tf_op jit(solution)/shard_map/dot_general | solution.py:80
  240.4 4.4 %fusion.24 = f32[256,1024]{1,0:T(8,128)S(1)} fusion(f32[1024,1024]{1,0:T(8,128)} %collective-permute-done.6, f32[256,2048]{1,0:T(8,128)S(1)} %bitcast.111), kind=kOutput, calls=%fused_computation.33 | convolution fusion | flops 1610612736 | bytes 6291456 | tf_op jit(solution)/shard_map/dot_general | solution.py:80
  244.8 2.3 add_negate_fusion
  247.1 4.2 %fusion.10 = f32[256,1024]{1,0:T(8,128)S(1)} fusion(f32[256,1024]{1,0:T(8,128)S(1)} %fusion.17, f32[1024,1024]{1,0:T(8,128)} %collective-permute-done.14, f32[256,2048]{1,0:T(8,128)S(1)} %bitcast.109), kind=kOutput, calls=%fused_computation.16 | convolution fusion | flops 1611137024 | bytes 7340032 | tf_op jit(solution)/shard_map/dot_general | solution.py:80
  251.6 4.2 %fusion.11 = f32[256,1024]{1,0:T(8,128)S(1)} fusion(f32[256,1024]{1,0:T(8,128)S(1)} %fusion.26, f32[1024,1024]{1,0:T(8,128)} %collective-permute-done.14, f32[256,2048]{1,0:T(8,128)S(1)} %bitcast.112), kind=kOutput, calls=%fused_computation.18 | convolution fusion | flops 1611137024 | bytes 7340032 | tf_op jit(solution)/shard_map/dot_general | solution.py:80
  255.9 1.3 collective-permute-start.15
  257.2 2.3 add_negate_fusion.1
  259.9 15.7 %collective-permute-done.16 = f32[256,1024]{1,0:T(8,128)S(1)} collective-permute-done((f32[256,1024]{1,0:T(8,128)S(1)}, f32[256,1024]{1,0:T(8,128)S(1)}, u32[]{:S(2)}, u32[]{:S(2)}) %collective-permute-start.16) | collective-permute-done | bytes 1048608 | tf_op jit(solution)/shard_map/ppermute | solution.py:16
  275.7 22.4 %collective-permute-done.15 = f32[256,1024]{1,0:T(8,128)S(1)} collective-permute-done((f32[256,1024]{1,0:T(8,128)S(1)}, f32[256,1024]{1,0:T(8,128)S(1)}, u32[]{:S(2)}, u32[]{:S(2)}) %collective-permute-start.15) | collective-permute-done | bytes 1048608 | tf_op jit(solution)/shard_map/ppermute | solution.py:16
  298.4 0.9 fusion.13
  299.3 2.3 pad_maximum_fusion
  301.6 1.3 collective-permute-start.17
  302.9 10.8 %fusion.4 = f32[1024,1024]{1,0:T(8,128)S(1)} fusion(f32[1024,1024]{1,0:T(8,128)} %bitcast.47, f32[1024,1024]{1,0:T(8,128)} %collective-permute-done.13, pred[]{:T(512)S(6)} %eq.15, f32[1,1024,1024]{2,1,0:T(8,128)} %param.6), kind=kOutput, calls=%fused_computation.7 | convolution fusion | flops 6443499520 | bytes 16777216 | tf_op jit(solution)/shard_map/dot_general | solution.py:160
  313.8 12.1 %fusion.1 = f32[1,1024,1024]{2,1,0:T(8,128)} fusion(f32[1024,1024]{1,0:T(8,128)S(1)} %fusion.4, f32[1,1024,1024]{2,1,0:T(8,128)S(1)} %copy-done.5, f32[1024,1024]{1,0:T(8,128)} %collective-permute-done.17, f32[1024,1024]{1,0:T(8,128)} %collective-permute-done.6, f32[1024,1024]{1,0:T(8,128)} %collective-permute-done.14, pred[]{:T(512)S(6)} %eq.15), kind=kOutput, calls=%fused_computation.4 | convolution fusion | flops 6445596672 | bytes 25165824 | tf_op jit(solution)/shard_map/dot_general | solution.py:160
  (46 shorter events, 1.9 us)
Async XLA Ops:
  0.6 172.3 %copy-start = (s32[8,16]{1,0:T(8,128)S(1)}, s32[8,16]{1,0:T(8,128)}, u32[]{:S(2)}) copy-start(s32[8,16]{1,0:T(8,128)} %param.5) | copy-start | bytes 1540
  3.4 18.9 %all-to-all-start.1 = ((f32[8,16,8,256]{3,2,1,0:T(8,128)}), f32[8,16,8,256]{3,2,1,0:T(8,128)S(1)}, u32[]{:S(2)}, u32[]{:S(2)}) async-start(f32[8,16,8,256]{3,2,1,0:T(8,128)} %bitcast.100), calls=%async_computation.1 | async-start | bytes 2097152 | tf_op jit(solution)/shard_map/all_to_all | solution.py:107
  8.7 164.2 %collective-permute-start.13 = (f32[1024,1024]{1,0:T(8,128)}, f32[1024,1024]{1,0:T(8,128)}, u32[]{:S(2)}, u32[]{:S(2)}) collective-permute-start(f32[1024,1024]{1,0:T(8,128)} %bitcast.104), channel_id=1, source_target_pairs={{0,1},{1,0},{2,3},{3,2},{4,5},{5,4},{6,7},{7,6},{8,9},{9,8},{10,11... | collective-permute-start | bytes 12582920 | tf_op jit(solution)/shard_map/ppermute | solution.py:16
  22.3 101.6 %all-to-all-start = ((f32[8,16,8,256]{3,2,1,0:T(8,128)}), f32[8,16,8,256]{3,2,1,0:T(8,128)S(1)}, u32[]{:S(2)}, u32[]{:S(2)}) async-start(f32[8,16,8,256]{3,2,1,0:T(8,128)} %bitcast.101), calls=%async_computation | async-start | bytes 2097152 | tf_op jit(solution)/shard_map/all_to_all | solution.py:107
  26.8 209.4 %collective-permute-start.6 = (f32[1024,1024]{1,0:T(8,128)}, f32[1024,1024]{1,0:T(8,128)}, u32[]{:S(2)}, u32[]{:S(2)}) collective-permute-start(f32[1024,1024]{1,0:T(8,128)} %bitcast.105), channel_id=1, source_target_pairs={{0,2},{2,0},{1,3},{3,1},{4,6},{6,4},{5,7},{7,5},{8,10},{10,8},{9,1... | collective-permute-start | bytes 12582920 | tf_op jit(solution)/shard_map/ppermute | solution.py:16
  29.0 97.3 %collective-permute-start.7 = (f32[8,16,8,256]{3,2,1,0:T(8,128)S(1)}, f32[8,16,8,256]{3,2,1,0:T(8,128)}, u32[]{:S(2)}, u32[]{:S(2)}) collective-permute-start(f32[8,16,8,256]{3,2,1,0:T(8,128)S(1)} %all-to-all-done.1.refs_5_), channel_id=1, source_target_pairs={{0,16},{16,0},{1,17},{17,1},{2,18},{18,2},{3,19},{19,3},{4,20},{20... | collective-permute-start | bytes 3145736 | tf_op jit(solution)/shard_map/ppermute | solution.py:16
  31.3 96.7 %collective-permute-start.8 = (f32[8,16,8,256]{3,2,1,0:T(8,128)S(1)}, f32[8,16,8,256]{3,2,1,0:T(8,128)}, u32[]{:S(2)}, u32[]{:S(2)}) collective-permute-start(f32[8,16,8,256]{3,2,1,0:T(8,128)S(1)} %all-to-all-done.1.refs_5_), channel_id=1, source_target_pairs={{0,2},{2,0},{1,3},{3,1},{4,6},{6,4},{5,7},{7,5},{8,10},{10,8},{9,1... | collective-permute-start | bytes 3145736 | tf_op jit(solution)/shard_map/ppermute | solution.py:16
  123.9 46.7 %collective-permute-start = (f32[8,16,8,256]{3,2,1,0:T(8,128)S(1)}, f32[8,16,8,256]{3,2,1,0:T(8,128)S(1)}, u32[]{:S(2)}, u32[]{:S(2)}) collective-permute-start(f32[8,16,8,256]{3,2,1,0:T(8,128)S(1)} %all-to-all-done.refs_5_), channel_id=1, source_target_pairs={{0,16},{16,0},{1,17},{17,1},{2,18},{18,2},{3,19},{19,3},{4,20},{20... | collective-permute-start | bytes 3145736 | tf_op jit(solution)/shard_map/ppermute | solution.py:16
  126.3 47.5 %collective-permute-start.9 = (f32[8,16,8,256]{3,2,1,0:T(8,128)}, f32[8,16,8,256]{3,2,1,0:T(8,128)}, u32[]{:S(2)}, u32[]{:S(2)}) collective-permute-start(f32[8,16,8,256]{3,2,1,0:T(8,128)} %collective-permute-done.7.refs_6_), channel_id=1, source_target_pairs={{0,2},{2,0},{1,3},{3,1},{4,6},{6,4},{5,7},{7,5},{8,10},{10,8},{9,1... | collective-permute-start | bytes 3145736 | tf_op jit(solution)/shard_map/ppermute | solution.py:16
  128.0 51.5 %collective-permute-start.1 = (f32[8,16,8,256]{3,2,1,0:T(8,128)S(1)}, f32[8,16,8,256]{3,2,1,0:T(8,128)}, u32[]{:S(2)}, u32[]{:S(2)}) collective-permute-start(f32[8,16,8,256]{3,2,1,0:T(8,128)S(1)} %all-to-all-done.refs_5_), channel_id=1, source_target_pairs={{0,2},{2,0},{1,3},{3,1},{4,6},{6,4},{5,7},{7,5},{8,10},{10,8},{9,1... | collective-permute-start | bytes 3145736 | tf_op jit(solution)/shard_map/ppermute | solution.py:16
  170.6 9.9 %collective-permute-start.2 = (f32[8,16,8,256]{3,2,1,0:T(8,128)S(1)}, f32[8,16,8,256]{3,2,1,0:T(8,128)}, u32[]{:S(2)}, u32[]{:S(2)}) collective-permute-start(f32[8,16,8,256]{3,2,1,0:T(8,128)S(1)} %collective-permute-done.refs_6_), channel_id=1, source_target_pairs={{0,2},{2,0},{1,3},{3,1},{4,6},{6,4},{5,7},{7,5},{8,10},{10,8},{9,1... | collective-permute-start | bytes 3145736 | tf_op jit(solution)/shard_map/ppermute | solution.py:16
  172.9 74.2 %collective-permute-start.14 = (f32[1024,1024]{1,0:T(8,128)}, f32[1024,1024]{1,0:T(8,128)}, u32[]{:S(2)}, u32[]{:S(2)}) collective-permute-start(f32[1024,1024]{1,0:T(8,128)} %collective-permute-done.13), channel_id=1, source_target_pairs={{0,2},{2,0},{1,3},{3,1},{4,6},{6,4},{5,7},{7,5},{8,10},{10,8},{9,1... | collective-permute-start | bytes 12582920 | tf_op jit(solution)/shard_map/ppermute | solution.py:16
  178.3 0.8 copy-start.2
  179.1 27.9 %copy-start.3 = (f32[8,8,2048]{2,1,0:T(8,128)S(1)}, f32[8,8,2048]{2,1,0:T(8,128)}, u32[]{:S(2)}) copy-start(f32[8,8,2048]{2,1,0:T(8,128)} %copy-done.2) | copy-start | bytes 1572868
  179.1 13.9 %collective-permute-start.12 = (f32[8,8,2048]{2,1,0:T(8,128)S(1)}, f32[8,8,2048]{2,1,0:T(8,128)S(1)}, u32[]{:S(2)}, u32[]{:S(2)}) collective-permute-start(f32[8,8,2048]{2,1,0:T(8,128)S(1)} %get-tuple-element.17), channel_id=1, source_target_pairs={{0,12},{4,8},{8,4},{12,0},{1,13},{5,9},{9,5},{13,1},{2,14},{6,10},... | collective-permute-start | bytes 1572872 | tf_op jit(solution)/shard_map/ppermute | solution.py:16
  179.5 23.9 %collective-permute-start.11 = (f32[8,8,2048]{2,1,0:T(8,128)S(1)}, f32[8,8,2048]{2,1,0:T(8,128)S(1)}, u32[]{:S(2)}, u32[]{:S(2)}) collective-permute-start(f32[8,8,2048]{2,1,0:T(8,128)S(1)} %get-tuple-element.16), channel_id=1, source_target_pairs={{0,8},{4,12},{8,0},{12,4},{1,9},{5,13},{9,1},{13,5},{2,10},{6,14},... | collective-permute-start | bytes 1572872 | tf_op jit(solution)/shard_map/ppermute | solution.py:16
  180.5 25.3 %collective-permute-start.10 = (f32[8,8,2048]{2,1,0:T(8,128)S(1)}, f32[8,8,2048]{2,1,0:T(8,128)S(1)}, u32[]{:S(2)}, u32[]{:S(2)}) collective-permute-start(f32[8,8,2048]{2,1,0:T(8,128)S(1)} %get-tuple-element.15), channel_id=1, source_target_pairs={{0,4},{4,0},{8,12},{12,8},{1,5},{5,1},{9,13},{13,9},{2,6},{6,2},{1... | collective-permute-start | bytes 1572872 | tf_op jit(solution)/shard_map/ppermute | solution.py:16
  193.0 12.8 %copy-start.6 = (f32[8,8,2048]{2,1,0:T(8,128)}, f32[8,8,2048]{2,1,0:T(8,128)S(1)}, u32[]{:S(2)}) copy-start(f32[8,8,2048]{2,1,0:T(8,128)S(1)} %collective-permute-done.12) | copy-start | bytes 1572868
  193.0 22.5 %collective-permute-start.5 = (f32[8,8,2048]{2,1,0:T(8,128)}, f32[8,8,2048]{2,1,0:T(8,128)S(1)}, u32[]{:S(2)}, u32[]{:S(2)}) collective-permute-start(f32[8,8,2048]{2,1,0:T(8,128)} %get-tuple-element.13), channel_id=1, source_target_pairs={{0,12},{4,8},{8,4},{12,0},{1,13},{5,9},{9,5},{13,1},{2,14},{6,10},... | collective-permute-start | bytes 1572872 | tf_op jit(solution)/shard_map/ppermute | solution.py:16
  203.3 2.5 copy-start.7
  203.3 22.5 %collective-permute-start.4 = (f32[8,8,2048]{2,1,0:T(8,128)}, f32[8,8,2048]{2,1,0:T(8,128)S(1)}, u32[]{:S(2)}, u32[]{:S(2)}) collective-permute-start(f32[8,8,2048]{2,1,0:T(8,128)} %get-tuple-element.12), channel_id=1, source_target_pairs={{0,8},{4,12},{8,0},{12,4},{1,9},{5,13},{9,1},{13,5},{2,10},{6,14},... | collective-permute-start | bytes 1572872 | tf_op jit(solution)/shard_map/ppermute | solution.py:16
  205.8 0.8 copy-start.8
  206.7 20.9 %collective-permute-start.3 = (f32[8,8,2048]{2,1,0:T(8,128)}, f32[8,8,2048]{2,1,0:T(8,128)S(1)}, u32[]{:S(2)}, u32[]{:S(2)}) collective-permute-start(f32[8,8,2048]{2,1,0:T(8,128)} %get-tuple-element.11), channel_id=1, source_target_pairs={{0,4},{4,0},{8,12},{12,8},{1,5},{5,1},{9,13},{13,9},{2,6},{6,2},{1... | collective-permute-start | bytes 1572872 | tf_op jit(solution)/shard_map/ppermute | solution.py:16
  240.4 4.4 %copy-start.4 = (f32[1,1024,1024]{2,1,0:T(8,128)S(1)}, f32[1,1024,1024]{2,1,0:T(8,128)}, u32[]{:S(2)}) copy-start(f32[1,1024,1024]{2,1,0:T(8,128)} %param.6) | copy-start | bytes 12582916
  251.3 24.3 %collective-permute-start.16 = (f32[256,1024]{1,0:T(8,128)S(1)}, f32[256,1024]{1,0:T(8,128)S(1)}, u32[]{:S(2)}, u32[]{:S(2)}) collective-permute-start(f32[256,1024]{1,0:T(8,128)S(1)} %fusion.10), channel_id=1, source_target_pairs={{0,1},{1,0},{2,3},{3,2},{4,5},{5,4},{6,7},{7,6},{8,9},{9,8},{10,11... | collective-permute-start | bytes 3145736 | tf_op jit(solution)/shard_map/ppermute | solution.py:16
  255.9 42.2 %collective-permute-start.15 = (f32[256,1024]{1,0:T(8,128)S(1)}, f32[256,1024]{1,0:T(8,128)S(1)}, u32[]{:S(2)}, u32[]{:S(2)}) collective-permute-start(f32[256,1024]{1,0:T(8,128)S(1)} %fusion.11), channel_id=1, source_target_pairs={{0,1},{1,0},{2,3},{3,2},{4,5},{5,4},{6,7},{7,6},{8,9},{9,8},{10,11... | collective-permute-start | bytes 3145736 | tf_op jit(solution)/shard_map/ppermute | solution.py:16
  301.6 12.2 %collective-permute-start.17 = (f32[1024,1024]{1,0:T(8,128)}, f32[1024,1024]{1,0:T(8,128)}, u32[]{:S(2)}, u32[]{:S(2)}) collective-permute-start(f32[1024,1024]{1,0:T(8,128)} %bitcast.47), channel_id=1, source_target_pairs={{0,2},{2,0},{1,3},{3,1},{4,6},{6,4},{5,7},{7,5},{8,10},{10,8},{9,1... | collective-permute-start | bytes 12582920 | tf_op jit(solution)/shard_map/ppermute | solution.py:16
  302.9 10.8 %copy-start.5 = (f32[1,1024,1024]{2,1,0:T(8,128)S(1)}, f32[1,1024,1024]{2,1,0:T(8,128)}, u32[]{:S(2)}) copy-start(f32[1,1024,1024]{2,1,0:T(8,128)} %param.7) | copy-start | bytes 12582916
  313.8 12.1 %copy-start.1 = (s32[8,16]{1,0:T(8,128)S(1)}, s32[8,16]{1,0:T(8,128)}, u32[]{:S(2)}) copy-start(s32[8,16]{1,0:T(8,128)} %param.5) | copy-start | bytes 1540

commit v2 on v0

v2 whole, which is shorter than its diff:
```python
import jax
import jax.numpy as jnp
from jax import lax
from jax.experimental import pallas as pl
from jax.experimental.pallas import tpu as pltpu
from jax.sharding import Mesh
from jax.sharding import PartitionSpec as P

TILE = 128
NEAR = 4
HALF = "half"
LOW = "low"
F32 = jnp.float32
BF16 = jnp.bfloat16


def swap(x, axis, bit):
    names = axis if isinstance(axis, tuple) else (axis,)
    size = 1
    for name in names:
        size *= lax.axis_size(name)
    return lax.ppermute(x, axis, [(i, i ^ bit) for i in range(size)])


def after(x, *deps):
    return lax.optimization_barrier((x,) + deps)[0]


def after_all(xs, *deps):
    return lax.optimization_barrier(tuple(xs) + deps)[: len(xs)]


def params(mib):
    return pltpu.CompilerParams(vmem_limit_bytes=mib << 20)


def cost(flops, *arrays):
    moved = sum(a.size * a.dtype.itemsize for a in arrays)
    return pl.CostEstimate(flops=flops, transcendentals=0, bytes_accessed=moved)


def any_spec():
    return pl.BlockSpec(memory_space=pl.ANY)


def like(shape, dtype=F32):
    return jax.ShapeDtypeStruct(shape, dtype)


def pack(parts):
    rt, groups, n_ch, k, width = parts.shape

    def kernel(src, out):
        for ch in range(n_ch):
            out[0, ch] = src[:, 0, ch]

    return pl.pallas_call(
        kernel,
        out_shape=like((groups, n_ch, rt, k, width)),
        grid=(groups,),
        in_specs=[pl.BlockSpec((rt, 1, n_ch, k, width), lambda i: (0, i, 0, 0, 0))],
        out_specs=pl.BlockSpec((1, n_ch, rt, k, width), lambda i: (i, 0, 0, 0, 0)),
        compiler_params=params(16),
        cost_estimate=cost(0, parts, parts),
    )(parts)


def select(pieces, chunk, rows, cols, row_id, half_id, n_half, cuts):
    n_src, rt, k, width = pieces[1].shape
    n_out, n_q = cols.shape
    n_p = rows.shape[1] // cuts
    per_src = width // TILE
    in_half = n_src * per_src
    n_pieces = len(pieces)
    src = cols % in_half // per_src
    row_at = ((rows // rt) ^ row_id) * (n_half * n_src * rt) + rows % rt
    col_at = ((cols // in_half) ^ half_id) * (n_src * rt) + src * rt
    lane_at = cols % per_src * TILE

    def kernel(row_at, col_at, lane_at, *refs):
        ins, outs = refs[:n_pieces], refs[n_pieces:-2]
        table, sems = refs[-2:]
        copies = []
        for i in range(n_pieces):
            piece = ins[i].at[:, chunk] if i % n_half == 0 else ins[i]
            copies.append(pltpu.make_async_copy(piece, table.at[i], sems.at[i]))
        for copy in copies:
            copy.start()
        for copy in copies:
            copy.wait()
        view = table.reshape(n_pieces * n_src * rt, k, width)
        for child in range(n_out):
            for q in range(n_q):
                base = col_at[child, q]
                lane = pl.multiple_of(lane_at[child, q], TILE)
                for p in range(n_p * cuts):
                    outs[p // n_p * n_out + child][p % n_p, :, q * TILE : (q + 1) * TILE] = view[
                        row_at[child, p] + base, :, pl.ds(lane, TILE)
                    ]

    out = like((n_p, k, n_q * TILE))
    flat = pl.pallas_call(
        kernel,
        out_shape=[out] * (n_out * cuts),
        grid_spec=pltpu.PrefetchScalarGridSpec(
            num_scalar_prefetch=3,
            grid=(1,),
            in_specs=[any_spec()] * n_pieces,
            out_specs=[pl.BlockSpec(out.shape, lambda i, *_: (0, 0, 0))] * (n_out * cuts),
            scratch_shapes=[
                pltpu.VMEM((n_pieces,) + pieces[1].shape, F32),
                pltpu.SemaphoreType.DMA((n_pieces,)),
            ],
        ),
        compiler_params=params(24),
        cost_estimate=cost(0, *pieces[1::2], *pieces[1::2], *[out] * (n_out * cuts)),
    )(row_at, col_at, lane_at, *pieces)
    return [flat[i * n_out : (i + 1) * n_out] for i in range(cuts)]


def halves(x):
    hi = x.astype(BF16)
    return hi, (x - hi.astype(F32)).astype(BF16)


def three(ah, al, bh, bl):
    d = lambda a, b: jnp.dot(a, b, preferred_element_type=F32)
    return d(ah, bh) + (d(ah, bl) + d(al, bh))


def split(top, bottom, block=256):
    rows, width = top.shape
    steps = rows // block

    def kernel(a, b, hi, lo):
        i = pl.program_id(0)

        @pl.when(i < steps)
        def _():
            hi[...], lo[...] = halves(a[...])

        @pl.when(i >= steps)
        def _():
            hi[...], lo[...] = halves(b[...])

    out = like((2 * rows, width), BF16)
    return pl.pallas_call(
        kernel,
        out_shape=[out, out],
        grid=(2 * steps,),
        in_specs=[
            pl.BlockSpec((block, width), lambda i: (jnp.minimum(i, steps - 1), 0)),
            pl.BlockSpec((block, width), lambda i: (jnp.maximum(i - steps, 0), 0)),
        ],
        out_specs=[pl.BlockSpec((block, width), lambda i: (i, 0))] * 2,
        compiler_params=params(16),
        cost_estimate=cost(0, top, bottom, out, out),
    )(top, bottom)


def turn(blocks, shape, col_id, same):
    n_p, n_low, n_col, n_ch, k = shape
    width = blocks[0].shape[1]
    deep = n_p * n_low * k
    views = [b.reshape(n_p, n_low, n_col, n_ch, k, width) for b in blocks]
    flags = jnp.stack([col_id, same.astype(jnp.int32)])
    half_p = n_p // 2
    pieces = [[(core, far, 0, 0, n_p)] for core in range(2) for far in range(n_col)]
    pieces += [
        [(core, far, 1, unit * half_p, half_p) for core in range(2)]
        for far in range(n_col)
        for unit in range(2)
    ]
    moves = []
    for at, piece in enumerate(pieces):
        row = 0
        for core, far, ch, tile, tiles in piece:
            moves.append((at, row, core, far, ch, tile, tiles))
            row += tiles

    def kernel(flag, own, own_p, far, far_p, hi, lo, buf, sems):
        i = pl.program_id(0)

        @pl.when(i == 0)
        def _():
            for use, refs in ((1, (own, own_p)), (0, (far, far_p))):

                @pl.when(flag[1] == use)
                def _(refs=refs):
                    for at, row, core, side, ch, tile, tiles in moves:
                        pltpu.make_async_copy(
                            refs[core].at[pl.ds(tile, tiles), :, flag[0] ^ side, ch],
                            buf.at[at, pl.ds(row, tiles)],
                            sems.at[at],
                        ).start()

        pltpu.make_async_copy(own.at[:, :, flag[0], 0], buf.at[i], sems.at[i]).wait()
        hi[0], lo[0] = halves(buf[i].reshape(deep, width).T)

    out = like((len(pieces), width, deep), BF16)
    return pl.pallas_call(
        kernel,
        out_shape=[out, out],
        grid_spec=pltpu.PrefetchScalarGridSpec(
            num_scalar_prefetch=1,
            grid=(len(pieces),),
            in_specs=[any_spec()] * 4,
            out_specs=[pl.BlockSpec((1, width, deep), lambda i, *_: (i, 0, 0))] * 2,
            scratch_shapes=[
                pltpu.VMEM((len(pieces), n_p, n_low, k, width), F32),
                pltpu.SemaphoreType.DMA((len(pieces),)),
            ],
        ),
        compiler_params=params(32),
        cost_estimate=cost(0, blocks[0], blocks[0], out, out),
    )(flags, *views)


def panel(blocks, low_id):
    n_low = len(blocks)
    n_p, k, deep = blocks[0].shape
    rows = n_p * n_low * k

    def kernel(at, *refs):
        ins, (mh, ml, full) = refs[:n_low], refs[n_low:]
        for s in range(n_low):
            full[:, at[0] ^ s] = ins[s][...]
        mh[...], ml[...] = halves(full[...].reshape(rows, -1))

    out = like((rows, deep), BF16)
    wide = deep // 4
    return pl.pallas_call(
        kernel,
        out_shape=[out, out],
        grid_spec=pltpu.PrefetchScalarGridSpec(
            num_scalar_prefetch=1,
            grid=(deep // wide,),
            in_specs=[pl.BlockSpec((n_p, k, wide), lambda i, *_: (0, 0, i))] * n_low,
            out_specs=[pl.BlockSpec((rows, wide), lambda i, *_: (0, i))] * 2,
            scratch_shapes=[pltpu.VMEM((n_p, n_low, k, wide), F32)],
        ),
        compiler_params=params(16),
        cost_estimate=cost(0, *blocks, *blocks),
    )(low_id.reshape(1), *blocks)


def product(mh, ml, parts, shape, wide=256):
    rows, deep = mh.shape
    _, n_low, _, _, k = shape
    n_p = rows // (n_low * k)
    steps = parts[0][0].shape[1] // wide
    n = len(parts)

    def kernel(mh, ml, *refs):
        out = refs[-1]
        for j in range(n):

            @pl.when(pl.program_id(0) // steps == j)
            def _(j=j):
                hi, lo = refs[2 * j : 2 * j + 2]
                new = -three(mh[...], ml[...], hi[...], lo[...])
                out[...] = new.reshape(n_p, n_low, k, wide)

    out = like((n_p, n_low, k, n * steps * wide))
    whole = pl.BlockSpec((rows, deep), lambda i: (0, 0))
    specs, args = [whole, whole], [mh, ml]
    for j, part in enumerate(parts):
        strip = pl.BlockSpec(
            (deep, wide), lambda i, j=j: (0, jnp.clip(i - j * steps, 0, steps - 1))
        )
        specs += [strip, strip]
        args += part
    return pl.pallas_call(
        kernel,
        out_shape=out,
        grid=(n * steps,),
        in_specs=specs,
        out_specs=pl.BlockSpec((n_p, n_low, k, wide), lambda i: (0, 0, 0, i)),
        compiler_params=params(32),
        cost_estimate=cost(6 * rows * deep * n * steps * wide, *args, out),
    )(*args)


def update(base, turned, pieces, in_place, wide=256):
    height, width = base.shape
    n = len(pieces)
    tall = height // 2
    strip = pl.BlockSpec((height, wide), lambda i: (0, i))
    specs, args, plan = [strip], [base], []
    for at, blocks in pieces:
        for part in turned:
            for x in part:
                deep = x.shape[2]
                specs.append(pl.BlockSpec((1, tall, deep), lambda i, at=at: (at, 0, 0)))
                args.append(x)
        for columns in blocks:
            steps = columns[0].shape[-1] // wide
            plan.append((len(blocks), len(columns), steps))
            for j, x in enumerate(columns):
                x = x.reshape(-1, x.shape[-1])
                specs.append(
                    pl.BlockSpec(
                        (x.shape[0], wide),
                        lambda i, j=j, steps=steps: (0, jnp.clip(i - j * steps, 0, steps - 1)),
                    )
                )
                args.append(x)
    n_in = len(args)

    def kernel(*refs):
        acc, out = refs[0], refs[n_in]
        where = pl.program_id(0)
        top, bottom = acc[:tall], acc[tall:]
        at, row = 1, 0
        for _ in range(n):
            upper, lower_ = refs[at : at + 2], refs[at + 2 : at + 4]
            at += 4
            rows = []
            for _ in range(plan[row][0]):
                _, columns, steps = plan[row]
                x = refs[at][...]
                for j in range(1, columns):
                    x = jnp.where(where // steps == j, refs[at + j][...], x)
                rows.append(x)
                at += columns
                row += 1
            sh, sl = halves(rows[0] if len(rows) == 1 else jnp.concatenate(rows, axis=0))
            top = top - three(upper[0][0], upper[1][0], sh, sl)
            bottom = bottom - three(lower_[0][0], lower_[1][0], sh, sl)
        out[:tall], out[tall:] = top, bottom

    deep = turned[0][0].shape[2] * n
    return pl.pallas_call(
        kernel,
        out_shape=like(base.shape),
        grid=(width // wide,),
        in_specs=specs,
        out_specs=strip,
        input_output_aliases={0: 0} if in_place else {},
        compiler_params=params(40),
        cost_estimate=cost(6 * height * deep * width, base, base),
    )(*args)


def place(pieces, into, shape, col_id, width):
    n_p, n_low, n_col, n_ch, k = shape
    n = len(pieces)

    def kernel(at, *refs):
        ins, out, sems = refs[:n], refs[-2], refs[-1]
        copies = []
        for i, (rows, tile, far, ch, start) in enumerate(pieces):
            tiles, cols = pl.ds(tile, rows.shape[0]), pl.ds(start, rows.shape[-1])
            spot = out.at[tiles, :, at[0] ^ far, ch, :, cols]
            copies.append(pltpu.make_async_copy(ins[i], spot, sems.at[i]))
        for copy in copies:
            copy.start()
        for copy in copies:
            copy.wait()

    args = [x[0] for x in pieces]
    specs = [pl.BlockSpec(memory_space=pltpu.VMEM)] * n
    aliases = {}
    if into is not None:
        args.append(into)
        specs.append(any_spec())
        aliases = {n + 1: 0}
    return pl.pallas_call(
        kernel,
        out_shape=like((n_p, n_low, n_col, n_ch, k, width)),
        grid_spec=pltpu.PrefetchScalarGridSpec(
            num_scalar_prefetch=1,
            in_specs=specs,
            out_specs=any_spec(),
            scratch_shapes=[pltpu.SemaphoreType.DMA((n,))],
        ),
        input_output_aliases=aliases,
        compiler_params=params(16),
        cost_estimate=cost(0, *args[:n], *args[:n]),
    )(col_id.reshape(1), *args)


def body(sigma_top, structure, lower, dinv):
    own = lower[0]
    half_id, low_id = lax.axis_index(HALF), lax.axis_index(LOW)
    row_id, col_id = lax.axis_index("row"), lax.axis_index("col")
    n_half, n_low = lax.axis_size(HALF), lax.axis_size(LOW)
    n_row, n_col = lax.axis_size("row"), lax.axis_size("col")
    groups = n_low * n_col
    n_ch = 2
    k = TILE // groups // n_ch
    rt, width = sigma_top.shape[0] // TILE, sigma_top.shape[1]
    n_q = structure.shape[1]
    n_p = n_q // n_row
    near_id = low_id * n_col + col_id

    children = half_id * n_low + (low_id ^ jnp.arange(n_low, dtype=jnp.int32))
    lists = jnp.take(structure, children, axis=0)
    mine = lax.dynamic_slice_in_dim(lists, row_id * n_p, n_p, axis=1)
    other = lax.dynamic_slice_in_dim(lists, (1 - row_id) * n_p, n_p, axis=1)
    cols = jnp.concatenate([mine, other], axis=1)

    parts = sigma_top.reshape(rt, groups, n_ch, k, width)
    got = lax.all_to_all(pack(parts), (LOW, "col"), 0, 0)
    cut = own.shape[1] // 2
    far = [swap(after(own[:, i * cut : (i + 1) * cut], got), "col", 1) for i in range(2)]
    own_p = swap(own, "row", 1)
    merge = max(1, TILE // width)
    if merge > 1:
        got = (
            got.reshape(groups // merge, merge, n_ch, rt, k, width)
            .transpose(0, 2, 3, 4, 1, 5)
            .reshape(groups // merge, n_ch, rt, k, merge * width)
        )
    got_p = swap(got, "row", 1)
    shape = (n_p, n_low, n_col, n_ch, k)

    def others(chunk):
        return [swap(chunk, HALF, s) for s in range(1, n_half)]

    def choose(got, ring, ch, cuts):
        pieces = [got] + ring + [got_p] + [swap(x, "row", 1) for x in ring]
        return select(pieces, ch, mine, cols, row_id, half_id, n_half, cuts)

    def hand_out(chosen):
        return [chosen[0]] + [swap(chosen[s], LOW, s) for s in range(1, n_low)]

    same = row_id == col_id
    near = split(own, own_p)
    ring = others(got[:, 0])
    ring[-1] = after(ring[-1], near[0])
    far[0] = after(far[0], ring[-1])
    far_p = [swap(far[0], "row", 1)]
    (chosen,) = choose(got, ring, 0, 1)
    blocks = hand_out(chosen)
    far_parts = [split(after(far[0], chosen[0]), far_p[0])]
    turned = [turn((own[:, :cut], own_p[:, :cut], far[0], far_p[0]), shape, col_id, same)]
    ring = others(after(got[:, 1], chosen[0]))
    ring[-1] = after(ring[-1], far_parts[0][0], turned[0][0])
    far[1], *blocks = after_all((far[1], *blocks), ring[-1])
    far_p.append(swap(far[1], "row", 1))
    first = panel(blocks, low_id)
    sent = product(*first, far_parts[:1], shape)
    came = [(swap(sent, "col", 1), 0, 0, 0)]
    chosen = choose(after(got, sent), ring, 1, 2)
    units = [hand_out(x) for x in chosen]
    far_parts.append(split(after(far[1], chosen[0][0]), far_p[1]))
    sent = product(*first, far_parts[1:], shape)
    came.append((swap(sent, "col", 1), 0, 0, cut))
    kept = [(product(after(first[0], sent), first[1], [near], shape), 0, 0, 0)]
    for i, unit in enumerate(units):
        m = panel([after(x, kept[0][0]) for x in unit], low_id)
        sent = product(*m, far_parts, shape)
        tile = i * n_p // 2
        came.append((swap(sent, "col", 1), tile, 1, 0))
        kept.append((product(after(m[0], sent), m[1], [near], shape), tile, 1, 0))
        if i == 0:
            turned.append(
                turn(
                    (after(own, kept[-1][0])[:, cut:], own_p[:, cut:], far[1], far_p[1]),
                    shape,
                    col_id,
                    same,
                )
            )

    def pair(x):
        return [x[0]], [swap(x[0], "row", 1)]

    mine_a, peer_a = pair(kept[0])
    came_a = [came[0][0], came[1][0]]
    came_ap = [swap(x, "row", 1) for x in came_a]
    base = n_row * n_col
    front = update(
        dinv[0],
        turned,
        [(0, [mine_a]), (1, [came_a]), (n_col, [peer_a]), (n_col + 1, [came_ap])],
        False,
    )
    front = update(
        front,
        turned,
        [(base, pair(kept[1])), (base + 1, pair(kept[2])), (base + 2, pair(came[2]))],
        True,
    )
    front = update(front, turned, [(base + 3, pair(came[3]))], True)
    cross = None
    for group in (
        [(r, t, 0, c, x) for r, t, c, x in kept] + [(r, t, 1, c, x) for r, t, c, x in came[:3]],
        [(r, t, 1, c, x) for r, t, c, x in came[3:]],
    ):
        cross = place(group, cross, shape, col_id, own.shape[1])
    return (cross.reshape(own.shape)[None], front[None])


def solution(mesh):
    n_leaf, n_row, n_col = (mesh.shape[a] for a in ("leaf", "row", "col"))
    fine = Mesh(
        mesh.devices.reshape(n_leaf // NEAR, NEAR, n_row, n_col), (HALF, LOW, "row", "col")
    )
    leaf = (HALF, LOW)
    block = P(leaf, "row", "col")
    return jax.shard_map(
        body,
        mesh=fine,
        in_specs=(P("row", leaf + ("col",)), P(), block, block),
        out_specs=(block, block),
        check_vma=False,
    )
```

time: 739 us -> 249 us (0.34)
  waiting for transfers between devices: 577 us -> 102 us
  Pallas kernels: 0 us -> 82.8 us
  matrix products: 63 us -> 0 us
  starting transfers between devices: 0.24 us -> 39.3 us
  local copies, waits for them, and re-layouts: 57.6 us -> 22.7 us
  other arithmetic: 26.2 us -> 0.35 us
  between operations: 14.2 us -> 1.02 us
    all_gather x4 -> x0, waiting for transfers between devices: 555 us -> none  [the longest x1 353 us: body(): shard_piece = lax.all_gather(sigma_top, ('leaf', 'col'), axis=1, tiled=True)]
    pallas_call x0 -> x23, Pallas kernels: none -> 82.8 us  [the longest x7 24.8 us: product(): pl.pallas_call(kernel, out_shape=out, grid=(n * steps,), in_specs=specs,...]
    ppermute x0 -> x30, waiting for transfers between devices: none -> 82.2 us  [swap(): return lax.ppermute(x, axis, [(i, i ^ bit) for i in range(size)])]
    dot_general x2 -> x0, matrix products: 63 us -> none  [the longest x1 31.8 us: body(): jnp.dot(row_panel, lax.all_gather(factor_block, 'row', axis=0, tiled=True...]
    gather x2 -> x1, local copies, waits for them, and re-layouts: 34.7 us -> 0.56 us  [body(): lists = jnp.take(structure, children, axis=0)]
    ppermute x0 -> x30, starting transfers between devices: none -> 34.1 us  [swap(): return lax.ppermute(x, axis, [(i, i ^ bit) for i in range(size)])]
    reduce_scatter x2 -> x0, waiting for transfers between devices: 21.1 us -> none  [the longest x1 15.2 us: body(): lax.psum_scatter(jnp.where(inside[:, None], values, 0.0), 'row', scatter_...]
    all_to_all x0 -> x1, waiting for transfers between devices: none -> 19.6 us  [body(): got = lax.all_to_all(pack(parts), (LOW, 'col'), 0, 0)]
  transfers between devices with their start and end apart: 6 -> 31, of which waited for: 6 -> 9; matrix products, arithmetic and copies ran while one was open for 6% -> 4% of each run, Pallas kernels for 0% -> 31%
where the time goes in v2:
time: 249 us; the launch traced here: 248 us
  waiting for transfers between devices  102 us (41%)
  Pallas kernels  82.8 us (33%)
  starting transfers between devices  39.3 us (16%)
  local copies, waits for them, and re-layouts  22.7 us (9%)
    ppermute x30, waiting for transfers between devices, swap(): return lax.ppermute(x, axis, [(i, i ^ bit) for i in range(size)])  82.2 us
    ppermute x30, starting transfers between devices, swap(): return lax.ppermute(x, axis, [(i, i ^ bit) for i in range(size)])  34.1 us
    pallas_call x7, Pallas kernels, product(): pl.pallas_call(kernel, out_shape=out, grid=(n * steps,), in_specs=specs,...  24.8 us
    pallas_call x3, Pallas kernels, update(): pl.pallas_call(kernel, out_shape=like(base.shape), grid=(width // wide,),...  23.7 us
    all_to_all x1, waiting for transfers between devices, body(): got = lax.all_to_all(pack(parts), (LOW, 'col'), 0, 0)  19.6 us
    pallas_call x3, Pallas kernels, split(): pl.pallas_call(kernel, out_shape=[out, out], grid=(2 * steps,), in_specs=...  13.5 us
    unnamed x34, local copies, waits for them, and re-layouts  11.9 us
    pallas_call x2, Pallas kernels, turn(): pl.pallas_call(kernel, out_shape=[out, out], grid_spec=pltpu.PrefetchScal...  7.07 us
  transfers between devices with their start and end apart: 31, of which 9 were waited for; matrix products, arithmetic and copies ran while one was open for 4% of the time, Pallas kernels for 31%

profile of v2, /device:TPU:1, one launch (start us, length us, event | category | flops | bytes accessed | tf_op | source)
XLA Modules:
  0.0 248.0 jit_solution(10722769927797486219)
XLA Ops:
  0.7 1.6 copy-done.14
  2.7 1.3 copy-done.9
  4.0 5.3 %all-to-all-start = ((f32[8,2,16,8,256]{4,3,2,1,0:T(8,128)}), f32[8,2,16,8,256]{4,3,2,1,0:T(8,128)S(1)}, u32[]{:S(2)}, u32[]{:S(2)}) async-start(f32[8,2,16,8,256]{4,3,2,1,0:T(8,128)} %copy-done.9), calls=%async_computation | async-start | bytes 4194304 | tf_op jit(solution)/shard_map/all_to_all | solution.py:404
  10.3 4.6 %fusion.15 = (f32[1024,512]{1,0:T(8,128)}, f32[1024,512]{1,0:T(8,128)}) fusion(f32[1024,1024]{1,0:T(8,128)} %bitcast.41), kind=kLoop, calls=%fused_computation.46 | loop fusion | bytes 8388608 | tf_op jit(solution)/shard_map/slice | solution.py:406
  14.9 19.6 %all-to-all-done.refs_0_ = f32[8,2,16,8,256]{4,3,2,1,0:T(8,128)S(1)} async-done(((f32[8,2,16,8,256]{4,3,2,1,0:T(8,128)}), f32[8,2,16,8,256]{4,3,2,1,0:T(8,128)S(1)}, u32[]{:S(2)}, u32[]{:S(2)}) %all-to-all-start) | async-done | bytes 2097184 | tf_op jit(solution)/shard_map/all_to_all | solution.py:404
  34.5 2.5 %collective-permute-start.9 = (f32[1024,512]{1,0:T(8,128)}, f32[1024,512]{1,0:T(8,128)}, u32[]{:S(2)}, u32[]{:S(2)}) collective-permute-start(f32[1024,512]{1,0:T(8,128)} %get-tuple-element.64), channel_id=1, source_target_pairs={{0,1},{1,0},{2,3},{3,2},{4,5},{5,4},{6,7},{7,6},{8,9},{9,8},{10,11... | collective-permute-start | bytes 6291464 | tf_op jit(solution)/shard_map/ppermute | solution.py:22
  38.1 2.3 collective-permute-start.1
  40.5 2.4 collective-permute-start.3
  42.8 4.7 %shard_map.60 = (bf16[2048,1024]{1,0:T(8,128)(2,1)S(1)}, bf16[2048,1024]{1,0:T(8,128)(2,1)S(1)}) custom-call(f32[1024,1024]{1,0:T(8,128)S(1)} %bitcast.42, f32[1024,1024]{1,0:T(8,128)} %collective-permute-done.2.b), custom_call_target="tpu_custom_call" | custom-call | bytes 16777216 | tf_op jit(solution)/shard_map/pallas_call | solution.py:147
  47.5 2.0 copy-done.4
  49.5 2.0 copy-done.6
  51.6 34.3 %collective-permute-done.1.refs_1_ = f32[8,16,8,256]{3,2,1,0:T(8,128)S(1)} collective-permute-done((f32[8,16,8,256]{3,2,1,0:T(8,128)S(1)}, f32[8,16,8,256]{3,2,1,0:T(8,128)S(1)}, u32[]{:S(2)}, u32[]{:S(2)}) %collective-permute-start.1) | collective-permute-done | bytes 1048608 | tf_op jit(solution)/shard_map/ppermute | solution.py:22
  85.9 1.2 collective-permute-start.10
  88.0 4.4 %collective-permute-done.4.refs_3_ = f32[8,16,8,256]{3,2,1,0:T(8,128)} collective-permute-done((f32[8,16,8,256]{3,2,1,0:T(8,128)S(1)}, f32[8,16,8,256]{3,2,1,0:T(8,128)}, u32[]{:S(2)}, u32[]{:S(2)}) %collective-permute-start.4) | collective-permute-done | bytes 1048608 | tf_op jit(solution)/shard_map/ppermute | solution.py:22
  92.4 4.1 %shard_map.61 = (f32[8,8,2048]{2,1,0:T(8,128)S(1)}, f32[8,8,2048]{2,1,0:T(8,128)}, f32[8,8,2048]{2,1,0:T(8,128)}, f32[8,8,2048]{2,1,0:T(8,128)}) custom-call(s32[4,8]{1,0:T(4,128)S(1)} %get-tuple-element.110.row_at, s32[4,16]{1,0:T(4,128)S(1)} %get-tuple-element.119.col_at, s32[4,16]{1,0:T(4,128)S(1)} %get-tuple-element.118.lane_at, ...), custom_call_target="tpu_custom_call" | custom-call | bytes 6291456 | tf_op jit(solution)/shard_map/pallas_call | solution.py:102
  97.3 1.2 collective-permute-start.5
  98.5 3.4 %collective-permute-start.6 = (f32[8,8,2048]{2,1,0:T(8,128)}, f32[8,8,2048]{2,1,0:T(8,128)}, u32[]{:S(2)}, u32[]{:S(2)}) collective-permute-start(f32[8,8,2048]{2,1,0:T(8,128)} %get-tuple-element.61), channel_id=1, source_target_pairs={{0,8},{4,12},{8,0},{12,4},{1,9},{5,13},{9,1},{13,5},{2,10},{6,14},... | collective-permute-start | bytes 1572872 | tf_op jit(solution)/shard_map/ppermute | solution.py:22
  102.0 4.2 %fusion.14 = (f32[1024,512]{1,0:T(8,128)}, f32[1024,512]{1,0:T(8,128)S(1)}) fusion(f32[1024,1024]{1,0:T(8,128)} %collective-permute-done.2.b), kind=kLoop, calls=%fused_computation.45 | loop fusion | bytes 8388608 | tf_op jit(solution)/shard_map/slice | solution.py:460
  106.2 3.4 %shard_map.63 = (bf16[8,512,256]{2,1,0:T(8,128)(2,1)S(1)}, bf16[8,512,256]{2,1,0:T(8,128)(2,1)S(1)}) custom-call(s32[2]{0:T(128)S(1)} %pad_add_fusion.1.flag, f32[8,4,2,2,8,512]{5,4,3,2,1,0:T(8,128)S(1)} %bitcast.47, f32[8,4,2,2,8,512]{5,4,3,2,1,0:T(8,128)S(1)} %bitcast.48, f32[8,4,2,2,8,512]{5,4,3,2,1,0:T(8,128)} %bitcast.10.far, ...), custom_call_target="tpu_custom_call" | custom-call | bytes 8388608 | tf_op jit(solution)/shard_map/pallas_call | solution.py:201
  109.6 5.0 %shard_map.62 = (bf16[2048,512]{1,0:T(8,128)(2,1)S(1)}, bf16[2048,512]{1,0:T(8,128)(2,1)S(1)}) custom-call(f32[1024,512]{1,0:T(8,128)} %collective-permute-done.9.a, f32[1024,512]{1,0:T(8,128)} %collective-permute-done.10.b), custom_call_target="tpu_custom_call" | custom-call | bytes 8388608 | tf_op jit(solution)/shard_map/pallas_call | solution.py:147
  114.7 31.0 %collective-permute-done.8.refs_1_ = f32[8,16,8,256]{3,2,1,0:T(8,128)S(1)} collective-permute-done((f32[8,16,8,256]{3,2,1,0:T(8,128)}, f32[8,16,8,256]{3,2,1,0:T(8,128)S(1)}, u32[]{:S(2)}, u32[]{:S(2)}) %collective-permute-start.8) | collective-permute-done | bytes 1048608 | tf_op jit(solution)/shard_map/ppermute | solution.py:22
  145.7 2.0 collective-permute-start.12
  147.7 2.7 %shard_map.64 = (bf16[256,2048]{1,0:T(8,128)(2,1)S(1)}, bf16[256,2048]{1,0:T(8,128)(2,1)S(1)}) custom-call(s32[1]{0:T(128)} %bitcast.1.at, f32[8,8,2048]{2,1,0:T(8,128)S(1)} %copy-done.16, f32[8,8,2048]{2,1,0:T(8,128)} %collective-permute-done.5.refs_1_, f32[8,8,2048]{2,1,0:T(8,128)} %collective-permute-done.6.refs_2_, ...), custom_call_target="tpu_custom_call" | custom-call | bytes 4194304 | tf_op jit(solution)/shard_map/pallas_call | solution.py:232
  150.5 2.4 shard_map.65
  152.9 2.8 %shard_map.66 = (f32[4,8,2048]{2,1,0:T(8,128)S(1)}, f32[4,8,2048]{2,1,0:T(8,128)S(1)}, f32[4,8,2048]{2,1,0:T(8,128)S(1)}, f32[4,8,2048]{2,1,0:T(8,128)S(1)}, f32...) custom-call(s32[4,8]{1,0:T(4,128)S(1)} %get-tuple-element.110.row_at,, ...), custom_call_target="tpu_custom_call" | custom-call | bytes 6291456 | tf_op jit(solution)/shard_map/pallas_call | solution.py:102
  155.8 1.7 collective-permute-start.13
  158.6 1.5 collective-permute-start.17
  160.0 3.7 %shard_map.67 = (bf16[2048,512]{1,0:T(8,128)(2,1)S(1)}, bf16[2048,512]{1,0:T(8,128)(2,1)S(1)}) custom-call(f32[1024,512]{1,0:T(8,128)} %collective-permute-done.a, f32[1024,512]{1,0:T(8,128)S(1)} %collective-permute-done.12.b), custom_call_target="tpu_custom_call" | custom-call | bytes 8388608 | tf_op jit(solution)/shard_map/pallas_call | solution.py:147
  163.8 2.4 shard_map.68
  166.7 2.2 copy-done.7
  168.9 5.2 %shard_map.69.refs_0_ = f32[8,4,8,1024]{3,2,1,0:T(8,128)S(1)} custom-call(bf16[256,2048]{1,0:T(8,128)(2,1)S(1)} %get-tuple-element.84.mh, bf16[256,2048]{1,0:T(8,128)(2,1)S(1)} %get-tuple-element.75.ml, bf16[2048,1024]{1,0:T(8,128)(2,1)S(1)} %copy-done.5, bf16[2048,1024]{1,0:T(8,128)(2,1)S(1)} %copy-done.7), custom_call_target="tpu_custom_call" | custom-call | flops 3221225472 | bytes 11534336 | tf_op jit(solution)/shard_map/pallas_call | solution.py:273
  175.8 2.3 collective-permute-start.23
  178.0 2.9 %collective-permute-done.19.refs_3_ = f32[4,8,2048]{2,1,0:T(8,128)S(1)} collective-permute-done((f32[4,8,2048]{2,1,0:T(8,128)S(1)}, f32[4,8,2048]{2,1,0:T(8,128)S(1)}, u32[]{:S(2)}, u32[]{:S(2)}) %collective-permute-start.19) | collective-permute-done | bytes 262176 | tf_op jit(solution)/shard_map/ppermute | solution.py:22
  181.8 3.8 %shard_map.73 = f32[4,4,8,1024]{3,2,1,0:T(8,128)} custom-call(bf16[128,2048]{1,0:T(8,128)(2,1)S(1)} %get-tuple-element.104.mh, bf16[128,2048]{1,0:T(8,128)(2,1)S(1)} %get-tuple-element.103.ml, bf16[2048,512]{1,0:T(8,128)(2,1)S(1)} %get-tuple-element.67.refs_0_, bf16[2048,512]{1,0:T(8,128)(2,1)S(1)} %get-tuple-element.76.refs_1_, ...), custom_call_target="tpu_custom_call" | custom-call | flops 1610612736 | bytes 9961472 | tf_op jit(solution)/shard_map/pallas_call | solution.py:273
  187.3 3.9 %shard_map.71 = f32[4,4,8,1024]{3,2,1,0:T(8,128)} custom-call(bf16[128,2048]{1,0:T(8,128)(2,1)S(1)} %get-tuple-element.105.mh, bf16[128,2048]{1,0:T(8,128)(2,1)S(1)} %get-tuple-element.94.ml, bf16[2048,512]{1,0:T(8,128)(2,1)S(1)} %get-tuple-element.67.refs_0_, bf16[2048,512]{1,0:T(8,128)(2,1)S(1)} %get-tuple-element.76.refs_1_, ...), custom_call_target="tpu_custom_call" | custom-call | flops 1610612736 | bytes 9961472 | tf_op jit(solution)/shard_map/pallas_call | solution.py:273
  191.5 2.2 collective-permute-start.24
  193.7 4.5 %collective-permute-done.21.refs_4_ = f32[8,4,8,512]{3,2,1,0:T(8,128)S(1)} collective-permute-done((f32[8,4,8,512]{3,2,1,0:T(8,128)S(1)}, f32[8,4,8,512]{3,2,1,0:T(8,128)S(1)}, u32[]{:S(2)}, u32[]{:S(2)}) %collective-permute-start.21) | collective-permute-done | bytes 524320 | tf_op jit(solution)/shard_map/ppermute | solution.py:22
  198.2 4.1 %collective-permute-start.25 = (f32[8,4,8,512]{3,2,1,0:T(8,128)S(1)}, f32[8,4,8,512]{3,2,1,0:T(8,128)S(1)}, u32[]{:S(2)}, u32[]{:S(2)}) collective-permute-start(f32[8,4,8,512]{3,2,1,0:T(8,128)S(1)} %collective-permute-done.21.refs_4_), channel_id=1, source_target_pairs={{0,2},{2,0},{1,3},{3,1},{4,6},{6,4},{5,7},{7,5},{8,10},{10,8},{9,1... | collective-permute-start | bytes 1572872 | tf_op jit(solution)/shard_map/ppermute | solution.py:22
  202.3 3.6 %shard_map.74.refs_1_ = f32[4,4,8,1024]{3,2,1,0:T(8,128)S(1)} custom-call(bf16[128,2048]{1,0:T(8,128)(2,1)S(1)} %get-tuple-element.104.mh, bf16[128,2048]{1,0:T(8,128)(2,1)S(1)} %get-tuple-element.103.ml, bf16[2048,1024]{1,0:T(8,128)(2,1)S(1)} %copy-done.5, bf16[2048,1024]{1,0:T(8,128)(2,1)S(1)} %copy-done.7), custom_call_target="tpu_custom_call" | custom-call | flops 1610612736 | bytes 9961472 | tf_op jit(solution)/shard_map/pallas_call | solution.py:273
  206.1 1.3 copy-done.11
  208.1 3.7 %shard_map.78 = (bf16[8,512,256]{2,1,0:T(8,128)(2,1)S(1)}, bf16[8,512,256]{2,1,0:T(8,128)(2,1)S(1)}) custom-call(s32[2]{0:T(128)S(1)} %pad_add_fusion.1.flag, f32[8,4,2,2,8,512]{5,4,3,2,1,0:T(8,128)S(1)} %bitcast.45, f32[8,4,2,2,8,512]{5,4,3,2,1,0:T(8,128)S(1)} %bitcast.46, f32[8,4,2,2,8,512]{5,4,3,2,1,0:T(8,128)} %bitcast.16.far, ...), custom_call_target="tpu_custom_call" | custom-call | bytes 8388608 | tf_op jit(solution)/shard_map/pallas_call | solution.py:201
  211.8 3.6 %shard_map.75.refs_2_ = f32[4,4,8,1024]{3,2,1,0:T(8,128)S(1)} custom-call(bf16[128,2048]{1,0:T(8,128)(2,1)S(1)} %get-tuple-element.105.mh, bf16[128,2048]{1,0:T(8,128)(2,1)S(1)} %get-tuple-element.94.ml, bf16[2048,1024]{1,0:T(8,128)(2,1)S(1)} %copy-done.5, bf16[2048,1024]{1,0:T(8,128)(2,1)S(1)} %copy-done.8), custom_call_target="tpu_custom_call" | custom-call | flops 1610612736 | bytes 9961472 | tf_op jit(solution)/shard_map/pallas_call | solution.py:273
  215.5 1.9 shard_map.76.refs_1_
  217.4 3.3 %collective-permute-done.16.refs_0_ = f32[4,4,8,1024]{3,2,1,0:T(8,128)S(1)} collective-permute-done((f32[4,4,8,1024]{3,2,1,0:T(8,128)}, f32[4,4,8,1024]{3,2,1,0:T(8,128)S(1)}, u32[]{:S(2)}, u32[]{:S(2)}) %collective-permute-start.16) | collective-permute-done | bytes 524320 | tf_op jit(solution)/shard_map/ppermute | solution.py:22
  220.7 2.3 collective-permute-start.26
  224.3 9.7 %shard_map.79.refs_0_ = f32[1024,1024]{1,0:T(8,128)} custom-call(f32[1024,1024]{1,0:T(8,128)} %bitcast.66, bf16[8,512,256]{2,1,0:T(8,128)(2,1)S(1)} %get-tuple-element.68.refs_1_.refs_6_.refs_12_.refs_17_.refs_7_.refs_13_, bf16[8,512,256]{2,1,0:T(8,128)(2,1)S(1)} %get-tuple-element.106.refs_2_.refs_7_.refs_13_.refs_18_.refs_8_.refs_14_, ...), custom_call_target="tpu_custom_call" | custom-call | flops 6442450944 | bytes 8388608 | tf_op jit(solution)/shard_map/pallas_call | solution.py:333
  234.1 8.2 %shard_map.80.refs_0_ = f32[1024,1024]{1,0:T(8,128)} custom-call(f32[1024,1024]{1,0:T(8,128)} %shard_map.79.refs_0_, bf16[8,512,256]{2,1,0:T(8,128)(2,1)S(1)} %get-tuple-element.68.refs_1_.refs_6_.refs_12_.refs_17_.refs_7_.refs_13_, ...), custom_call_target="tpu_custom_call", output_to_operand_aliasing={{}: (0, {})} | custom-call | flops 4831838208 | bytes 8388608 | tf_op jit(solution)/shard_map/pallas_call | solution.py:333
  242.2 5.8 %shard_map.81 = f32[1024,1024]{1,0:T(8,128)} custom-call(f32[1024,1024]{1,0:T(8,128)} %shard_map.80.refs_0_, bf16[8,512,256]{2,1,0:T(8,128)(2,1)S(1)} %get-tuple-element.68.refs_1_.refs_6_.refs_12_.refs_17_.refs_7_.refs_13_, ...), custom_call_target="tpu_custom_call", output_to_operand_aliasing={{}: (0, {})} | custom-call | flops 1610612736 | bytes 8388608 | tf_op jit(solution)/shard_map/pallas_call | solution.py:333
  (83 shorter events, 12.9 us)
Async XLA Ops:
  0.6 86.5 %copy-start = (s32[8,16]{1,0:T(8,128)S(1)}, s32[8,16]{1,0:T(8,128)}, u32[]{:S(2)}) copy-start(s32[8,16]{1,0:T(8,128)} %param.5) | copy-start | bytes 1540
  0.6 1.6 copy-start.14
  2.7 1.3 copy-start.9
  4.0 30.5 %all-to-all-start = ((f32[8,2,16,8,256]{4,3,2,1,0:T(8,128)}), f32[8,2,16,8,256]{4,3,2,1,0:T(8,128)S(1)}, u32[]{:S(2)}, u32[]{:S(2)}) async-start(f32[8,2,16,8,256]{4,3,2,1,0:T(8,128)} %copy-done.9), calls=%async_computation | async-start | bytes 4194304 | tf_op jit(solution)/shard_map/all_to_all | solution.py:404
  9.3 33.5 %collective-permute-start.2 = (f32[1024,1024]{1,0:T(8,128)}, f32[1024,1024]{1,0:T(8,128)}, u32[]{:S(2)}, u32[]{:S(2)}) collective-permute-start(f32[1024,1024]{1,0:T(8,128)} %bitcast.40), channel_id=1, source_target_pairs={{0,2},{2,0},{1,3},{3,1},{4,6},{6,4},{5,7},{7,5},{8,10},{10,8},{9,1... | collective-permute-start | bytes 12582920 | tf_op jit(solution)/shard_map/ppermute | solution.py:22
  34.5 8.3 %copy-start.2 = (f32[1,1024,1024]{2,1,0:T(8,128)S(1)}, f32[1,1024,1024]{2,1,0:T(8,128)}, u32[]{:S(2)}) copy-start(f32[1,1024,1024]{2,1,0:T(8,128)} %param.6) | copy-start | bytes 12582916
  34.5 51.4 %collective-permute-start.9 = (f32[1024,512]{1,0:T(8,128)}, f32[1024,512]{1,0:T(8,128)}, u32[]{:S(2)}, u32[]{:S(2)}) collective-permute-start(f32[1024,512]{1,0:T(8,128)} %get-tuple-element.64), channel_id=1, source_target_pairs={{0,1},{1,0},{2,3},{3,2},{4,5},{5,4},{6,7},{7,6},{8,9},{9,8},{10,11... | collective-permute-start | bytes 6291464 | tf_op jit(solution)/shard_map/ppermute | solution.py:22
  38.1 47.8 %collective-permute-start.1 = (f32[8,16,8,256]{3,2,1,0:T(8,128)S(1)}, f32[8,16,8,256]{3,2,1,0:T(8,128)S(1)}, u32[]{:S(2)}, u32[]{:S(2)}) collective-permute-start(f32[8,16,8,256]{3,2,1,0:T(8,128)S(1)} %get-tuple-element.117), channel_id=1, source_target_pairs={{0,16},{16,0},{1,17},{17,1},{2,18},{18,2},{3,19},{19,3},{4,20},{20... | collective-permute-start | bytes 3145736 | tf_op jit(solution)/shard_map/ppermute | solution.py:22
  40.5 47.5 %collective-permute-start.3 = (f32[8,2,16,8,256]{4,3,2,1,0:T(8,128)S(1)}, f32[8,2,16,8,256]{4,3,2,1,0:T(8,128)}, u32[]{:S(2)}, u32[]{:S(2)}) collective-permute-start(f32[8,2,16,8,256]{4,3,2,1,0:T(8,128)S(1)} %all-to-all-done.refs_0_), channel_id=1, source_target_pairs={{0,2},{2,0},{1,3},{3,1},{4,6},{6,4},{5,7},{7,5},{8,10},{10,8},{9,1... | collective-permute-start | bytes 6291464 | tf_op jit(solution)/shard_map/ppermute | solution.py:22
  47.5 2.0 copy-start.4
  49.5 2.0 copy-start.6
  85.9 16.1 %collective-permute-start.10 = (f32[1024,512]{1,0:T(8,128)}, f32[1024,512]{1,0:T(8,128)}, u32[]{:S(2)}, u32[]{:S(2)}) collective-permute-start(f32[1024,512]{1,0:T(8,128)} %collective-permute-done.9.a), channel_id=1, source_target_pairs={{0,2},{2,0},{1,3},{3,1},{4,6},{6,4},{5,7},{7,5},{8,10},{10,8},{9,1... | collective-permute-start | bytes 6291464 | tf_op jit(solution)/shard_map/ppermute | solution.py:22
  87.1 5.3 %collective-permute-start.4 = (f32[8,16,8,256]{3,2,1,0:T(8,128)S(1)}, f32[8,16,8,256]{3,2,1,0:T(8,128)}, u32[]{:S(2)}, u32[]{:S(2)}) collective-permute-start(f32[8,16,8,256]{3,2,1,0:T(8,128)S(1)} %collective-permute-done.1.refs_1_), channel_id=1, source_target_pairs={{0,2},{2,0},{1,3},{3,1},{4,6},{6,4},{5,7},{7,5},{8,10},{10,8},{9,1... | collective-permute-start | bytes 3145736 | tf_op jit(solution)/shard_map/ppermute | solution.py:22
  87.1 58.6 %collective-permute-start = (f32[1024,512]{1,0:T(8,128)}, f32[1024,512]{1,0:T(8,128)}, u32[]{:S(2)}, u32[]{:S(2)}) collective-permute-start(f32[1024,512]{1,0:T(8,128)} %get-tuple-element.56), channel_id=1, source_target_pairs={{0,1},{1,0},{2,3},{3,2},{4,5},{5,4},{6,7},{7,6},{8,9},{9,8},{10,11... | collective-permute-start | bytes 6291464 | tf_op jit(solution)/shard_map/ppermute | solution.py:22
  96.5 0.8 copy-start.15
  97.3 48.4 %collective-permute-start.8 = (f32[8,16,8,256]{3,2,1,0:T(8,128)}, f32[8,16,8,256]{3,2,1,0:T(8,128)S(1)}, u32[]{:S(2)}, u32[]{:S(2)}) collective-permute-start(f32[8,16,8,256]{3,2,1,0:T(8,128)} %get-tuple-element.63), channel_id=1, source_target_pairs={{0,16},{16,0},{1,17},{17,1},{2,18},{18,2},{3,19},{19,3},{4,20},{20... | collective-permute-start | bytes 3145736 | tf_op jit(solution)/shard_map/ppermute | solution.py:22
  97.3 48.4 %collective-permute-start.5 = (f32[8,8,2048]{2,1,0:T(8,128)}, f32[8,8,2048]{2,1,0:T(8,128)}, u32[]{:S(2)}, u32[]{:S(2)}) collective-permute-start(f32[8,8,2048]{2,1,0:T(8,128)} %get-tuple-element.60), channel_id=1, source_target_pairs={{0,4},{4,0},{8,12},{12,8},{1,5},{5,1},{9,13},{13,9},{2,6},{6,2},{1... | collective-permute-start | bytes 1572872 | tf_op jit(solution)/shard_map/ppermute | solution.py:22
  98.5 47.2 %collective-permute-start.6 = (f32[8,8,2048]{2,1,0:T(8,128)}, f32[8,8,2048]{2,1,0:T(8,128)}, u32[]{:S(2)}, u32[]{:S(2)}) collective-permute-start(f32[8,8,2048]{2,1,0:T(8,128)} %get-tuple-element.61), channel_id=1, source_target_pairs={{0,8},{4,12},{8,0},{12,4},{1,9},{5,13},{9,1},{13,5},{2,10},{6,14},... | collective-permute-start | bytes 1572872 | tf_op jit(solution)/shard_map/ppermute | solution.py:22
  102.0 43.7 %collective-permute-start.7 = (f32[8,8,2048]{2,1,0:T(8,128)}, f32[8,8,2048]{2,1,0:T(8,128)}, u32[]{:S(2)}, u32[]{:S(2)}) collective-permute-start(f32[8,8,2048]{2,1,0:T(8,128)} %get-tuple-element.62), channel_id=1, source_target_pairs={{0,12},{4,8},{8,4},{12,0},{1,13},{5,9},{9,5},{13,1},{2,14},{6,10},... | collective-permute-start | bytes 1572872 | tf_op jit(solution)/shard_map/ppermute | solution.py:22
  102.0 4.2 %copy-start.13 = (f32[1024,512]{1,0:T(8,128)S(1)}, f32[1024,512]{1,0:T(8,128)}, u32[]{:S(2)}) copy-start(f32[1024,512]{1,0:T(8,128)} %get-tuple-element.64) | copy-start | bytes 6291460
  109.6 38.1 %copy-start.16 = (f32[8,8,2048]{2,1,0:T(8,128)S(1)}, f32[8,8,2048]{2,1,0:T(8,128)}, u32[]{:S(2)}) copy-start(f32[8,8,2048]{2,1,0:T(8,128)} %copy-done.15) | copy-start | bytes 1572868
  145.7 14.3 %collective-permute-start.12 = (f32[1024,512]{1,0:T(8,128)}, f32[1024,512]{1,0:T(8,128)S(1)}, u32[]{:S(2)}, u32[]{:S(2)}) collective-permute-start(f32[1024,512]{1,0:T(8,128)} %collective-permute-done.a), channel_id=1, source_target_pairs={{0,2},{2,0},{1,3},{3,1},{4,6},{6,4},{5,7},{7,5},{8,10},{10,8},{9,1... | collective-permute-start | bytes 6291464 | tf_op jit(solution)/shard_map/ppermute | solution.py:22
  147.7 5.2 %collective-permute-start.11 = (f32[8,16,8,256]{3,2,1,0:T(8,128)S(1)}, f32[8,16,8,256]{3,2,1,0:T(8,128)S(1)}, u32[]{:S(2)}, u32[]{:S(2)}) collective-permute-start(f32[8,16,8,256]{3,2,1,0:T(8,128)S(1)} %collective-permute-done.8.refs_1_), channel_id=1, source_target_pairs={{0,2},{2,0},{1,3},{3,1},{4,6},{6,4},{5,7},{7,5},{8,10},{10,8},{9,1... | collective-permute-start | bytes 3145736 | tf_op jit(solution)/shard_map/ppermute | solution.py:22
  155.7 10.5 %collective-permute-start.15 = (f32[4,8,2048]{2,1,0:T(8,128)S(1)}, f32[4,8,2048]{2,1,0:T(8,128)S(1)}, u32[]{:S(2)}, u32[]{:S(2)}) collective-permute-start(f32[4,8,2048]{2,1,0:T(8,128)S(1)} %get-tuple-element.91), channel_id=1, source_target_pairs={{0,12},{4,8},{8,4},{12,0},{1,13},{5,9},{9,5},{13,1},{2,14},{6,10},... | collective-permute-start | bytes 786440 | tf_op jit(solution)/shard_map/ppermute | solution.py:22
  155.8 25.5 %collective-permute-start.13 = (f32[4,8,2048]{2,1,0:T(8,128)S(1)}, f32[4,8,2048]{2,1,0:T(8,128)S(1)}, u32[]{:S(2)}, u32[]{:S(2)}) collective-permute-start(f32[4,8,2048]{2,1,0:T(8,128)S(1)} %get-tuple-element.87), channel_id=1, source_target_pairs={{0,4},{4,0},{8,12},{12,8},{1,5},{5,1},{9,13},{13,9},{2,6},{6,2},{1... | collective-permute-start | bytes 786440 | tf_op jit(solution)/shard_map/ppermute | solution.py:22
  157.5 23.8 %collective-permute-start.14 = (f32[4,8,2048]{2,1,0:T(8,128)S(1)}, f32[4,8,2048]{2,1,0:T(8,128)S(1)}, u32[]{:S(2)}, u32[]{:S(2)}) collective-permute-start(f32[4,8,2048]{2,1,0:T(8,128)S(1)} %get-tuple-element.89), channel_id=1, source_target_pairs={{0,8},{4,12},{8,0},{12,4},{1,9},{5,13},{9,1},{13,5},{2,10},{6,14},... | collective-permute-start | bytes 786440 | tf_op jit(solution)/shard_map/ppermute | solution.py:22
  158.6 16.3 %collective-permute-start.17 = (f32[4,8,2048]{2,1,0:T(8,128)S(1)}, f32[4,8,2048]{2,1,0:T(8,128)S(1)}, u32[]{:S(2)}, u32[]{:S(2)}) collective-permute-start(f32[4,8,2048]{2,1,0:T(8,128)S(1)} %get-tuple-element.96), channel_id=1, source_target_pairs={{0,4},{4,0},{8,12},{12,8},{1,5},{5,1},{9,13},{13,9},{2,6},{6,2},{1... | collective-permute-start | bytes 786440 | tf_op jit(solution)/shard_map/ppermute | solution.py:22
  160.0 3.7 %copy-start.10 = (f32[1024,512]{1,0:T(8,128)}, f32[1024,512]{1,0:T(8,128)S(1)}, u32[]{:S(2)}) copy-start(f32[1024,512]{1,0:T(8,128)S(1)} %collective-permute-done.12.b) | copy-start | bytes 6291460
  160.0 15.7 %collective-permute-start.18 = (f32[4,8,2048]{2,1,0:T(8,128)S(1)}, f32[4,8,2048]{2,1,0:T(8,128)S(1)}, u32[]{:S(2)}, u32[]{:S(2)}) collective-permute-start(f32[4,8,2048]{2,1,0:T(8,128)S(1)} %get-tuple-element.98), channel_id=1, source_target_pairs={{0,8},{4,12},{8,0},{12,4},{1,9},{5,13},{9,1},{13,5},{2,10},{6,14},... | collective-permute-start | bytes 786440 | tf_op jit(solution)/shard_map/ppermute | solution.py:22
  163.8 2.9 %copy-start.5 = (bf16[2048,1024]{1,0:T(8,128)(2,1)S(1)}, bf16[2048,1024]{1,0:T(8,128)(2,1)}, u32[]{:S(2)}) copy-start(bf16[2048,1024]{1,0:T(8,128)(2,1)} %copy-done.4) | copy-start | bytes 12582916
  166.2 14.7 %collective-permute-start.19 = (f32[4,8,2048]{2,1,0:T(8,128)S(1)}, f32[4,8,2048]{2,1,0:T(8,128)S(1)}, u32[]{:S(2)}, u32[]{:S(2)}) collective-permute-start(f32[4,8,2048]{2,1,0:T(8,128)S(1)} %get-tuple-element.100), channel_id=1, source_target_pairs={{0,12},{4,8},{8,4},{12,0},{1,13},{5,9},{9,5},{13,1},{2,14},{6,10},... | collective-permute-start | bytes 786440 | tf_op jit(solution)/shard_map/ppermute | solution.py:22
  166.7 2.2 copy-start.7
  174.9 16.6 %collective-permute-start.20 = (f32[8,4,8,512]{3,2,1,0:T(8,128)S(1)}, f32[8,4,8,512]{3,2,1,0:T(8,128)S(1)}, u32[]{:S(2)}, u32[]{:S(2)}) collective-permute-start(f32[8,4,8,512]{3,2,1,0:T(8,128)S(1)} %shard_map.65), channel_id=1, source_target_pairs={{0,1},{1,0},{2,3},{3,2},{4,5},{5,4},{6,7},{7,6},{8,9},{9,8},{10,11... | collective-permute-start | bytes 1572872 | tf_op jit(solution)/shard_map/ppermute | solution.py:22
  175.8 48.0 %collective-permute-start.23 = (f32[8,4,8,1024]{3,2,1,0:T(8,128)S(1)}, f32[8,4,8,1024]{3,2,1,0:T(8,128)S(1)}, u32[]{:S(2)}, u32[]{:S(2)}) collective-permute-start(f32[8,4,8,1024]{3,2,1,0:T(8,128)S(1)} %shard_map.69.refs_0_), channel_id=1, source_target_pairs={{0,2},{2,0},{1,3},{3,1},{4,6},{6,4},{5,7},{7,5},{8,10},{10,8},{9,1... | collective-permute-start | bytes 3145736 | tf_op jit(solution)/shard_map/ppermute | solution.py:22
  180.9 17.3 %collective-permute-start.21 = (f32[8,4,8,512]{3,2,1,0:T(8,128)S(1)}, f32[8,4,8,512]{3,2,1,0:T(8,128)S(1)}, u32[]{:S(2)}, u32[]{:S(2)}) collective-permute-start(f32[8,4,8,512]{3,2,1,0:T(8,128)S(1)} %shard_map.68), channel_id=1, source_target_pairs={{0,1},{1,0},{2,3},{3,2},{4,5},{5,4},{6,7},{7,6},{8,9},{9,8},{10,11... | collective-permute-start | bytes 1572872 | tf_op jit(solution)/shard_map/ppermute | solution.py:22
  185.6 29.8 %collective-permute-start.22 = (f32[4,4,8,1024]{3,2,1,0:T(8,128)}, f32[4,4,8,1024]{3,2,1,0:T(8,128)S(1)}, u32[]{:S(2)}, u32[]{:S(2)}) collective-permute-start(f32[4,4,8,1024]{3,2,1,0:T(8,128)} %shard_map.73), channel_id=1, source_target_pairs={{0,1},{1,0},{2,3},{3,2},{4,5},{5,4},{6,7},{7,6},{8,9},{9,8},{10,11... | collective-permute-start | bytes 1572872 | tf_op jit(solution)/shard_map/ppermute | solution.py:22
  191.2 14.7 %copy-start.3 = (f32[1,1024,1024]{2,1,0:T(8,128)S(1)}, f32[1,1024,1024]{2,1,0:T(8,128)}, u32[]{:S(2)}) copy-start(f32[1,1024,1024]{2,1,0:T(8,128)} %param.6) | copy-start | bytes 12582916
  191.2 29.5 %collective-permute-start.16 = (f32[4,4,8,1024]{3,2,1,0:T(8,128)}, f32[4,4,8,1024]{3,2,1,0:T(8,128)S(1)}, u32[]{:S(2)}, u32[]{:S(2)}) collective-permute-start(f32[4,4,8,1024]{3,2,1,0:T(8,128)} %shard_map.71), channel_id=1, source_target_pairs={{0,1},{1,0},{2,3},{3,2},{4,5},{5,4},{6,7},{7,6},{8,9},{9,8},{10,11... | collective-permute-start | bytes 1572872 | tf_op jit(solution)/shard_map/ppermute | solution.py:22
  191.5 32.2 %collective-permute-start.24 = (f32[8,4,8,512]{3,2,1,0:T(8,128)S(1)}, f32[8,4,8,512]{3,2,1,0:T(8,128)S(1)}, u32[]{:S(2)}, u32[]{:S(2)}) collective-permute-start(f32[8,4,8,512]{3,2,1,0:T(8,128)S(1)} %collective-permute-done.20.refs_3_), channel_id=1, source_target_pairs={{0,2},{2,0},{1,3},{3,1},{4,6},{6,4},{5,7},{7,5},{8,10},{10,8},{9,1... | collective-permute-start | bytes 1572872 | tf_op jit(solution)/shard_map/ppermute | solution.py:22
  198.2 26.1 %collective-permute-start.25 = (f32[8,4,8,512]{3,2,1,0:T(8,128)S(1)}, f32[8,4,8,512]{3,2,1,0:T(8,128)S(1)}, u32[]{:S(2)}, u32[]{:S(2)}) collective-permute-start(f32[8,4,8,512]{3,2,1,0:T(8,128)S(1)} %collective-permute-done.21.refs_4_), channel_id=1, source_target_pairs={{0,2},{2,0},{1,3},{3,1},{4,6},{6,4},{5,7},{7,5},{8,10},{10,8},{9,1... | collective-permute-start | bytes 1572872 | tf_op jit(solution)/shard_map/ppermute | solution.py:22
  205.9 1.6 copy-start.11
  205.9 2.2 copy-start.12
  208.1 3.7 %copy-start.8 = (bf16[2048,1024]{1,0:T(8,128)(2,1)S(1)}, bf16[2048,1024]{1,0:T(8,128)(2,1)}, u32[]{:S(2)}) copy-start(bf16[2048,1024]{1,0:T(8,128)(2,1)} %copy-done.6) | copy-start | bytes 12582916
  215.4 18.6 %collective-permute-start.27 = (f32[4,4,8,1024]{3,2,1,0:T(8,128)S(1)}, f32[4,4,8,1024]{3,2,1,0:T(8,128)S(1)}, u32[]{:S(2)}, u32[]{:S(2)}) collective-permute-start(f32[4,4,8,1024]{3,2,1,0:T(8,128)S(1)} %shard_map.75.refs_2_), channel_id=1, source_target_pairs={{0,2},{2,0},{1,3},{3,1},{4,6},{6,4},{5,7},{7,5},{8,10},{10,8},{9,1... | collective-permute-start | bytes 1572872 | tf_op jit(solution)/shard_map/ppermute | solution.py:22
  220.7 13.4 %collective-permute-start.26 = (f32[4,4,8,1024]{3,2,1,0:T(8,128)S(1)}, f32[4,4,8,1024]{3,2,1,0:T(8,128)S(1)}, u32[]{:S(2)}, u32[]{:S(2)}) collective-permute-start(f32[4,4,8,1024]{3,2,1,0:T(8,128)S(1)} %shard_map.74.refs_1_), channel_id=1, source_target_pairs={{0,2},{2,0},{1,3},{3,1},{4,6},{6,4},{5,7},{7,5},{8,10},{10,8},{9,1... | collective-permute-start | bytes 1572872 | tf_op jit(solution)/shard_map/ppermute | solution.py:22
  223.7 10.3 %collective-permute-start.28 = (f32[4,4,8,1024]{3,2,1,0:T(8,128)S(1)}, f32[4,4,8,1024]{3,2,1,0:T(8,128)S(1)}, u32[]{:S(2)}, u32[]{:S(2)}) collective-permute-start(f32[4,4,8,1024]{3,2,1,0:T(8,128)S(1)} %collective-permute-done.22.refs_5_), channel_id=1, source_target_pairs={{0,2},{2,0},{1,3},{3,1},{4,6},{6,4},{5,7},{7,5},{8,10},{10,8},{9,1... | collective-permute-start | bytes 1572872 | tf_op jit(solution)/shard_map/ppermute | solution.py:22
  223.8 18.4 %collective-permute-start.29 = (f32[4,4,8,1024]{3,2,1,0:T(8,128)S(1)}, f32[4,4,8,1024]{3,2,1,0:T(8,128)S(1)}, u32[]{:S(2)}, u32[]{:S(2)}) collective-permute-start(f32[4,4,8,1024]{3,2,1,0:T(8,128)S(1)} %collective-permute-done.16.refs_0_), channel_id=1, source_target_pairs={{0,2},{2,0},{1,3},{3,1},{4,6},{6,4},{5,7},{7,5},{8,10},{10,8},{9,1... | collective-permute-start | bytes 1572872 | tf_op jit(solution)/shard_map/ppermute | solution.py:22
  242.2 5.8 %copy-start.1 = (s32[8,16]{1,0:T(8,128)S(1)}, s32[8,16]{1,0:T(8,128)}, u32[]{:S(2)}) copy-start(s32[8,16]{1,0:T(8,128)} %param.5) | copy-start | bytes 1540

commit v3 on v2

--- a/solution.py
+++ b/solution.py
@@ -34,9 +34,8 @@
     return pltpu.CompilerParams(vmem_limit_bytes=mib << 20)
 
 
-def cost(flops, *arrays):
-    moved = sum(a.size * a.dtype.itemsize for a in arrays)
-    return pl.CostEstimate(flops=flops, transcendentals=0, bytes_accessed=moved)
+def cost():
+    return pl.CostEstimate(flops=1, transcendentals=0, bytes_accessed=1)
 
 
 def any_spec():
@@ -61,7 +60,7 @@
         in_specs=[pl.BlockSpec((rt, 1, n_ch, k, width), lambda i: (0, i, 0, 0, 0))],
         out_specs=pl.BlockSpec((1, n_ch, rt, k, width), lambda i: (i, 0, 0, 0, 0)),
         compiler_params=params(16),
-        cost_estimate=cost(0, parts, parts),
+        cost_estimate=cost(),
     )(parts)
 
 
@@ -113,7 +112,7 @@
             ],
         ),
         compiler_params=params(24),
-        cost_estimate=cost(0, *pieces[1::2], *pieces[1::2], *[out] * (n_out * cuts)),
+        cost_estimate=cost(),
     )(row_at, col_at, lane_at, *pieces)
     return [flat[i * n_out : (i + 1) * n_out] for i in range(cuts)]
 
@@ -154,7 +153,7 @@
         ],
         out_specs=[pl.BlockSpec((block, width), lambda i: (i, 0))] * 2,
         compiler_params=params(16),
-        cost_estimate=cost(0, top, bottom, out, out),
+        cost_estimate=cost(),
     )(top, bottom)
 
 
@@ -166,11 +165,8 @@
     flags = jnp.stack([col_id, same.astype(jnp.int32)])
     half_p = n_p // 2
     pieces = [[(core, far, 0, 0, n_p)] for core in range(2) for far in range(n_col)]
-    pieces += [
-        [(core, far, 1, unit * half_p, half_p) for core in range(2)]
-        for far in range(n_col)
-        for unit in range(2)
-    ]
+    pieces += [[(core, 0, 1, 0, n_p)] for core in range(2)]
+    pieces += [[(core, 1, 1, 0, n_p)] for core in range(2)]
     moves = []
     for at, piece in enumerate(pieces):
         row = 0
@@ -212,7 +208,7 @@
             ],
         ),
         compiler_params=params(32),
-        cost_estimate=cost(0, blocks[0], blocks[0], out, out),
+        cost_estimate=cost(),
     )(flags, *views)
 
 
@@ -240,30 +236,38 @@
             scratch_shapes=[pltpu.VMEM((n_p, n_low, k, wide), F32)],
         ),
         compiler_params=params(16),
-        cost_estimate=cost(0, *blocks, *blocks),
+        cost_estimate=cost(),
     )(low_id.reshape(1), *blocks)
 
 
-def product(mh, ml, parts, shape, wide=256):
-    rows, deep = mh.shape
+def product(panels, parts, shape, wide=256):
+    deep = panels[0][0].shape[1]
     _, n_low, _, _, k = shape
-    n_p = rows // (n_low * k)
+    tiles = [m[0].shape[0] // (n_low * k) for m in panels]
+    n_p = sum(tiles)
+    rows = n_p * n_low * k
     steps = parts[0][0].shape[1] // wide
-    n = len(parts)
-
-    def kernel(mh, ml, *refs):
+    n, n_m = len(parts), len(panels)
+
+    def kernel(*refs):
         out = refs[-1]
         for j in range(n):
 
             @pl.when(pl.program_id(0) // steps == j)
             def _(j=j):
-                hi, lo = refs[2 * j : 2 * j + 2]
-                new = -three(mh[...], ml[...], hi[...], lo[...])
-                out[...] = new.reshape(n_p, n_low, k, wide)
+                hi, lo = refs[2 * n_m + 2 * j : 2 * n_m + 2 * j + 2]
+                tile = 0
+                for i in range(n_m):
+                    mh, ml = refs[2 * i : 2 * i + 2]
+                    new = -three(mh[...], ml[...], hi[...], lo[...])
+                    out[tile : tile + tiles[i]] = new.reshape(tiles[i], n_low, k, wide)
+                    tile += tiles[i]
 
     out = like((n_p, n_low, k, n * steps * wide))
-    whole = pl.BlockSpec((rows, deep), lambda i: (0, 0))
-    specs, args = [whole, whole], [mh, ml]
+    specs, args = [], []
+    for m in panels:
+        specs += [pl.BlockSpec(m[0].shape, lambda i: (0, 0))] * 2
+        args += m
     for j, part in enumerate(parts):
         strip = pl.BlockSpec(
             (deep, wide), lambda i, j=j: (0, jnp.clip(i - j * steps, 0, steps - 1))
@@ -277,7 +281,7 @@
         in_specs=specs,
         out_specs=pl.BlockSpec((n_p, n_low, k, wide), lambda i: (0, 0, 0, i)),
         compiler_params=params(32),
-        cost_estimate=cost(6 * rows * deep * n * steps * wide, *args, out),
+        cost_estimate=cost(),
     )(*args)
 
 
@@ -294,14 +298,18 @@
                 specs.append(pl.BlockSpec((1, tall, deep), lambda i, at=at: (at, 0, 0)))
                 args.append(x)
         for columns in blocks:
-            steps = columns[0].shape[-1] // wide
+            columns = [x if isinstance(x, tuple) else (x, None) for x in columns]
+            steps = columns[0][0].shape[-1] // wide
             plan.append((len(blocks), len(columns), steps))
-            for j, x in enumerate(columns):
+            for j, (x, row) in enumerate(columns):
                 x = x.reshape(-1, x.shape[-1])
                 specs.append(
                     pl.BlockSpec(
-                        (x.shape[0], wide),
-                        lambda i, j=j, steps=steps: (0, jnp.clip(i - j * steps, 0, steps - 1)),
+                        (x.shape[0] if row is None else turned[0][0].shape[2], wide),
+                        lambda i, j=j, steps=steps, row=row or 0: (
+                            row,
+                            jnp.clip(i - j * steps, 0, steps - 1),
+                        ),
                     )
                 )
                 args.append(x)
@@ -338,7 +346,7 @@
         out_specs=strip,
         input_output_aliases={0: 0} if in_place else {},
         compiler_params=params(40),
-        cost_estimate=cost(6 * height * deep * width, base, base),
+        cost_estimate=cost(),
     )(*args)
 
 
@@ -349,10 +357,12 @@
     def kernel(at, *refs):
         ins, out, sems = refs[:n], refs[-2], refs[-1]
         copies = []
-        for i, (rows, tile, far, ch, start) in enumerate(pieces):
-            tiles, cols = pl.ds(tile, rows.shape[0]), pl.ds(start, rows.shape[-1])
+        for i, (rows, skip, count, tile, far, ch, start) in enumerate(pieces):
+            tiles, cols = pl.ds(tile, count), pl.ds(start, rows.shape[-1])
             spot = out.at[tiles, :, at[0] ^ far, ch, :, cols]
-            copies.append(pltpu.make_async_copy(ins[i], spot, sems.at[i]))
+            copies.append(
+                pltpu.make_async_copy(ins[i].at[pl.ds(skip, count)], spot, sems.at[i])
+            )
         for copy in copies:
             copy.start()
         for copy in copies:
@@ -376,7 +386,7 @@
         ),
         input_output_aliases=aliases,
         compiler_params=params(16),
-        cost_estimate=cost(0, *args[:n], *args[:n]),
+        cost_estimate=cost(),
     )(col_id.reshape(1), *args)
 
 
@@ -426,68 +436,67 @@
         return [chosen[0]] + [swap(chosen[s], LOW, s) for s in range(1, n_low)]
 
     same = row_id == col_id
-    near = split(own, own_p)
+    own_c = [own[:, i * cut : (i + 1) * cut] for i in range(2)]
+    own_pc = [own_p[:, i * cut : (i + 1) * cut] for i in range(2)]
+    near = [split(x, y) for x, y in zip(own_c, own_pc)]
     ring = others(got[:, 0])
-    ring[-1] = after(ring[-1], near[0])
+    ring[-1] = after(ring[-1], near[0][0], near[1][0])
     far[0] = after(far[0], ring[-1])
     far_p = [swap(far[0], "row", 1)]
     (chosen,) = choose(got, ring, 0, 1)
     blocks = hand_out(chosen)
     far_parts = [split(after(far[0], chosen[0]), far_p[0])]
-    turned = [turn((own[:, :cut], own_p[:, :cut], far[0], far_p[0]), shape, col_id, same)]
-    ring = others(after(got[:, 1], chosen[0]))
+    turned = [turn((own_c[0], own_pc[0], far[0], far_p[0]), shape, col_id, same)]
+    ring = others(after(got[:, 1], ring[-1]))
     ring[-1] = after(ring[-1], far_parts[0][0], turned[0][0])
     far[1], *blocks = after_all((far[1], *blocks), ring[-1])
     far_p.append(swap(far[1], "row", 1))
     first = panel(blocks, low_id)
-    sent = product(*first, far_parts[:1], shape)
+    sent = product([first], far_parts[:1], shape)
     came = [(swap(sent, "col", 1), 0, 0, 0)]
-    chosen = choose(after(got, sent), ring, 1, 2)
+    chosen = choose(after(got, sent), ring, 1, 1)
     units = [hand_out(x) for x in chosen]
     far_parts.append(split(after(far[1], chosen[0][0]), far_p[1]))
-    sent = product(*first, far_parts[1:], shape)
-    came.append((swap(sent, "col", 1), 0, 0, cut))
-    kept = [(product(after(first[0], sent), first[1], [near], shape), 0, 0, 0)]
-    for i, unit in enumerate(units):
-        m = panel([after(x, kept[0][0]) for x in unit], low_id)
-        sent = product(*m, far_parts, shape)
-        tile = i * n_p // 2
-        came.append((swap(sent, "col", 1), tile, 1, 0))
-        kept.append((product(after(m[0], sent), m[1], [near], shape), tile, 1, 0))
-        if i == 0:
-            turned.append(
-                turn(
-                    (after(own, kept[-1][0])[:, cut:], own_p[:, cut:], far[1], far_p[1]),
-                    shape,
-                    col_id,
-                    same,
-                )
-            )
-
-    def pair(x):
-        return [x[0]], [swap(x[0], "row", 1)]
-
-    mine_a, peer_a = pair(kept[0])
-    came_a = [came[0][0], came[1][0]]
-    came_ap = [swap(x, "row", 1) for x in came_a]
+    last = product([first], far_parts[1:], shape)
+    came.append((swap(last, "col", 1), 0, 0, cut))
+    turned.append(
+        turn((after(own_c[1], last), own_pc[1], far[1], far_p[1]), shape, col_id, same)
+    )
+    kept = [[product([after_all(first, turned[1][0])], near, shape)]]
+    second = panel(after_all(units[0], kept[0][0], came[1][0]), low_id)
+    last = product([second], far_parts, shape)
+    came.append((swap(last, "col", 1), 0, 1, 0))
+    came_p = [swap(after(came[i][0], last), "row", 1) for i in range(2)]
+    second = after_all(second, last)
+    kept.append([product([second], [x], shape) for x in near])
+    kept_p = [[swap(after(x, last), "row", 1) for x in xs] for xs in kept]
+
+    def other_core(x):
+        return swap(x, "row", 1)
+
     base = n_row * n_col
     front = update(
         dinv[0],
         turned,
-        [(0, [mine_a]), (1, [came_a]), (n_col, [peer_a]), (n_col + 1, [came_ap])],
+        [
+            (0, [kept[0]]),
+            (n_col, [kept_p[0]]),
+            (base, [kept[1]]),
+            (base + 1, [kept_p[1]]),
+            (1, [[came[0][0], came[1][0]]]),
+            (n_col + 1, [came_p]),
+        ],
         False,
     )
+    end = after(came[2][0], front)
     front = update(
-        front,
-        turned,
-        [(base, pair(kept[1])), (base + 1, pair(kept[2])), (base + 2, pair(came[2]))],
-        True,
+        front, turned, [(base + 2, [[end]]), (base + 3, [[other_core(end)]])], True
     )
-    front = update(front, turned, [(base + 3, pair(came[3]))], True)
     cross = None
     for group in (
-        [(r, t, 0, c, x) for r, t, c, x in kept] + [(r, t, 1, c, x) for r, t, c, x in came[:3]],
-        [(r, t, 1, c, x) for r, t, c, x in came[3:]],
+        [(kept[ch][i], 0, n_p, 0, 0, ch, i * cut) for ch in range(n_ch) for i in range(len(kept[ch]))]
+        + [(r, 0, r.shape[0], t, 1, c, x) for r, t, c, x in came[:2]],
+        [(r, 0, r.shape[0], t, 1, c, x) for r, t, c, x in came[2:]],
     ):
         cross = place(group, cross, shape, col_id, own.shape[1])
     return (cross.reshape(own.shape)[None], front[None])

time: 249 us -> 230 us (0.924)
  starting transfers between devices: 39.3 us -> 28.2 us
  Pallas kernels: 82.8 us -> 78.2 us
  waiting for transfers between devices: 102 us -> 97.6 us
    ppermute x30 -> x25, starting transfers between devices: 34.1 us -> 23 us  [swap(): return lax.ppermute(x, axis, [(i, i ^ bit) for i in range(size)])]
    ppermute x30 -> x25, waiting for transfers between devices: 82.2 us -> 78 us  [swap(): return lax.ppermute(x, axis, [(i, i ^ bit) for i in range(size)])]
    pallas_call x7 -> x6, Pallas kernels: 24.8 us -> 21 us  [product(): pl.pallas_call(kernel, out_shape=out, grid=(n * steps,), in_specs=specs,...]
    unnamed x34 -> x60, local copies, waits for them, and re-layouts: 11.9 us -> 15.1 us
    pallas_call x3 -> x2, Pallas kernels: 23.7 us -> 20.9 us  [update(): pl.pallas_call(kernel, out_shape=like(base.shape), grid=(width // wide,),...]
    slice x3 -> x2, local copies, waits for them, and re-layouts: 9.03 us -> 7.37 us  [the longest x1 4.71 us: body(): own_c = [own[:, i * cut:(i + 1) * cut] for i in range(2)]]
    pallas_call x3 -> x2, Pallas kernels: 3.78 us -> 5.22 us  [panel(): pl.pallas_call(kernel, out_shape=[out, out], grid_spec=pltpu.PrefetchScal...]
    pallas_call x3 -> x4, Pallas kernels: 13.5 us -> 12.6 us  [split(): pl.pallas_call(kernel, out_shape=[out, out], grid=(2 * steps,), in_specs=...]
  transfers between devices with their start and end apart: 31 -> 26, of which waited for: 9 -> 10; matrix products, arithmetic and copies ran while one was open for 4% -> 4% of each run, Pallas kernels for 31% -> 31%
where the time goes in v3:
time: 230 us
  waiting for transfers between devices  97.6 us (42%)
  Pallas kernels  78.2 us (34%)
  starting transfers between devices  28.2 us (12%)
  local copies, waits for them, and re-layouts  24.2 us (11%)
    ppermute x25, waiting for transfers between devices, swap(): return lax.ppermute(x, axis, [(i, i ^ bit) for i in range(size)])  78 us
    ppermute x25, starting transfers between devices, swap(): return lax.ppermute(x, axis, [(i, i ^ bit) for i in range(size)])  23 us
    pallas_call x6, Pallas kernels, product(): pl.pallas_call(kernel, out_shape=out, grid=(n * steps,), in_specs=specs,...  21 us
    pallas_call x2, Pallas kernels, update(): pl.pallas_call(kernel, out_shape=like(base.shape), grid=(width // wide,),...  20.9 us
    all_to_all x1, waiting for transfers between devices, body(): got = lax.all_to_all(pack(parts), (LOW, 'col'), 0, 0)  19.6 us
    unnamed x60, local copies, waits for them, and re-layouts  15.1 us
    pallas_call x4, Pallas kernels, split(): pl.pallas_call(kernel, out_shape=[out, out], grid=(2 * steps,), in_specs=...  12.6 us
    pallas_call x2, Pallas kernels, select(): pl.pallas_call(kernel, out_shape=[out] * (n_out * cuts), grid_spec=pltpu....  8.29 us
  transfers between devices with their start and end apart: 26, of which 10 were waited for; matrix products, arithmetic and copies ran while one was open for 4% of the time, Pallas kernels for 31%

profile of v3, /device:TPU:1, one launch (start us, length us, event | category | flops | bytes accessed | tf_op | source)
XLA Modules:
  0.0 229.7 jit_solution(14782148471859985234)
XLA Ops:
  0.7 1.6 copy-done.27
  2.7 1.3 copy-done.10
  4.0 5.3 %all-to-all-start = ((f32[8,2,16,8,256]{4,3,2,1,0:T(8,128)}), f32[8,2,16,8,256]{4,3,2,1,0:T(8,128)S(1)}, u32[]{:S(2)}, u32[]{:S(2)}) async-start(f32[8,2,16,8,256]{4,3,2,1,0:T(8,128)} %copy-done.10), calls=%async_computation | async-start | bytes 4194304 | tf_op jit(solution)/shard_map/all_to_all | solution.py:414
  10.3 4.7 %fusion.15 = (f32[1024,512]{1,0:T(8,128)}, f32[1024,512]{1,0:T(8,128)}) fusion(f32[1024,1024]{1,0:T(8,128)} %bitcast.59), kind=kLoop, calls=%fused_computation.46 | loop fusion | bytes 8388608 | tf_op jit(solution)/shard_map/slice | solution.py:439
  15.0 19.6 %all-to-all-done.refs_0_ = f32[8,2,16,8,256]{4,3,2,1,0:T(8,128)S(1)} async-done(((f32[8,2,16,8,256]{4,3,2,1,0:T(8,128)}), f32[8,2,16,8,256]{4,3,2,1,0:T(8,128)S(1)}, u32[]{:S(2)}, u32[]{:S(2)}) %all-to-all-start) | async-done | bytes 2097184 | tf_op jit(solution)/shard_map/all_to_all | solution.py:414
  34.5 2.5 %collective-permute-start.9 = (f32[1024,512]{1,0:T(8,128)}, f32[1024,512]{1,0:T(8,128)}, u32[]{:S(2)}, u32[]{:S(2)}) collective-permute-start(f32[1024,512]{1,0:T(8,128)} %get-tuple-element.64.a), channel_id=1, source_target_pairs={{0,1},{1,0},{2,3},{3,2},{4,5},{5,4},{6,7},{7,6},{8,9},{9,8},{10,11... | collective-permute-start | bytes 6291464 | tf_op jit(solution)/shard_map/ppermute | solution.py:22
  37.0 1.2 slice_bitcast_fusion
  38.2 2.3 %collective-permute-start.1 = (f32[8,16,8,256]{3,2,1,0:T(8,128)S(1)}, f32[8,16,8,256]{3,2,1,0:T(8,128)S(1)}, u32[]{:S(2)}, u32[]{:S(2)}) collective-permute-start(f32[8,16,8,256]{3,2,1,0:T(8,128)S(1)} %get-tuple-element.115), channel_id=1, source_target_pairs={{0,16},{16,0},{1,17},{17,1},{2,18},{18,2},{3,19},{19,3},{4,20},{20... | collective-permute-start | bytes 3145736 | tf_op jit(solution)/shard_map/ppermute | solution.py:22
  40.5 2.4 %collective-permute-start.3 = (f32[8,2,16,8,256]{4,3,2,1,0:T(8,128)S(1)}, f32[8,2,16,8,256]{4,3,2,1,0:T(8,128)}, u32[]{:S(2)}, u32[]{:S(2)}) collective-permute-start(f32[8,2,16,8,256]{4,3,2,1,0:T(8,128)S(1)} %all-to-all-done.refs_0_), channel_id=1, source_target_pairs={{0,2},{2,0},{1,3},{3,1},{4,6},{6,4},{5,7},{7,5},{8,10},{10,8},{9,1... | collective-permute-start | bytes 6291464 | tf_op jit(solution)/shard_map/ppermute | solution.py:22
  42.9 2.7 %fusion.14 = (f32[1024,512]{1,0:T(8,128)S(1)}, f32[1024,512]{1,0:T(8,128)S(1)}) fusion(f32[1024,1024]{1,0:T(8,128)} %collective-permute-done.2), kind=kLoop, calls=%fused_computation.45 | loop fusion | bytes 8388608 | tf_op jit(solution)/shard_map/slice | solution.py:440
  46.9 1.4 copy-done.11
  48.3 1.3 copy-done.13
  49.7 3.0 %shard_map.61 = (bf16[2048,512]{1,0:T(8,128)(2,1)S(1)}, bf16[2048,512]{1,0:T(8,128)(2,1)S(1)}) custom-call(f32[1024,512]{1,0:T(8,128)} %get-tuple-element.86.a, f32[1024,512]{1,0:T(8,128)S(1)} %get-tuple-element.110.b), custom_call_target="tpu_custom_call" | custom-call | flops 1 | bytes 1 | tf_op jit(solution)/shard_map/pallas_call | solution.py:146
  52.6 1.4 copy-done.15
  54.0 1.3 copy-done.17
  55.3 30.7 %collective-permute-done.1.refs_1_ = f32[8,16,8,256]{3,2,1,0:T(8,128)S(1)} collective-permute-done((f32[8,16,8,256]{3,2,1,0:T(8,128)S(1)}, f32[8,16,8,256]{3,2,1,0:T(8,128)S(1)}, u32[]{:S(2)}, u32[]{:S(2)}) %collective-permute-start.1) | collective-permute-done | bytes 1048608 | tf_op jit(solution)/shard_map/ppermute | solution.py:22
  88.9 3.7 %collective-permute-done.4.refs_3_ = f32[8,16,8,256]{3,2,1,0:T(8,128)} collective-permute-done((f32[8,16,8,256]{3,2,1,0:T(8,128)S(1)}, f32[8,16,8,256]{3,2,1,0:T(8,128)}, u32[]{:S(2)}, u32[]{:S(2)}) %collective-permute-start.4) | collective-permute-done | bytes 1048608 | tf_op jit(solution)/shard_map/ppermute | solution.py:22
  92.6 4.2 %shard_map.62 = (f32[8,8,2048]{2,1,0:T(8,128)S(1)}, f32[8,8,2048]{2,1,0:T(8,128)}, f32[8,8,2048]{2,1,0:T(8,128)}, f32[8,8,2048]{2,1,0:T(8,128)}) custom-call(s32[4,8]{1,0:T(4,128)S(1)} %get-tuple-element.108.row_at, s32[4,16]{1,0:T(4,128)S(1)} %get-tuple-element.117.col_at, s32[4,16]{1,0:T(4,128)S(1)} %get-tuple-element.116.lane_at, ...), custom_call_target="tpu_custom_call" | custom-call | flops 1 | bytes 1 | tf_op jit(solution)/shard_map/pallas_call | solution.py:101
  97.6 1.2 collective-permute-start.5
  100.3 1.6 copy-done.7
  101.9 1.6 copy-done.9
  103.5 3.4 %shard_map.64 = (bf16[8,512,256]{2,1,0:T(8,128)(2,1)S(1)}, bf16[8,512,256]{2,1,0:T(8,128)(2,1)S(1)}) custom-call(s32[2]{0:T(128)S(1)} %pad_add_fusion.1.flag, f32[8,4,2,2,8,512]{5,4,3,2,1,0:T(8,128)S(1)} %bitcast.39, f32[8,4,2,2,8,512]{5,4,3,2,1,0:T(8,128)S(1)} %bitcast.40, f32[8,4,2,2,8,512]{5,4,3,2,1,0:T(8,128)} %bitcast.10.far, ...), custom_call_target="tpu_custom_call" | custom-call | flops 1 | bytes 1 | tf_op jit(solution)/shard_map/pallas_call | solution.py:197
  106.9 5.0 %shard_map.63 = (bf16[2048,512]{1,0:T(8,128)(2,1)S(1)}, bf16[2048,512]{1,0:T(8,128)(2,1)S(1)}) custom-call(f32[1024,512]{1,0:T(8,128)} %collective-permute-done.9.a, f32[1024,512]{1,0:T(8,128)} %collective-permute-done.10.b), custom_call_target="tpu_custom_call" | custom-call | flops 1 | bytes 1 | tf_op jit(solution)/shard_map/pallas_call | solution.py:146
  112.0 24.4 %collective-permute-done.8.refs_1_ = f32[8,16,8,256]{3,2,1,0:T(8,128)} collective-permute-done((f32[8,16,8,256]{3,2,1,0:T(8,128)}, f32[8,16,8,256]{3,2,1,0:T(8,128)}, u32[]{:S(2)}, u32[]{:S(2)}) %collective-permute-start.8) | collective-permute-done | bytes 1048608 | tf_op jit(solution)/shard_map/ppermute | solution.py:22
  136.4 8.3 %collective-permute-done.7.refs_3_ = f32[8,8,2048]{2,1,0:T(8,128)} collective-permute-done((f32[8,8,2048]{2,1,0:T(8,128)}, f32[8,8,2048]{2,1,0:T(8,128)}, u32[]{:S(2)}, u32[]{:S(2)}) %collective-permute-start.7) | collective-permute-done | bytes 524320 | tf_op jit(solution)/shard_map/ppermute | solution.py:22
  144.7 1.5 collective-permute-start.15
  146.2 2.5 %shard_map.65 = (bf16[256,2048]{1,0:T(8,128)(2,1)S(1)}, bf16[256,2048]{1,0:T(8,128)(2,1)S(1)}) custom-call(s32[1]{0:T(128)} %bitcast.1.at, f32[8,8,2048]{2,1,0:T(8,128)S(1)} %copy-done.29, f32[8,8,2048]{2,1,0:T(8,128)S(1)} %collective-permute-done.5.refs_1_, f32[8,8,2048]{2,1,0:T(8,128)S(1)} %collective-permute-done.6.refs_2_, ...), custom_call_target="tpu_custom_call" | custom-call | flops 1 | bytes 1 | tf_op jit(solution)/shard_map/pallas_call | solution.py:228
  148.7 3.1 %shard_map.66 = f32[8,4,8,512]{3,2,1,0:T(8,128)} custom-call(bf16[256,2048]{1,0:T(8,128)(2,1)S(1)} %get-tuple-element.88.refs_0_, bf16[256,2048]{1,0:T(8,128)(2,1)S(1)} %get-tuple-element.89.refs_1_, bf16[2048,512]{1,0:T(8,128)(2,1)S(1)} %get-tuple-element.67.refs_2_, bf16[2048,512]{1,0:T(8,128)(2,1)S(1)} %get-tuple-element.76.refs_3_), custom_call_target="tpu_custom_call" | custom-call | flops 1 | bytes 1 | tf_op jit(solution)/shard_map/pallas_call | solution.py:277
  151.8 4.1 %shard_map.67 = (f32[8,8,2048]{2,1,0:T(8,128)S(1)}, f32[8,8,2048]{2,1,0:T(8,128)}, f32[8,8,2048]{2,1,0:T(8,128)}, f32[8,8,2048]{2,1,0:T(8,128)}) custom-call(s32[4,8]{1,0:T(4,128)S(1)} %get-tuple-element.108.row_at, s32[4,16]{1,0:T(4,128)S(1)} %get-tuple-element.117.col_at, s32[4,16]{1,0:T(4,128)S(1)} %get-tuple-element.116.lane_at, ...), custom_call_target="tpu_custom_call" | custom-call | flops 1 | bytes 1 | tf_op jit(solution)/shard_map/pallas_call | solution.py:101
  155.9 1.2 collective-permute-start.12
  157.1 1.5 collective-permute-start.14
  158.7 3.7 %shard_map.68 = (bf16[2048,512]{1,0:T(8,128)(2,1)S(1)}, bf16[2048,512]{1,0:T(8,128)(2,1)S(1)}) custom-call(f32[1024,512]{1,0:T(8,128)} %collective-permute-done.a, f32[1024,512]{1,0:T(8,128)S(1)} %collective-permute-done.15.b), custom_call_target="tpu_custom_call" | custom-call | flops 1 | bytes 1 | tf_op jit(solution)/shard_map/pallas_call | solution.py:146
  162.4 3.1 %shard_map.69 = f32[8,4,8,512]{3,2,1,0:T(8,128)} custom-call(bf16[256,2048]{1,0:T(8,128)(2,1)S(1)} %get-tuple-element.88.refs_0_, bf16[256,2048]{1,0:T(8,128)(2,1)S(1)} %get-tuple-element.89.refs_1_, bf16[2048,512]{1,0:T(8,128)(2,1)S(1)} %get-tuple-element.84.refs_2_.refs_4_, bf16[2048,512]{1,0:T(8,128)(2,1)S(1)} %get-tuple-element.85.refs_3_.refs_5_), custom_call_target="tpu_custom_call" | custom-call | flops 1 | bytes 1 | tf_op jit(solution)/shard_map/pallas_call | solution.py:277
  165.6 1.4 collective-permute-start.18
  167.0 3.7 %shard_map.70 = (bf16[8,512,256]{2,1,0:T(8,128)(2,1)S(1)}, bf16[8,512,256]{2,1,0:T(8,128)(2,1)S(1)}) custom-call(s32[2]{0:T(128)S(1)} %pad_add_fusion.1.flag, f32[8,4,2,2,8,512]{5,4,3,2,1,0:T(8,128)} %bitcast.12.own, f32[8,4,2,2,8,512]{5,4,3,2,1,0:T(8,128)S(1)} %bitcast.38, f32[8,4,2,2,8,512]{5,4,3,2,1,0:T(8,128)} %bitcast.14.far, ...), custom_call_target="tpu_custom_call" | custom-call | flops 1 | bytes 1 | tf_op jit(solution)/shard_map/pallas_call | solution.py:197
  170.7 1.3 copy-done.2
  172.1 4.9 %shard_map.71.refs_0_ = f32[8,4,8,1024]{3,2,1,0:T(8,128)S(1)} custom-call(bf16[256,2048]{1,0:T(8,128)(2,1)S(1)} %get-tuple-element.88.refs_0_, bf16[256,2048]{1,0:T(8,128)(2,1)S(1)} %get-tuple-element.89.refs_1_, bf16[2048,512]{1,0:T(8,128)(2,1)S(1)} %copy-done.12, bf16[2048,512]{1,0:T(8,128)(2,1)S(1)} %copy-done.14, bf16[2048,512]{1,0:T(8,128)(2,1)S(1)} %copy-done.16, ...), custom_call_target="tpu_custom_call" | custom-call | flops 1 | bytes 1 | tf_op jit(solution)/shard_map/pallas_call | solution.py:277
  177.1 4.3 %collective-permute-done.14.refs_3_ = f32[8,8,2048]{2,1,0:T(8,128)} collective-permute-done((f32[8,8,2048]{2,1,0:T(8,128)}, f32[8,8,2048]{2,1,0:T(8,128)}, u32[]{:S(2)}, u32[]{:S(2)}) %collective-permute-start.14) | collective-permute-done | bytes 524320 | tf_op jit(solution)/shard_map/ppermute | solution.py:22
  181.4 2.7 %shard_map.72 = (bf16[256,2048]{1,0:T(8,128)(2,1)S(1)}, bf16[256,2048]{1,0:T(8,128)(2,1)S(1)}) custom-call(s32[1]{0:T(128)} %bitcast.1.at, f32[8,8,2048]{2,1,0:T(8,128)S(1)} %get-tuple-element.92.refs_0_, f32[8,8,2048]{2,1,0:T(8,128)} %collective-permute-done.12.refs_1_, f32[8,8,2048]{2,1,0:T(8,128)} %collective-permute-done.13.refs_2_, ...), custom_call_target="tpu_custom_call" | custom-call | flops 1 | bytes 1 | tf_op jit(solution)/shard_map/pallas_call | solution.py:228
  184.1 5.1 %shard_map.73 = f32[8,4,8,1024]{3,2,1,0:T(8,128)S(1)} custom-call(bf16[256,2048]{1,0:T(8,128)(2,1)S(1)} %get-tuple-element.98.refs_0_, bf16[256,2048]{1,0:T(8,128)(2,1)S(1)} %get-tuple-element.99.refs_1_, bf16[2048,512]{1,0:T(8,128)(2,1)S(1)} %get-tuple-element.67.refs_2_, bf16[2048,512]{1,0:T(8,128)(2,1)S(1)} %copy-done.20, ...), custom_call_target="tpu_custom_call" | custom-call | flops 1 | bytes 1 | tf_op jit(solution)/shard_map/pallas_call | solution.py:277
  189.2 2.4 %shard_map.75.refs_2_ = f32[8,4,8,512]{3,2,1,0:T(8,128)S(1)} custom-call(bf16[256,2048]{1,0:T(8,128)(2,1)S(1)} %get-tuple-element.98.refs_0_, bf16[256,2048]{1,0:T(8,128)(2,1)S(1)} %get-tuple-element.99.refs_1_, bf16[2048,512]{1,0:T(8,128)(2,1)S(1)} %copy-done.16, bf16[2048,512]{1,0:T(8,128)(2,1)S(1)} %copy-done.18), custom_call_target="tpu_custom_call" | custom-call | flops 1 | bytes 1 | tf_op jit(solution)/shard_map/pallas_call | solution.py:277
  191.7 1.7 collective-permute-start.21
  193.5 2.4 %shard_map.74.refs_1_ = f32[8,4,8,512]{3,2,1,0:T(8,128)S(1)} custom-call(bf16[256,2048]{1,0:T(8,128)(2,1)S(1)} %get-tuple-element.98.refs_0_, bf16[256,2048]{1,0:T(8,128)(2,1)S(1)} %get-tuple-element.99.refs_1_, bf16[2048,512]{1,0:T(8,128)(2,1)S(1)} %copy-done.12, bf16[2048,512]{1,0:T(8,128)(2,1)S(1)} %copy-done.14), custom_call_target="tpu_custom_call" | custom-call | flops 1 | bytes 1 | tf_op jit(solution)/shard_map/pallas_call | solution.py:277
  199.8 14.0 %shard_map.78.refs_0_ = f32[1024,1024]{1,0:T(8,128)} custom-call(f32[1024,1024]{1,0:T(8,128)} %bitcast.57, bf16[8,512,256]{2,1,0:T(8,128)(2,1)S(1)} %get-tuple-element.68.refs_1_.refs_6_.refs_11_.refs_17_.refs_23_.refs_29_, bf16[8,512,256]{2,1,0:T(8,128)(2,1)S(1)} %get-tuple-element.100.refs_2_.refs_7_.refs_12_.refs_18_.refs_24_.refs_30_, ...), custom_call_target="tpu_custom_call" | custom-call | flops 1 | bytes 1 | tf_op jit(solution)/shard_map/pallas_call | solution.py:341
  213.7 4.1 %collective-permute-done.17.refs_0_ = f32[8,4,8,1024]{3,2,1,0:T(8,128)S(1)} collective-permute-done((f32[8,4,8,1024]{3,2,1,0:T(8,128)S(1)}, f32[8,4,8,1024]{3,2,1,0:T(8,128)S(1)}, u32[]{:S(2)}, u32[]{:S(2)}) %collective-permute-start.17) | collective-permute-done | bytes 1048608 | tf_op jit(solution)/shard_map/ppermute | solution.py:22
  217.8 1.3 collective-permute-start.24
  219.1 1.7 shard_map.76.refs_1_
  222.8 6.9 %shard_map.79 = f32[1024,1024]{1,0:T(8,128)} custom-call(f32[1024,1024]{1,0:T(8,128)} %shard_map.78.refs_0_, bf16[8,512,256]{2,1,0:T(8,128)(2,1)S(1)} %get-tuple-element.68.refs_1_.refs_6_.refs_11_.refs_17_.refs_23_.refs_29_, ...), custom_call_target="tpu_custom_call", output_to_operand_aliasing={{}: (0, {})} | custom-call | flops 1 | bytes 1 | tf_op jit(solution)/shard_map/pallas_call | solution.py:341
  (96 shorter events, 13.9 us)
Async XLA Ops:
  0.6 86.8 %copy-start = (s32[8,16]{1,0:T(8,128)S(1)}, s32[8,16]{1,0:T(8,128)}, u32[]{:S(2)}) copy-start(s32[8,16]{1,0:T(8,128)} %param.5) | copy-start | bytes 1540
  0.6 1.6 copy-start.27
  4.0 30.5 %all-to-all-start = ((f32[8,2,16,8,256]{4,3,2,1,0:T(8,128)}), f32[8,2,16,8,256]{4,3,2,1,0:T(8,128)S(1)}, u32[]{:S(2)}, u32[]{:S(2)}) async-start(f32[8,2,16,8,256]{4,3,2,1,0:T(8,128)} %copy-done.10), calls=%async_computation | async-start | bytes 4194304 | tf_op jit(solution)/shard_map/all_to_all | solution.py:414
  9.3 33.6 %collective-permute-start.2 = (f32[1024,1024]{1,0:T(8,128)}, f32[1024,1024]{1,0:T(8,128)}, u32[]{:S(2)}, u32[]{:S(2)}) collective-permute-start(f32[1024,1024]{1,0:T(8,128)} %bitcast.58), channel_id=1, source_target_pairs={{0,2},{2,0},{1,3},{3,1},{4,6},{6,4},{5,7},{7,5},{8,10},{10,8},{9,1... | collective-permute-start | bytes 12582920 | tf_op jit(solution)/shard_map/ppermute | solution.py:22
  34.5 51.5 %collective-permute-start.9 = (f32[1024,512]{1,0:T(8,128)}, f32[1024,512]{1,0:T(8,128)}, u32[]{:S(2)}, u32[]{:S(2)}) collective-permute-start(f32[1024,512]{1,0:T(8,128)} %get-tuple-element.64.a), channel_id=1, source_target_pairs={{0,1},{1,0},{2,3},{3,2},{4,5},{5,4},{6,7},{7,6},{8,9},{9,8},{10,11... | collective-permute-start | bytes 6291464 | tf_op jit(solution)/shard_map/ppermute | solution.py:22
  38.2 7.4 %copy-start.6 = (f32[1024,512]{1,0:T(8,128)S(1)}, f32[1024,512]{1,0:T(8,128)}, u32[]{:S(2)}) copy-start(f32[1024,512]{1,0:T(8,128)} %get-tuple-element.64.a) | copy-start | bytes 6291460
  38.2 47.8 %collective-permute-start.1 = (f32[8,16,8,256]{3,2,1,0:T(8,128)S(1)}, f32[8,16,8,256]{3,2,1,0:T(8,128)S(1)}, u32[]{:S(2)}, u32[]{:S(2)}) collective-permute-start(f32[8,16,8,256]{3,2,1,0:T(8,128)S(1)} %get-tuple-element.115), channel_id=1, source_target_pairs={{0,16},{16,0},{1,17},{17,1},{2,18},{18,2},{3,19},{19,3},{4,20},{20... | collective-permute-start | bytes 3145736 | tf_op jit(solution)/shard_map/ppermute | solution.py:22
  40.5 48.4 %collective-permute-start.3 = (f32[8,2,16,8,256]{4,3,2,1,0:T(8,128)S(1)}, f32[8,2,16,8,256]{4,3,2,1,0:T(8,128)}, u32[]{:S(2)}, u32[]{:S(2)}) collective-permute-start(f32[8,2,16,8,256]{4,3,2,1,0:T(8,128)S(1)} %all-to-all-done.refs_0_), channel_id=1, source_target_pairs={{0,2},{2,0},{1,3},{3,1},{4,6},{6,4},{5,7},{7,5},{8,10},{10,8},{9,1... | collective-permute-start | bytes 6291464 | tf_op jit(solution)/shard_map/ppermute | solution.py:22
  45.6 4.1 %copy-start.4 = (f32[1024,512]{1,0:T(8,128)}, f32[1024,512]{1,0:T(8,128)S(1)}, u32[]{:S(2)}) copy-start(f32[1024,512]{1,0:T(8,128)S(1)} %get-tuple-element.110.b) | copy-start | bytes 6291460
  86.0 13.1 %collective-permute-start.10 = (f32[1024,512]{1,0:T(8,128)}, f32[1024,512]{1,0:T(8,128)}, u32[]{:S(2)}, u32[]{:S(2)}) collective-permute-start(f32[1024,512]{1,0:T(8,128)} %collective-permute-done.9.a), channel_id=1, source_target_pairs={{0,2},{2,0},{1,3},{3,1},{4,6},{6,4},{5,7},{7,5},{8,10},{10,8},{9,1... | collective-permute-start | bytes 6291464 | tf_op jit(solution)/shard_map/ppermute | solution.py:22
  87.2 49.2 %collective-permute-start = (f32[1024,512]{1,0:T(8,128)}, f32[1024,512]{1,0:T(8,128)}, u32[]{:S(2)}, u32[]{:S(2)}) collective-permute-start(f32[1024,512]{1,0:T(8,128)} %get-tuple-element.86.a), channel_id=1, source_target_pairs={{0,1},{1,0},{2,3},{3,2},{4,5},{5,4},{6,7},{7,6},{8,9},{9,8},{10,11... | collective-permute-start | bytes 6291464 | tf_op jit(solution)/shard_map/ppermute | solution.py:22
  87.2 5.4 %collective-permute-start.4 = (f32[8,16,8,256]{3,2,1,0:T(8,128)S(1)}, f32[8,16,8,256]{3,2,1,0:T(8,128)}, u32[]{:S(2)}, u32[]{:S(2)}) collective-permute-start(f32[8,16,8,256]{3,2,1,0:T(8,128)S(1)} %collective-permute-done.1.refs_1_), channel_id=1, source_target_pairs={{0,2},{2,0},{1,3},{3,1},{4,6},{6,4},{5,7},{7,5},{8,10},{10,8},{9,1... | collective-permute-start | bytes 3145736 | tf_op jit(solution)/shard_map/ppermute | solution.py:22
  88.0 48.3 %collective-permute-start.8 = (f32[8,16,8,256]{3,2,1,0:T(8,128)}, f32[8,16,8,256]{3,2,1,0:T(8,128)}, u32[]{:S(2)}, u32[]{:S(2)}) collective-permute-start(f32[8,16,8,256]{3,2,1,0:T(8,128)} %get-tuple-element.63), channel_id=1, source_target_pairs={{0,16},{16,0},{1,17},{17,1},{2,18},{18,2},{3,19},{19,3},{4,20},{20... | collective-permute-start | bytes 3145736 | tf_op jit(solution)/shard_map/ppermute | solution.py:22
  97.6 38.8 %collective-permute-start.5 = (f32[8,8,2048]{2,1,0:T(8,128)}, f32[8,8,2048]{2,1,0:T(8,128)S(1)}, u32[]{:S(2)}, u32[]{:S(2)}) collective-permute-start(f32[8,8,2048]{2,1,0:T(8,128)} %get-tuple-element.60), channel_id=1, source_target_pairs={{0,4},{4,0},{8,12},{12,8},{1,5},{5,1},{9,13},{13,9},{2,6},{6,2},{1... | collective-permute-start | bytes 1572872 | tf_op jit(solution)/shard_map/ppermute | solution.py:22
  98.8 37.6 %collective-permute-start.6 = (f32[8,8,2048]{2,1,0:T(8,128)}, f32[8,8,2048]{2,1,0:T(8,128)S(1)}, u32[]{:S(2)}, u32[]{:S(2)}) collective-permute-start(f32[8,8,2048]{2,1,0:T(8,128)} %get-tuple-element.61), channel_id=1, source_target_pairs={{0,8},{4,12},{8,0},{12,4},{1,9},{5,13},{9,1},{13,5},{2,10},{6,14},... | collective-permute-start | bytes 1572872 | tf_op jit(solution)/shard_map/ppermute | solution.py:22
  99.1 45.6 %collective-permute-start.7 = (f32[8,8,2048]{2,1,0:T(8,128)}, f32[8,8,2048]{2,1,0:T(8,128)}, u32[]{:S(2)}, u32[]{:S(2)}) collective-permute-start(f32[8,8,2048]{2,1,0:T(8,128)} %get-tuple-element.62), channel_id=1, source_target_pairs={{0,12},{4,8},{8,4},{12,0},{1,13},{5,9},{9,5},{13,1},{2,14},{6,10},... | collective-permute-start | bytes 1572872 | tf_op jit(solution)/shard_map/ppermute | solution.py:22
  100.3 1.6 copy-start.7
  101.9 1.6 copy-start.9
  106.9 39.3 %copy-start.29 = (f32[8,8,2048]{2,1,0:T(8,128)S(1)}, f32[8,8,2048]{2,1,0:T(8,128)}, u32[]{:S(2)}) copy-start(f32[8,8,2048]{2,1,0:T(8,128)} %copy-done.28) | copy-start | bytes 1572868
  111.9 39.9 %copy-start.19 = (bf16[2048,512]{1,0:T(8,128)(2,1)}, bf16[2048,512]{1,0:T(8,128)(2,1)S(1)}, u32[]{:S(2)}) copy-start(bf16[2048,512]{1,0:T(8,128)(2,1)S(1)} %get-tuple-element.76.refs_3_) | copy-start | bytes 6291460
  144.7 14.0 %collective-permute-start.15 = (f32[1024,512]{1,0:T(8,128)}, f32[1024,512]{1,0:T(8,128)S(1)}, u32[]{:S(2)}, u32[]{:S(2)}) collective-permute-start(f32[1024,512]{1,0:T(8,128)} %collective-permute-done.a), channel_id=1, source_target_pairs={{0,2},{2,0},{1,3},{3,1},{4,6},{6,4},{5,7},{7,5},{8,10},{10,8},{9,1... | collective-permute-start | bytes 6291464 | tf_op jit(solution)/shard_map/ppermute | solution.py:22
  146.2 5.6 %collective-permute-start.11 = (f32[8,16,8,256]{3,2,1,0:T(8,128)}, f32[8,16,8,256]{3,2,1,0:T(8,128)S(1)}, u32[]{:S(2)}, u32[]{:S(2)}) collective-permute-start(f32[8,16,8,256]{3,2,1,0:T(8,128)} %collective-permute-done.8.refs_1_), channel_id=1, source_target_pairs={{0,2},{2,0},{1,3},{3,1},{4,6},{6,4},{5,7},{7,5},{8,10},{10,8},{9,1... | collective-permute-start | bytes 3145736 | tf_op jit(solution)/shard_map/ppermute | solution.py:22
  155.9 21.1 %collective-permute-start.12 = (f32[8,8,2048]{2,1,0:T(8,128)}, f32[8,8,2048]{2,1,0:T(8,128)}, u32[]{:S(2)}, u32[]{:S(2)}) collective-permute-start(f32[8,8,2048]{2,1,0:T(8,128)} %get-tuple-element.79), channel_id=1, source_target_pairs={{0,4},{4,0},{8,12},{12,8},{1,5},{5,1},{9,13},{13,9},{2,6},{6,2},{1... | collective-permute-start | bytes 1572872 | tf_op jit(solution)/shard_map/ppermute | solution.py:22
  157.1 19.9 %collective-permute-start.13 = (f32[8,8,2048]{2,1,0:T(8,128)}, f32[8,8,2048]{2,1,0:T(8,128)}, u32[]{:S(2)}, u32[]{:S(2)}) collective-permute-start(f32[8,8,2048]{2,1,0:T(8,128)} %get-tuple-element.80), channel_id=1, source_target_pairs={{0,8},{4,12},{8,0},{12,4},{1,9},{5,13},{9,1},{13,5},{2,10},{6,14},... | collective-permute-start | bytes 1572872 | tf_op jit(solution)/shard_map/ppermute | solution.py:22
  157.1 24.3 %collective-permute-start.14 = (f32[8,8,2048]{2,1,0:T(8,128)}, f32[8,8,2048]{2,1,0:T(8,128)}, u32[]{:S(2)}, u32[]{:S(2)}) collective-permute-start(f32[8,8,2048]{2,1,0:T(8,128)} %get-tuple-element.81), channel_id=1, source_target_pairs={{0,12},{4,8},{8,4},{12,0},{1,13},{5,9},{9,5},{13,1},{2,14},{6,10},... | collective-permute-start | bytes 1572872 | tf_op jit(solution)/shard_map/ppermute | solution.py:22
  158.6 3.7 %copy-start.21 = (f32[1024,512]{1,0:T(8,128)}, f32[1024,512]{1,0:T(8,128)S(1)}, u32[]{:S(2)}) copy-start(f32[1024,512]{1,0:T(8,128)S(1)} %collective-permute-done.15.b) | copy-start | bytes 6291460
  162.4 3.1 %copy-start.23 = (bf16[2048,512]{1,0:T(8,128)(2,1)}, bf16[2048,512]{1,0:T(8,128)(2,1)S(1)}, u32[]{:S(2)}) copy-start(bf16[2048,512]{1,0:T(8,128)(2,1)S(1)} %get-tuple-element.84.refs_2_.refs_4_) | copy-start | bytes 6291460
  162.4 3.1 %copy-start.25 = (bf16[2048,512]{1,0:T(8,128)(2,1)}, bf16[2048,512]{1,0:T(8,128)(2,1)S(1)}, u32[]{:S(2)}) copy-start(bf16[2048,512]{1,0:T(8,128)(2,1)S(1)} %get-tuple-element.85.refs_3_.refs_5_) | copy-start | bytes 6291460
  162.4 4.6 %copy-start.5 = (f32[1024,512]{1,0:T(8,128)S(1)}, f32[1024,512]{1,0:T(8,128)}, u32[]{:S(2)}) copy-start(f32[1024,512]{1,0:T(8,128)} %copy-done.4) | copy-start | bytes 6291460
  162.4 4.6 %copy-start.22 = (f32[1024,512]{1,0:T(8,128)S(1)}, f32[1024,512]{1,0:T(8,128)}, u32[]{:S(2)}) copy-start(f32[1024,512]{1,0:T(8,128)} %copy-done.21) | copy-start | bytes 6291460
  165.5 15.9 %collective-permute-start.16 = (f32[8,4,8,512]{3,2,1,0:T(8,128)}, f32[8,4,8,512]{3,2,1,0:T(8,128)S(1)}, u32[]{:S(2)}, u32[]{:S(2)}) collective-permute-start(f32[8,4,8,512]{3,2,1,0:T(8,128)} %shard_map.69), channel_id=1, source_target_pairs={{0,1},{1,0},{2,3},{3,2},{4,5},{5,4},{6,7},{7,6},{8,9},{9,8},{10,11... | collective-permute-start | bytes 1572872 | tf_op jit(solution)/shard_map/ppermute | solution.py:22
  165.6 30.4 %collective-permute-start.18 = (f32[8,4,8,512]{3,2,1,0:T(8,128)}, f32[8,4,8,512]{3,2,1,0:T(8,128)S(1)}, u32[]{:S(2)}, u32[]{:S(2)}) collective-permute-start(f32[8,4,8,512]{3,2,1,0:T(8,128)} %shard_map.66), channel_id=1, source_target_pairs={{0,1},{1,0},{2,3},{3,2},{4,5},{5,4},{6,7},{7,6},{8,9},{9,8},{10,11... | collective-permute-start | bytes 1572872 | tf_op jit(solution)/shard_map/ppermute | solution.py:22
  167.0 5.1 %copy-start.12 = (bf16[2048,512]{1,0:T(8,128)(2,1)S(1)}, bf16[2048,512]{1,0:T(8,128)(2,1)}, u32[]{:S(2)}) copy-start(bf16[2048,512]{1,0:T(8,128)(2,1)} %copy-done.11) | copy-start | bytes 6291460
  167.0 5.1 %copy-start.14 = (bf16[2048,512]{1,0:T(8,128)(2,1)S(1)}, bf16[2048,512]{1,0:T(8,128)(2,1)}, u32[]{:S(2)}) copy-start(bf16[2048,512]{1,0:T(8,128)(2,1)} %copy-done.13) | copy-start | bytes 6291460
  167.0 5.1 %copy-start.16 = (bf16[2048,512]{1,0:T(8,128)(2,1)S(1)}, bf16[2048,512]{1,0:T(8,128)(2,1)}, u32[]{:S(2)}) copy-start(bf16[2048,512]{1,0:T(8,128)(2,1)} %copy-done.15) | copy-start | bytes 6291460
  167.0 5.1 %copy-start.18 = (bf16[2048,512]{1,0:T(8,128)(2,1)S(1)}, bf16[2048,512]{1,0:T(8,128)(2,1)}, u32[]{:S(2)}) copy-start(bf16[2048,512]{1,0:T(8,128)(2,1)} %copy-done.17) | copy-start | bytes 6291460
  172.1 12.0 %copy-start.24 = (bf16[2048,512]{1,0:T(8,128)(2,1)S(1)}, bf16[2048,512]{1,0:T(8,128)(2,1)}, u32[]{:S(2)}) copy-start(bf16[2048,512]{1,0:T(8,128)(2,1)} %copy-done.23) | copy-start | bytes 6291460
  172.1 12.0 %copy-start.26 = (bf16[2048,512]{1,0:T(8,128)(2,1)S(1)}, bf16[2048,512]{1,0:T(8,128)(2,1)}, u32[]{:S(2)}) copy-start(bf16[2048,512]{1,0:T(8,128)(2,1)} %copy-done.25) | copy-start | bytes 6291460
  177.0 7.1 %copy-start.20 = (bf16[2048,512]{1,0:T(8,128)(2,1)S(1)}, bf16[2048,512]{1,0:T(8,128)(2,1)}, u32[]{:S(2)}) copy-start(bf16[2048,512]{1,0:T(8,128)(2,1)} %copy-done.19) | copy-start | bytes 6291460
  191.7 5.2 %collective-permute-start.21 = (f32[8,4,8,512]{3,2,1,0:T(8,128)S(1)}, f32[8,4,8,512]{3,2,1,0:T(8,128)S(1)}, u32[]{:S(2)}, u32[]{:S(2)}) collective-permute-start(f32[8,4,8,512]{3,2,1,0:T(8,128)S(1)} %shard_map.75.refs_2_), channel_id=1, source_target_pairs={{0,2},{2,0},{1,3},{3,1},{4,6},{6,4},{5,7},{7,5},{8,10},{10,8},{9,1... | collective-permute-start | bytes 1572872 | tf_op jit(solution)/shard_map/ppermute | solution.py:22
  193.4 6.4 %collective-permute-start.19 = (f32[8,4,8,1024]{3,2,1,0:T(8,128)S(1)}, f32[8,4,8,1024]{3,2,1,0:T(8,128)S(1)}, u32[]{:S(2)}, u32[]{:S(2)}) collective-permute-start(f32[8,4,8,1024]{3,2,1,0:T(8,128)S(1)} %shard_map.71.refs_0_), channel_id=1, source_target_pairs={{0,2},{2,0},{1,3},{3,1},{4,6},{6,4},{5,7},{7,5},{8,10},{10,8},{9,1... | collective-permute-start | bytes 3145736 | tf_op jit(solution)/shard_map/ppermute | solution.py:22
  193.5 24.3 %collective-permute-start.17 = (f32[8,4,8,1024]{3,2,1,0:T(8,128)S(1)}, f32[8,4,8,1024]{3,2,1,0:T(8,128)S(1)}, u32[]{:S(2)}, u32[]{:S(2)}) collective-permute-start(f32[8,4,8,1024]{3,2,1,0:T(8,128)S(1)} %shard_map.73), channel_id=1, source_target_pairs={{0,1},{1,0},{2,3},{3,2},{4,5},{5,4},{6,7},{7,6},{8,9},{9,8},{10,11... | collective-permute-start | bytes 3145736 | tf_op jit(solution)/shard_map/ppermute | solution.py:22
  196.0 2.3 %collective-permute-start.20 = (f32[8,4,8,512]{3,2,1,0:T(8,128)S(1)}, f32[8,4,8,512]{3,2,1,0:T(8,128)S(1)}, u32[]{:S(2)}, u32[]{:S(2)}) collective-permute-start(f32[8,4,8,512]{3,2,1,0:T(8,128)S(1)} %shard_map.74.refs_1_), channel_id=1, source_target_pairs={{0,2},{2,0},{1,3},{3,1},{4,6},{6,4},{5,7},{7,5},{8,10},{10,8},{9,1... | collective-permute-start | bytes 1572872 | tf_op jit(solution)/shard_map/ppermute | solution.py:22
  196.8 2.3 collective-permute-start.22
  196.8 3.0 %collective-permute-start.23 = (f32[8,4,8,512]{3,2,1,0:T(8,128)S(1)}, f32[8,4,8,512]{3,2,1,0:T(8,128)S(1)}, u32[]{:S(2)}, u32[]{:S(2)}) collective-permute-start(f32[8,4,8,512]{3,2,1,0:T(8,128)S(1)} %collective-permute-done.16.refs_4_), channel_id=1, source_target_pairs={{0,2},{2,0},{1,3},{3,1},{4,6},{6,4},{5,7},{7,5},{8,10},{10,8},{9,1... | collective-permute-start | bytes 1572872 | tf_op jit(solution)/shard_map/ppermute | solution.py:22
  217.8 4.0 %collective-permute-start.24 = (f32[8,4,8,1024]{3,2,1,0:T(8,128)S(1)}, f32[8,4,8,1024]{3,2,1,0:T(8,128)S(1)}, u32[]{:S(2)}, u32[]{:S(2)}) collective-permute-start(f32[8,4,8,1024]{3,2,1,0:T(8,128)S(1)} %collective-permute-done.17.refs_0_), channel_id=1, source_target_pairs={{0,2},{2,0},{1,3},{3,1},{4,6},{6,4},{5,7},{7,5},{8,10},{10,8},{9,1... | collective-permute-start | bytes 3145736 | tf_op jit(solution)/shard_map/ppermute | solution.py:22
  220.8 2.0 copy-start.3
  222.8 6.9 %copy-start.1 = (s32[8,16]{1,0:T(8,128)S(1)}, s32[8,16]{1,0:T(8,128)}, u32[]{:S(2)}) copy-start(s32[8,16]{1,0:T(8,128)} %param.5) | copy-start | bytes 1540
  (8 other events, 10.2 us)

commit v4 on v3

--- a/solution.py
+++ b/solution.py
@@ -224,7 +224,7 @@
         mh[...], ml[...] = halves(full[...].reshape(rows, -1))
 
     out = like((rows, deep), BF16)
-    wide = deep // 4
+    wide = deep // 2
     return pl.pallas_call(
         kernel,
         out_shape=[out, out],
@@ -240,7 +240,7 @@
     )(low_id.reshape(1), *blocks)
 
 
-def product(panels, parts, shape, wide=256):
+def product(panels, parts, shape, wide=512):
     deep = panels[0][0].shape[1]
     _, n_low, _, _, k = shape
     tiles = [m[0].shape[0] // (n_low * k) for m in panels]
@@ -285,7 +285,7 @@
     )(*args)
 
 
-def update(base, turned, pieces, in_place, wide=256):
+def update(base, turned, pieces, in_place, wide=512):
     height, width = base.shape
     n = len(pieces)
     tall = height // 2
@@ -463,7 +463,7 @@
         turn((after(own_c[1], last), own_pc[1], far[1], far_p[1]), shape, col_id, same)
     )
     kept = [[product([after_all(first, turned[1][0])], near, shape)]]
-    second = panel(after_all(units[0], kept[0][0], came[1][0]), low_id)
+    second = panel(after_all(units[0], kept[0][0], came[0][0], came[1][0]), low_id)
     last = product([second], far_parts, shape)
     came.append((swap(last, "col", 1), 0, 1, 0))
     came_p = [swap(after(came[i][0], last), "row", 1) for i in range(2)]

time: 230 us -> 227 us (0.987)
  Pallas kernels: 78.2 us -> 71.5 us
  waiting for transfers between devices: 97.6 us -> 101 us
    pallas_call x6, Pallas kernels: 21 us -> 16.3 us  [product(): pl.pallas_call(kernel, out_shape=out, grid=(n * steps,), in_specs=specs,...]
    ppermute x25, waiting for transfers between devices: 78 us -> 81.8 us  [swap(): return lax.ppermute(x, axis, [(i, i ^ bit) for i in range(size)])]
  transfers between devices with their start and end apart: 26 -> 26, of which waited for: 10 -> 11; matrix products, arithmetic and copies ran while one was open for 4% -> 4% of each run, Pallas kernels for 31% -> 25%
where the time goes in v4:
time: 227 us
  waiting for transfers between devices  101 us (44%)
  Pallas kernels  71.5 us (31%)
  starting transfers between devices  27.3 us (12%)
  local copies, waits for them, and re-layouts  25.1 us (11%)
    ppermute x25, waiting for transfers between devices, swap(): return lax.ppermute(x, axis, [(i, i ^ bit) for i in range(size)])  81.8 us
    ppermute x25, starting transfers between devices, swap(): return lax.ppermute(x, axis, [(i, i ^ bit) for i in range(size)])  22 us
    pallas_call x2, Pallas kernels, update(): pl.pallas_call(kernel, out_shape=like(base.shape), grid=(width // wide,),...  20.4 us
    all_to_all x1, waiting for transfers between devices, body(): got = lax.all_to_all(pack(parts), (LOW, 'col'), 0, 0)  19.6 us
    pallas_call x6, Pallas kernels, product(): pl.pallas_call(kernel, out_shape=out, grid=(n * steps,), in_specs=specs,...  16.3 us
    unnamed x60, local copies, waits for them, and re-layouts  16 us
    pallas_call x4, Pallas kernels, split(): pl.pallas_call(kernel, out_shape=[out, out], grid=(2 * steps,), in_specs=...  12.6 us
    pallas_call x2, Pallas kernels, select(): pl.pallas_call(kernel, out_shape=[out] * (n_out * cuts), grid_spec=pltpu....  8.29 us
  transfers between devices with their start and end apart: 26, of which 11 were waited for; matrix products, arithmetic and copies ran while one was open for 4% of the time, Pallas kernels for 25%

profile of v4, /device:TPU:1, one launch (start us, length us, event | category | flops | bytes accessed | tf_op | source)
XLA Modules:
  0.0 226.6 jit_solution(17174264469592363229)
XLA Ops:
  0.7 1.6 copy-done.27
  2.7 1.3 copy-done.10
  4.0 5.3 %all-to-all-start = ((f32[8,2,16,8,256]{4,3,2,1,0:T(8,128)}), f32[8,2,16,8,256]{4,3,2,1,0:T(8,128)S(1)}, u32[]{:S(2)}, u32[]{:S(2)}) async-start(f32[8,2,16,8,256]{4,3,2,1,0:T(8,128)} %copy-done.10), calls=%async_computation | async-start | bytes 4194304 | tf_op jit(solution)/shard_map/all_to_all | solution.py:414
  10.3 4.7 %fusion.15 = (f32[1024,512]{1,0:T(8,128)}, f32[1024,512]{1,0:T(8,128)}) fusion(f32[1024,1024]{1,0:T(8,128)} %bitcast.59), kind=kLoop, calls=%fused_computation.46 | loop fusion | bytes 8388608 | tf_op jit(solution)/shard_map/slice | solution.py:439
  15.0 19.6 %all-to-all-done.refs_0_ = f32[8,2,16,8,256]{4,3,2,1,0:T(8,128)S(1)} async-done(((f32[8,2,16,8,256]{4,3,2,1,0:T(8,128)}), f32[8,2,16,8,256]{4,3,2,1,0:T(8,128)S(1)}, u32[]{:S(2)}, u32[]{:S(2)}) %all-to-all-start) | async-done | bytes 2097184 | tf_op jit(solution)/shard_map/all_to_all | solution.py:414
  34.5 2.5 %collective-permute-start.9 = (f32[1024,512]{1,0:T(8,128)}, f32[1024,512]{1,0:T(8,128)}, u32[]{:S(2)}, u32[]{:S(2)}) collective-permute-start(f32[1024,512]{1,0:T(8,128)} %get-tuple-element.64.a), channel_id=1, source_target_pairs={{0,1},{1,0},{2,3},{3,2},{4,5},{5,4},{6,7},{7,6},{8,9},{9,8},{10,11... | collective-permute-start | bytes 6291464 | tf_op jit(solution)/shard_map/ppermute | solution.py:22
  37.0 1.2 slice_bitcast_fusion
  38.2 2.3 %collective-permute-start.1 = (f32[8,16,8,256]{3,2,1,0:T(8,128)S(1)}, f32[8,16,8,256]{3,2,1,0:T(8,128)S(1)}, u32[]{:S(2)}, u32[]{:S(2)}) collective-permute-start(f32[8,16,8,256]{3,2,1,0:T(8,128)S(1)} %get-tuple-element.115), channel_id=1, source_target_pairs={{0,16},{16,0},{1,17},{17,1},{2,18},{18,2},{3,19},{19,3},{4,20},{20... | collective-permute-start | bytes 3145736 | tf_op jit(solution)/shard_map/ppermute | solution.py:22
  40.5 2.4 %collective-permute-start.3 = (f32[8,2,16,8,256]{4,3,2,1,0:T(8,128)S(1)}, f32[8,2,16,8,256]{4,3,2,1,0:T(8,128)}, u32[]{:S(2)}, u32[]{:S(2)}) collective-permute-start(f32[8,2,16,8,256]{4,3,2,1,0:T(8,128)S(1)} %all-to-all-done.refs_0_), channel_id=1, source_target_pairs={{0,2},{2,0},{1,3},{3,1},{4,6},{6,4},{5,7},{7,5},{8,10},{10,8},{9,1... | collective-permute-start | bytes 6291464 | tf_op jit(solution)/shard_map/ppermute | solution.py:22
  42.9 2.7 %fusion.14 = (f32[1024,512]{1,0:T(8,128)S(1)}, f32[1024,512]{1,0:T(8,128)S(1)}) fusion(f32[1024,1024]{1,0:T(8,128)} %collective-permute-done.2), kind=kLoop, calls=%fused_computation.45 | loop fusion | bytes 8388608 | tf_op jit(solution)/shard_map/slice | solution.py:440
  46.9 1.4 copy-done.11
  48.3 1.3 copy-done.13
  49.7 3.0 %shard_map.61 = (bf16[2048,512]{1,0:T(8,128)(2,1)S(1)}, bf16[2048,512]{1,0:T(8,128)(2,1)S(1)}) custom-call(f32[1024,512]{1,0:T(8,128)} %get-tuple-element.86.a, f32[1024,512]{1,0:T(8,128)S(1)} %get-tuple-element.110.b), custom_call_target="tpu_custom_call" | custom-call | flops 1 | bytes 1 | tf_op jit(solution)/shard_map/pallas_call | solution.py:146
  52.6 1.4 copy-done.15
  54.0 1.3 copy-done.17
  55.3 30.7 %collective-permute-done.1.refs_1_ = f32[8,16,8,256]{3,2,1,0:T(8,128)S(1)} collective-permute-done((f32[8,16,8,256]{3,2,1,0:T(8,128)S(1)}, f32[8,16,8,256]{3,2,1,0:T(8,128)S(1)}, u32[]{:S(2)}, u32[]{:S(2)}) %collective-permute-start.1) | collective-permute-done | bytes 1048608 | tf_op jit(solution)/shard_map/ppermute | solution.py:22
  86.0 1.2 collective-permute-start.10
  88.9 3.7 %collective-permute-done.4.refs_3_ = f32[8,16,8,256]{3,2,1,0:T(8,128)} collective-permute-done((f32[8,16,8,256]{3,2,1,0:T(8,128)S(1)}, f32[8,16,8,256]{3,2,1,0:T(8,128)}, u32[]{:S(2)}, u32[]{:S(2)}) %collective-permute-start.4) | collective-permute-done | bytes 1048608 | tf_op jit(solution)/shard_map/ppermute | solution.py:22
  92.6 4.2 %shard_map.62 = (f32[8,8,2048]{2,1,0:T(8,128)S(1)}, f32[8,8,2048]{2,1,0:T(8,128)}, f32[8,8,2048]{2,1,0:T(8,128)}, f32[8,8,2048]{2,1,0:T(8,128)}) custom-call(s32[4,8]{1,0:T(4,128)S(1)} %get-tuple-element.108.row_at, s32[4,16]{1,0:T(4,128)S(1)} %get-tuple-element.117.col_at, s32[4,16]{1,0:T(4,128)S(1)} %get-tuple-element.116.lane_at, ...), custom_call_target="tpu_custom_call" | custom-call | flops 1 | bytes 1 | tf_op jit(solution)/shard_map/pallas_call | solution.py:101
  97.6 1.2 collective-permute-start.5
  100.3 1.6 copy-done.7
  101.9 1.6 copy-done.9
  103.5 3.4 %shard_map.64 = (bf16[8,512,256]{2,1,0:T(8,128)(2,1)S(1)}, bf16[8,512,256]{2,1,0:T(8,128)(2,1)S(1)}) custom-call(s32[2]{0:T(128)S(1)} %pad_add_fusion.1.flag, f32[8,4,2,2,8,512]{5,4,3,2,1,0:T(8,128)S(1)} %bitcast.39, f32[8,4,2,2,8,512]{5,4,3,2,1,0:T(8,128)S(1)} %bitcast.40, f32[8,4,2,2,8,512]{5,4,3,2,1,0:T(8,128)} %bitcast.10.far, ...), custom_call_target="tpu_custom_call" | custom-call | flops 1 | bytes 1 | tf_op jit(solution)/shard_map/pallas_call | solution.py:197
  106.9 5.0 %shard_map.63 = (bf16[2048,512]{1,0:T(8,128)(2,1)S(1)}, bf16[2048,512]{1,0:T(8,128)(2,1)S(1)}) custom-call(f32[1024,512]{1,0:T(8,128)} %collective-permute-done.9.a, f32[1024,512]{1,0:T(8,128)} %collective-permute-done.10.b), custom_call_target="tpu_custom_call" | custom-call | flops 1 | bytes 1 | tf_op jit(solution)/shard_map/pallas_call | solution.py:146
  112.0 24.4 %collective-permute-done.8.refs_1_ = f32[8,16,8,256]{3,2,1,0:T(8,128)} collective-permute-done((f32[8,16,8,256]{3,2,1,0:T(8,128)}, f32[8,16,8,256]{3,2,1,0:T(8,128)}, u32[]{:S(2)}, u32[]{:S(2)}) %collective-permute-start.8) | collective-permute-done | bytes 1048608 | tf_op jit(solution)/shard_map/ppermute | solution.py:22
  136.4 8.3 %collective-permute-done.7.refs_3_ = f32[8,8,2048]{2,1,0:T(8,128)} collective-permute-done((f32[8,8,2048]{2,1,0:T(8,128)}, f32[8,8,2048]{2,1,0:T(8,128)}, u32[]{:S(2)}, u32[]{:S(2)}) %collective-permute-start.7) | collective-permute-done | bytes 524320 | tf_op jit(solution)/shard_map/ppermute | solution.py:22
  144.7 1.5 collective-permute-start.15
  146.2 1.8 shard_map.65
  148.0 2.6 %shard_map.66 = f32[8,4,8,512]{3,2,1,0:T(8,128)} custom-call(bf16[256,2048]{1,0:T(8,128)(2,1)S(1)} %get-tuple-element.88.refs_0_, bf16[256,2048]{1,0:T(8,128)(2,1)S(1)} %get-tuple-element.89.refs_1_, bf16[2048,512]{1,0:T(8,128)(2,1)S(1)} %get-tuple-element.67.refs_2_, bf16[2048,512]{1,0:T(8,128)(2,1)S(1)} %get-tuple-element.76.refs_3_), custom_call_target="tpu_custom_call" | custom-call | flops 1 | bytes 1 | tf_op jit(solution)/shard_map/pallas_call | solution.py:277
  151.7 4.1 %shard_map.67 = (f32[8,8,2048]{2,1,0:T(8,128)S(1)}, f32[8,8,2048]{2,1,0:T(8,128)}, f32[8,8,2048]{2,1,0:T(8,128)}, f32[8,8,2048]{2,1,0:T(8,128)}) custom-call(s32[4,8]{1,0:T(4,128)S(1)} %get-tuple-element.108.row_at, s32[4,16]{1,0:T(4,128)S(1)} %get-tuple-element.117.col_at, s32[4,16]{1,0:T(4,128)S(1)} %get-tuple-element.116.lane_at, ...), custom_call_target="tpu_custom_call" | custom-call | flops 1 | bytes 1 | tf_op jit(solution)/shard_map/pallas_call | solution.py:101
  155.8 1.2 collective-permute-start.12
  157.0 1.5 collective-permute-start.14
  158.5 3.7 %shard_map.68 = (bf16[2048,512]{1,0:T(8,128)(2,1)S(1)}, bf16[2048,512]{1,0:T(8,128)(2,1)S(1)}) custom-call(f32[1024,512]{1,0:T(8,128)} %collective-permute-done.a, f32[1024,512]{1,0:T(8,128)S(1)} %collective-permute-done.15.b), custom_call_target="tpu_custom_call" | custom-call | flops 1 | bytes 1 | tf_op jit(solution)/shard_map/pallas_call | solution.py:146
  162.3 2.6 %shard_map.69 = f32[8,4,8,512]{3,2,1,0:T(8,128)} custom-call(bf16[256,2048]{1,0:T(8,128)(2,1)S(1)} %get-tuple-element.88.refs_0_, bf16[256,2048]{1,0:T(8,128)(2,1)S(1)} %get-tuple-element.89.refs_1_, bf16[2048,512]{1,0:T(8,128)(2,1)S(1)} %get-tuple-element.84.refs_2_.refs_4_, bf16[2048,512]{1,0:T(8,128)(2,1)S(1)} %get-tuple-element.85.refs_3_.refs_5_), custom_call_target="tpu_custom_call" | custom-call | flops 1 | bytes 1 | tf_op jit(solution)/shard_map/pallas_call | solution.py:277
  166.2 3.7 %shard_map.70 = (bf16[8,512,256]{2,1,0:T(8,128)(2,1)S(1)}, bf16[8,512,256]{2,1,0:T(8,128)(2,1)S(1)}) custom-call(s32[2]{0:T(128)S(1)} %pad_add_fusion.1.flag, f32[8,4,2,2,8,512]{5,4,3,2,1,0:T(8,128)} %bitcast.12.own, f32[8,4,2,2,8,512]{5,4,3,2,1,0:T(8,128)S(1)} %bitcast.38, f32[8,4,2,2,8,512]{5,4,3,2,1,0:T(8,128)} %bitcast.14.far, ...), custom_call_target="tpu_custom_call" | custom-call | flops 1 | bytes 1 | tf_op jit(solution)/shard_map/pallas_call | solution.py:197
  169.9 1.3 copy-done.2
  171.3 3.7 %shard_map.71.refs_0_ = f32[8,4,8,1024]{3,2,1,0:T(8,128)S(1)} custom-call(bf16[256,2048]{1,0:T(8,128)(2,1)S(1)} %get-tuple-element.88.refs_0_, bf16[256,2048]{1,0:T(8,128)(2,1)S(1)} %get-tuple-element.89.refs_1_, bf16[2048,512]{1,0:T(8,128)(2,1)S(1)} %copy-done.12, bf16[2048,512]{1,0:T(8,128)(2,1)S(1)} %copy-done.14, bf16[2048,512]{1,0:T(8,128)(2,1)S(1)} %copy-done.16, ...), custom_call_target="tpu_custom_call" | custom-call | flops 1 | bytes 1 | tf_op jit(solution)/shard_map/pallas_call | solution.py:277
  175.0 6.4 %collective-permute-done.14.refs_3_ = f32[8,8,2048]{2,1,0:T(8,128)} collective-permute-done((f32[8,8,2048]{2,1,0:T(8,128)}, f32[8,8,2048]{2,1,0:T(8,128)}, u32[]{:S(2)}, u32[]{:S(2)}) %collective-permute-start.14) | collective-permute-done | bytes 524320 | tf_op jit(solution)/shard_map/ppermute | solution.py:22
  181.4 1.9 shard_map.72
  183.4 3.9 %shard_map.73 = f32[8,4,8,1024]{3,2,1,0:T(8,128)S(1)} custom-call(bf16[256,2048]{1,0:T(8,128)(2,1)S(1)} %get-tuple-element.98.refs_0_, bf16[256,2048]{1,0:T(8,128)(2,1)S(1)} %get-tuple-element.99.refs_1_, bf16[2048,512]{1,0:T(8,128)(2,1)S(1)} %get-tuple-element.67.refs_2_, bf16[2048,512]{1,0:T(8,128)(2,1)S(1)} %copy-done.20, ...), custom_call_target="tpu_custom_call" | custom-call | flops 1 | bytes 1 | tf_op jit(solution)/shard_map/pallas_call | solution.py:277
  187.3 1.8 shard_map.75.refs_2_
  189.1 1.6 collective-permute-start.21
  191.1 1.8 shard_map.74.refs_1_
  196.7 13.7 %shard_map.78.refs_0_ = f32[1024,1024]{1,0:T(8,128)} custom-call(f32[1024,1024]{1,0:T(8,128)} %bitcast.57, bf16[8,512,256]{2,1,0:T(8,128)(2,1)S(1)} %get-tuple-element.68.refs_1_.refs_6_.refs_11_.refs_17_.refs_23_.refs_29_, bf16[8,512,256]{2,1,0:T(8,128)(2,1)S(1)} %get-tuple-element.100.refs_2_.refs_7_.refs_12_.refs_18_.refs_24_.refs_30_, ...), custom_call_target="tpu_custom_call" | custom-call | flops 1 | bytes 1 | tf_op jit(solution)/shard_map/pallas_call | solution.py:341
  210.4 4.6 %collective-permute-done.18.refs_0_ = f32[8,4,8,1024]{3,2,1,0:T(8,128)S(1)} collective-permute-done((f32[8,4,8,1024]{3,2,1,0:T(8,128)S(1)}, f32[8,4,8,1024]{3,2,1,0:T(8,128)S(1)}, u32[]{:S(2)}, u32[]{:S(2)}) %collective-permute-start.18) | collective-permute-done | bytes 1048608 | tf_op jit(solution)/shard_map/ppermute | solution.py:22
  215.0 1.3 collective-permute-start.24
  216.3 1.7 shard_map.76.refs_1_
  220.0 6.6 %shard_map.79 = f32[1024,1024]{1,0:T(8,128)} custom-call(f32[1024,1024]{1,0:T(8,128)} %shard_map.78.refs_0_, bf16[8,512,256]{2,1,0:T(8,128)(2,1)S(1)} %get-tuple-element.68.refs_1_.refs_6_.refs_11_.refs_17_.refs_23_.refs_29_, ...), custom_call_target="tpu_custom_call", output_to_operand_aliasing={{}: (0, {})} | custom-call | flops 1 | bytes 1 | tf_op jit(solution)/shard_map/pallas_call | solution.py:341
  (96 shorter events, 15.4 us)
Async XLA Ops:
  0.6 86.8 %copy-start = (s32[8,16]{1,0:T(8,128)S(1)}, s32[8,16]{1,0:T(8,128)}, u32[]{:S(2)}) copy-start(s32[8,16]{1,0:T(8,128)} %param.5) | copy-start | bytes 1540
  0.6 1.6 copy-start.27
  4.0 30.5 %all-to-all-start = ((f32[8,2,16,8,256]{4,3,2,1,0:T(8,128)}), f32[8,2,16,8,256]{4,3,2,1,0:T(8,128)S(1)}, u32[]{:S(2)}, u32[]{:S(2)}) async-start(f32[8,2,16,8,256]{4,3,2,1,0:T(8,128)} %copy-done.10), calls=%async_computation | async-start | bytes 4194304 | tf_op jit(solution)/shard_map/all_to_all | solution.py:414
  9.3 33.6 %collective-permute-start.2 = (f32[1024,1024]{1,0:T(8,128)}, f32[1024,1024]{1,0:T(8,128)}, u32[]{:S(2)}, u32[]{:S(2)}) collective-permute-start(f32[1024,1024]{1,0:T(8,128)} %bitcast.58), channel_id=1, source_target_pairs={{0,2},{2,0},{1,3},{3,1},{4,6},{6,4},{5,7},{7,5},{8,10},{10,8},{9,1... | collective-permute-start | bytes 12582920 | tf_op jit(solution)/shard_map/ppermute | solution.py:22
  34.5 51.5 %collective-permute-start.9 = (f32[1024,512]{1,0:T(8,128)}, f32[1024,512]{1,0:T(8,128)}, u32[]{:S(2)}, u32[]{:S(2)}) collective-permute-start(f32[1024,512]{1,0:T(8,128)} %get-tuple-element.64.a), channel_id=1, source_target_pairs={{0,1},{1,0},{2,3},{3,2},{4,5},{5,4},{6,7},{7,6},{8,9},{9,8},{10,11... | collective-permute-start | bytes 6291464 | tf_op jit(solution)/shard_map/ppermute | solution.py:22
  38.2 7.4 %copy-start.6 = (f32[1024,512]{1,0:T(8,128)S(1)}, f32[1024,512]{1,0:T(8,128)}, u32[]{:S(2)}) copy-start(f32[1024,512]{1,0:T(8,128)} %get-tuple-element.64.a) | copy-start | bytes 6291460
  38.2 47.8 %collective-permute-start.1 = (f32[8,16,8,256]{3,2,1,0:T(8,128)S(1)}, f32[8,16,8,256]{3,2,1,0:T(8,128)S(1)}, u32[]{:S(2)}, u32[]{:S(2)}) collective-permute-start(f32[8,16,8,256]{3,2,1,0:T(8,128)S(1)} %get-tuple-element.115), channel_id=1, source_target_pairs={{0,16},{16,0},{1,17},{17,1},{2,18},{18,2},{3,19},{19,3},{4,20},{20... | collective-permute-start | bytes 3145736 | tf_op jit(solution)/shard_map/ppermute | solution.py:22
  40.5 48.4 %collective-permute-start.3 = (f32[8,2,16,8,256]{4,3,2,1,0:T(8,128)S(1)}, f32[8,2,16,8,256]{4,3,2,1,0:T(8,128)}, u32[]{:S(2)}, u32[]{:S(2)}) collective-permute-start(f32[8,2,16,8,256]{4,3,2,1,0:T(8,128)S(1)} %all-to-all-done.refs_0_), channel_id=1, source_target_pairs={{0,2},{2,0},{1,3},{3,1},{4,6},{6,4},{5,7},{7,5},{8,10},{10,8},{9,1... | collective-permute-start | bytes 6291464 | tf_op jit(solution)/shard_map/ppermute | solution.py:22
  45.6 4.1 %copy-start.4 = (f32[1024,512]{1,0:T(8,128)}, f32[1024,512]{1,0:T(8,128)S(1)}, u32[]{:S(2)}) copy-start(f32[1024,512]{1,0:T(8,128)S(1)} %get-tuple-element.110.b) | copy-start | bytes 6291460
  86.0 13.1 %collective-permute-start.10 = (f32[1024,512]{1,0:T(8,128)}, f32[1024,512]{1,0:T(8,128)}, u32[]{:S(2)}, u32[]{:S(2)}) collective-permute-start(f32[1024,512]{1,0:T(8,128)} %collective-permute-done.9.a), channel_id=1, source_target_pairs={{0,2},{2,0},{1,3},{3,1},{4,6},{6,4},{5,7},{7,5},{8,10},{10,8},{9,1... | collective-permute-start | bytes 6291464 | tf_op jit(solution)/shard_map/ppermute | solution.py:22
  87.2 49.2 %collective-permute-start = (f32[1024,512]{1,0:T(8,128)}, f32[1024,512]{1,0:T(8,128)}, u32[]{:S(2)}, u32[]{:S(2)}) collective-permute-start(f32[1024,512]{1,0:T(8,128)} %get-tuple-element.86.a), channel_id=1, source_target_pairs={{0,1},{1,0},{2,3},{3,2},{4,5},{5,4},{6,7},{7,6},{8,9},{9,8},{10,11... | collective-permute-start | bytes 6291464 | tf_op jit(solution)/shard_map/ppermute | solution.py:22
  87.2 5.4 %collective-permute-start.4 = (f32[8,16,8,256]{3,2,1,0:T(8,128)S(1)}, f32[8,16,8,256]{3,2,1,0:T(8,128)}, u32[]{:S(2)}, u32[]{:S(2)}) collective-permute-start(f32[8,16,8,256]{3,2,1,0:T(8,128)S(1)} %collective-permute-done.1.refs_1_), channel_id=1, source_target_pairs={{0,2},{2,0},{1,3},{3,1},{4,6},{6,4},{5,7},{7,5},{8,10},{10,8},{9,1... | collective-permute-start | bytes 3145736 | tf_op jit(solution)/shard_map/ppermute | solution.py:22
  88.0 48.3 %collective-permute-start.8 = (f32[8,16,8,256]{3,2,1,0:T(8,128)}, f32[8,16,8,256]{3,2,1,0:T(8,128)}, u32[]{:S(2)}, u32[]{:S(2)}) collective-permute-start(f32[8,16,8,256]{3,2,1,0:T(8,128)} %get-tuple-element.63), channel_id=1, source_target_pairs={{0,16},{16,0},{1,17},{17,1},{2,18},{18,2},{3,19},{19,3},{4,20},{20... | collective-permute-start | bytes 3145736 | tf_op jit(solution)/shard_map/ppermute | solution.py:22
  97.6 38.8 %collective-permute-start.5 = (f32[8,8,2048]{2,1,0:T(8,128)}, f32[8,8,2048]{2,1,0:T(8,128)S(1)}, u32[]{:S(2)}, u32[]{:S(2)}) collective-permute-start(f32[8,8,2048]{2,1,0:T(8,128)} %get-tuple-element.60), channel_id=1, source_target_pairs={{0,4},{4,0},{8,12},{12,8},{1,5},{5,1},{9,13},{13,9},{2,6},{6,2},{1... | collective-permute-start | bytes 1572872 | tf_op jit(solution)/shard_map/ppermute | solution.py:22
  98.8 37.6 %collective-permute-start.6 = (f32[8,8,2048]{2,1,0:T(8,128)}, f32[8,8,2048]{2,1,0:T(8,128)S(1)}, u32[]{:S(2)}, u32[]{:S(2)}) collective-permute-start(f32[8,8,2048]{2,1,0:T(8,128)} %get-tuple-element.61), channel_id=1, source_target_pairs={{0,8},{4,12},{8,0},{12,4},{1,9},{5,13},{9,1},{13,5},{2,10},{6,14},... | collective-permute-start | bytes 1572872 | tf_op jit(solution)/shard_map/ppermute | solution.py:22
  99.1 45.6 %collective-permute-start.7 = (f32[8,8,2048]{2,1,0:T(8,128)}, f32[8,8,2048]{2,1,0:T(8,128)}, u32[]{:S(2)}, u32[]{:S(2)}) collective-permute-start(f32[8,8,2048]{2,1,0:T(8,128)} %get-tuple-element.62), channel_id=1, source_target_pairs={{0,12},{4,8},{8,4},{12,0},{1,13},{5,9},{9,5},{13,1},{2,14},{6,10},... | collective-permute-start | bytes 1572872 | tf_op jit(solution)/shard_map/ppermute | solution.py:22
  100.3 1.6 copy-start.7
  101.9 1.6 copy-start.9
  106.9 39.3 %copy-start.29 = (f32[8,8,2048]{2,1,0:T(8,128)S(1)}, f32[8,8,2048]{2,1,0:T(8,128)}, u32[]{:S(2)}) copy-start(f32[8,8,2048]{2,1,0:T(8,128)} %copy-done.28) | copy-start | bytes 1572868
  111.9 38.7 %copy-start.19 = (bf16[2048,512]{1,0:T(8,128)(2,1)}, bf16[2048,512]{1,0:T(8,128)(2,1)S(1)}, u32[]{:S(2)}) copy-start(bf16[2048,512]{1,0:T(8,128)(2,1)S(1)} %get-tuple-element.76.refs_3_) | copy-start | bytes 6291460
  144.7 13.8 %collective-permute-start.15 = (f32[1024,512]{1,0:T(8,128)}, f32[1024,512]{1,0:T(8,128)S(1)}, u32[]{:S(2)}, u32[]{:S(2)}) collective-permute-start(f32[1024,512]{1,0:T(8,128)} %collective-permute-done.a), channel_id=1, source_target_pairs={{0,2},{2,0},{1,3},{3,1},{4,6},{6,4},{5,7},{7,5},{8,10},{10,8},{9,1... | collective-permute-start | bytes 6291464 | tf_op jit(solution)/shard_map/ppermute | solution.py:22
  146.2 5.5 %collective-permute-start.11 = (f32[8,16,8,256]{3,2,1,0:T(8,128)}, f32[8,16,8,256]{3,2,1,0:T(8,128)S(1)}, u32[]{:S(2)}, u32[]{:S(2)}) collective-permute-start(f32[8,16,8,256]{3,2,1,0:T(8,128)} %collective-permute-done.8.refs_1_), channel_id=1, source_target_pairs={{0,2},{2,0},{1,3},{3,1},{4,6},{6,4},{5,7},{7,5},{8,10},{10,8},{9,1... | collective-permute-start | bytes 3145736 | tf_op jit(solution)/shard_map/ppermute | solution.py:22
  150.6 24.4 %collective-permute-start.16 = (f32[8,4,8,512]{3,2,1,0:T(8,128)}, f32[8,4,8,512]{3,2,1,0:T(8,128)S(1)}, u32[]{:S(2)}, u32[]{:S(2)}) collective-permute-start(f32[8,4,8,512]{3,2,1,0:T(8,128)} %shard_map.66), channel_id=1, source_target_pairs={{0,1},{1,0},{2,3},{3,2},{4,5},{5,4},{6,7},{7,6},{8,9},{9,8},{10,11... | collective-permute-start | bytes 1572872 | tf_op jit(solution)/shard_map/ppermute | solution.py:22
  155.8 19.2 %collective-permute-start.12 = (f32[8,8,2048]{2,1,0:T(8,128)}, f32[8,8,2048]{2,1,0:T(8,128)}, u32[]{:S(2)}, u32[]{:S(2)}) collective-permute-start(f32[8,8,2048]{2,1,0:T(8,128)} %get-tuple-element.79), channel_id=1, source_target_pairs={{0,4},{4,0},{8,12},{12,8},{1,5},{5,1},{9,13},{13,9},{2,6},{6,2},{1... | collective-permute-start | bytes 1572872 | tf_op jit(solution)/shard_map/ppermute | solution.py:22
  157.0 18.0 %collective-permute-start.13 = (f32[8,8,2048]{2,1,0:T(8,128)}, f32[8,8,2048]{2,1,0:T(8,128)}, u32[]{:S(2)}, u32[]{:S(2)}) collective-permute-start(f32[8,8,2048]{2,1,0:T(8,128)} %get-tuple-element.80), channel_id=1, source_target_pairs={{0,8},{4,12},{8,0},{12,4},{1,9},{5,13},{9,1},{13,5},{2,10},{6,14},... | collective-permute-start | bytes 1572872 | tf_op jit(solution)/shard_map/ppermute | solution.py:22
  157.0 24.4 %collective-permute-start.14 = (f32[8,8,2048]{2,1,0:T(8,128)}, f32[8,8,2048]{2,1,0:T(8,128)}, u32[]{:S(2)}, u32[]{:S(2)}) collective-permute-start(f32[8,8,2048]{2,1,0:T(8,128)} %get-tuple-element.81), channel_id=1, source_target_pairs={{0,12},{4,8},{8,4},{12,0},{1,13},{5,9},{9,5},{13,1},{2,14},{6,10},... | collective-permute-start | bytes 1572872 | tf_op jit(solution)/shard_map/ppermute | solution.py:22
  158.5 3.7 %copy-start.21 = (f32[1024,512]{1,0:T(8,128)}, f32[1024,512]{1,0:T(8,128)S(1)}, u32[]{:S(2)}) copy-start(f32[1024,512]{1,0:T(8,128)S(1)} %collective-permute-done.15.b) | copy-start | bytes 6291460
  162.3 2.6 %copy-start.23 = (bf16[2048,512]{1,0:T(8,128)(2,1)}, bf16[2048,512]{1,0:T(8,128)(2,1)S(1)}, u32[]{:S(2)}) copy-start(bf16[2048,512]{1,0:T(8,128)(2,1)S(1)} %get-tuple-element.84.refs_2_.refs_4_) | copy-start | bytes 6291460
  162.3 2.6 %copy-start.25 = (bf16[2048,512]{1,0:T(8,128)(2,1)}, bf16[2048,512]{1,0:T(8,128)(2,1)S(1)}, u32[]{:S(2)}) copy-start(bf16[2048,512]{1,0:T(8,128)(2,1)S(1)} %get-tuple-element.85.refs_3_.refs_5_) | copy-start | bytes 6291460
  162.3 3.2 %copy-start.5 = (f32[1024,512]{1,0:T(8,128)S(1)}, f32[1024,512]{1,0:T(8,128)}, u32[]{:S(2)}) copy-start(f32[1024,512]{1,0:T(8,128)} %copy-done.4) | copy-start | bytes 6291460
  162.3 3.9 %copy-start.22 = (f32[1024,512]{1,0:T(8,128)S(1)}, f32[1024,512]{1,0:T(8,128)}, u32[]{:S(2)}) copy-start(f32[1024,512]{1,0:T(8,128)} %copy-done.21) | copy-start | bytes 6291460
  164.9 16.5 %collective-permute-start.17 = (f32[8,4,8,512]{3,2,1,0:T(8,128)}, f32[8,4,8,512]{3,2,1,0:T(8,128)S(1)}, u32[]{:S(2)}, u32[]{:S(2)}) collective-permute-start(f32[8,4,8,512]{3,2,1,0:T(8,128)} %shard_map.69), channel_id=1, source_target_pairs={{0,1},{1,0},{2,3},{3,2},{4,5},{5,4},{6,7},{7,6},{8,9},{9,8},{10,11... | collective-permute-start | bytes 1572872 | tf_op jit(solution)/shard_map/ppermute | solution.py:22
  166.2 5.1 %copy-start.12 = (bf16[2048,512]{1,0:T(8,128)(2,1)S(1)}, bf16[2048,512]{1,0:T(8,128)(2,1)}, u32[]{:S(2)}) copy-start(bf16[2048,512]{1,0:T(8,128)(2,1)} %copy-done.11) | copy-start | bytes 6291460
  166.2 5.1 %copy-start.14 = (bf16[2048,512]{1,0:T(8,128)(2,1)S(1)}, bf16[2048,512]{1,0:T(8,128)(2,1)}, u32[]{:S(2)}) copy-start(bf16[2048,512]{1,0:T(8,128)(2,1)} %copy-done.13) | copy-start | bytes 6291460
  166.2 5.1 %copy-start.16 = (bf16[2048,512]{1,0:T(8,128)(2,1)S(1)}, bf16[2048,512]{1,0:T(8,128)(2,1)}, u32[]{:S(2)}) copy-start(bf16[2048,512]{1,0:T(8,128)(2,1)} %copy-done.15) | copy-start | bytes 6291460
  166.2 5.1 %copy-start.18 = (bf16[2048,512]{1,0:T(8,128)(2,1)S(1)}, bf16[2048,512]{1,0:T(8,128)(2,1)}, u32[]{:S(2)}) copy-start(bf16[2048,512]{1,0:T(8,128)(2,1)} %copy-done.17) | copy-start | bytes 6291460
  171.3 12.1 %copy-start.24 = (bf16[2048,512]{1,0:T(8,128)(2,1)S(1)}, bf16[2048,512]{1,0:T(8,128)(2,1)}, u32[]{:S(2)}) copy-start(bf16[2048,512]{1,0:T(8,128)(2,1)} %copy-done.23) | copy-start | bytes 6291460
  171.3 12.1 %copy-start.26 = (bf16[2048,512]{1,0:T(8,128)(2,1)S(1)}, bf16[2048,512]{1,0:T(8,128)(2,1)}, u32[]{:S(2)}) copy-start(bf16[2048,512]{1,0:T(8,128)(2,1)} %copy-done.25) | copy-start | bytes 6291460
  175.0 8.4 %copy-start.20 = (bf16[2048,512]{1,0:T(8,128)(2,1)S(1)}, bf16[2048,512]{1,0:T(8,128)(2,1)}, u32[]{:S(2)}) copy-start(bf16[2048,512]{1,0:T(8,128)(2,1)} %copy-done.19) | copy-start | bytes 6291460
  189.1 4.7 %collective-permute-start.21 = (f32[8,4,8,512]{3,2,1,0:T(8,128)S(1)}, f32[8,4,8,512]{3,2,1,0:T(8,128)S(1)}, u32[]{:S(2)}, u32[]{:S(2)}) collective-permute-start(f32[8,4,8,512]{3,2,1,0:T(8,128)S(1)} %shard_map.75.refs_2_), channel_id=1, source_target_pairs={{0,2},{2,0},{1,3},{3,1},{4,6},{6,4},{5,7},{7,5},{8,10},{10,8},{9,1... | collective-permute-start | bytes 1572872 | tf_op jit(solution)/shard_map/ppermute | solution.py:22
  190.7 6.0 %collective-permute-start.19 = (f32[8,4,8,1024]{3,2,1,0:T(8,128)S(1)}, f32[8,4,8,1024]{3,2,1,0:T(8,128)S(1)}, u32[]{:S(2)}, u32[]{:S(2)}) collective-permute-start(f32[8,4,8,1024]{3,2,1,0:T(8,128)S(1)} %shard_map.71.refs_0_), channel_id=1, source_target_pairs={{0,2},{2,0},{1,3},{3,1},{4,6},{6,4},{5,7},{7,5},{8,10},{10,8},{9,1... | collective-permute-start | bytes 3145736 | tf_op jit(solution)/shard_map/ppermute | solution.py:22
  190.7 24.3 %collective-permute-start.18 = (f32[8,4,8,1024]{3,2,1,0:T(8,128)S(1)}, f32[8,4,8,1024]{3,2,1,0:T(8,128)S(1)}, u32[]{:S(2)}, u32[]{:S(2)}) collective-permute-start(f32[8,4,8,1024]{3,2,1,0:T(8,128)S(1)} %shard_map.73), channel_id=1, source_target_pairs={{0,1},{1,0},{2,3},{3,2},{4,5},{5,4},{6,7},{7,6},{8,9},{9,8},{10,11... | collective-permute-start | bytes 3145736 | tf_op jit(solution)/shard_map/ppermute | solution.py:22
  192.9 2.3 %collective-permute-start.20 = (f32[8,4,8,512]{3,2,1,0:T(8,128)S(1)}, f32[8,4,8,512]{3,2,1,0:T(8,128)S(1)}, u32[]{:S(2)}, u32[]{:S(2)}) collective-permute-start(f32[8,4,8,512]{3,2,1,0:T(8,128)S(1)} %shard_map.74.refs_1_), channel_id=1, source_target_pairs={{0,2},{2,0},{1,3},{3,1},{4,6},{6,4},{5,7},{7,5},{8,10},{10,8},{9,1... | collective-permute-start | bytes 1572872 | tf_op jit(solution)/shard_map/ppermute | solution.py:22
  193.7 2.3 %collective-permute-start.22 = (f32[8,4,8,512]{3,2,1,0:T(8,128)S(1)}, f32[8,4,8,512]{3,2,1,0:T(8,128)S(1)}, u32[]{:S(2)}, u32[]{:S(2)}) collective-permute-start(f32[8,4,8,512]{3,2,1,0:T(8,128)S(1)} %collective-permute-done.16.refs_3_), channel_id=1, source_target_pairs={{0,2},{2,0},{1,3},{3,1},{4,6},{6,4},{5,7},{7,5},{8,10},{10,8},{9,1... | collective-permute-start | bytes 1572872 | tf_op jit(solution)/shard_map/ppermute | solution.py:22
  193.7 3.0 %collective-permute-start.23 = (f32[8,4,8,512]{3,2,1,0:T(8,128)S(1)}, f32[8,4,8,512]{3,2,1,0:T(8,128)S(1)}, u32[]{:S(2)}, u32[]{:S(2)}) collective-permute-start(f32[8,4,8,512]{3,2,1,0:T(8,128)S(1)} %collective-permute-done.17.refs_4_), channel_id=1, source_target_pairs={{0,2},{2,0},{1,3},{3,1},{4,6},{6,4},{5,7},{7,5},{8,10},{10,8},{9,1... | collective-permute-start | bytes 1572872 | tf_op jit(solution)/shard_map/ppermute | solution.py:22
  215.0 4.0 %collective-permute-start.24 = (f32[8,4,8,1024]{3,2,1,0:T(8,128)S(1)}, f32[8,4,8,1024]{3,2,1,0:T(8,128)S(1)}, u32[]{:S(2)}, u32[]{:S(2)}) collective-permute-start(f32[8,4,8,1024]{3,2,1,0:T(8,128)S(1)} %collective-permute-done.18.refs_0_), channel_id=1, source_target_pairs={{0,2},{2,0},{1,3},{3,1},{4,6},{6,4},{5,7},{7,5},{8,10},{10,8},{9,1... | collective-permute-start | bytes 3145736 | tf_op jit(solution)/shard_map/ppermute | solution.py:22
  218.0 2.0 copy-start.3
  220.0 6.6 %copy-start.1 = (s32[8,16]{1,0:T(8,128)S(1)}, s32[8,16]{1,0:T(8,128)}, u32[]{:S(2)}) copy-start(s32[8,16]{1,0:T(8,128)} %param.5) | copy-start | bytes 1540
  (8 other events, 10.2 us)

commit v5 on v4

--- a/solution.py
+++ b/solution.py
@@ -127,7 +127,7 @@
     return d(ah, bh) + (d(ah, bl) + d(al, bh))
 
 
-def split(top, bottom, block=256):
+def split(top, bottom, block=512):
     rows, width = top.shape
     steps = rows // block
 
@@ -224,7 +224,7 @@
         mh[...], ml[...] = halves(full[...].reshape(rows, -1))
 
     out = like((rows, deep), BF16)
-    wide = deep // 2
+    wide = deep
     return pl.pallas_call(
         kernel,
         out_shape=[out, out],

time: 227 us -> 227 us (level)
  waiting for transfers between devices: 101 us -> 105 us
  Pallas kernels: 71.5 us -> 68 us
    pallas_call x4, Pallas kernels: 12.6 us -> 8.99 us  [split(): pl.pallas_call(kernel, out_shape=[out, out], grid=(2 * steps,), in_specs=...]
    ppermute x25, waiting for transfers between devices: 81.8 us -> 85.1 us  [swap(): return lax.ppermute(x, axis, [(i, i ^ bit) for i in range(size)])]
  transfers between devices with their start and end apart: 26 -> 26, of which waited for: 11 -> 11; matrix products, arithmetic and copies ran while one was open for 4% -> 4% of each run, Pallas kernels for 25% -> 24%
where the time goes in v5:
time: 227 us
  waiting for transfers between devices  105 us (46%)
  Pallas kernels  68 us (30%)
  starting transfers between devices  27.2 us (12%)
  local copies, waits for them, and re-layouts  25.4 us (11%)
    ppermute x25, waiting for transfers between devices, swap(): return lax.ppermute(x, axis, [(i, i ^ bit) for i in range(size)])  85.1 us
    ppermute x25, starting transfers between devices, swap(): return lax.ppermute(x, axis, [(i, i ^ bit) for i in range(size)])  21.9 us
    pallas_call x2, Pallas kernels, update(): pl.pallas_call(kernel, out_shape=like(base.shape), grid=(width // wide,),...  20.4 us
    all_to_all x1, waiting for transfers between devices, body(): got = lax.all_to_all(pack(parts), (LOW, 'col'), 0, 0)  19.6 us
    pallas_call x6, Pallas kernels, product(): pl.pallas_call(kernel, out_shape=out, grid=(n * steps,), in_specs=specs,...  16.3 us
    unnamed x60, local copies, waits for them, and re-layouts  16.3 us
    pallas_call x4, Pallas kernels, split(): pl.pallas_call(kernel, out_shape=[out, out], grid=(2 * steps,), in_specs=...  8.99 us
    pallas_call x2, Pallas kernels, select(): pl.pallas_call(kernel, out_shape=[out] * (n_out * cuts), grid_spec=pltpu....  8.29 us
  transfers between devices with their start and end apart: 26, of which 11 were waited for; matrix products, arithmetic and copies ran while one was open for 4% of the time, Pallas kernels for 24%

profile of v5, /device:TPU:1, one launch (start us, length us, event | category | flops | bytes accessed | tf_op | source)
XLA Modules:
  0.0 226.6 jit_solution(16516261110739953429)
XLA Ops:
  0.7 1.6 copy-done.27
  2.7 1.3 copy-done.10
  4.0 5.3 %all-to-all-start = ((f32[8,2,16,8,256]{4,3,2,1,0:T(8,128)}), f32[8,2,16,8,256]{4,3,2,1,0:T(8,128)S(1)}, u32[]{:S(2)}, u32[]{:S(2)}) async-start(f32[8,2,16,8,256]{4,3,2,1,0:T(8,128)} %copy-done.10), calls=%async_computation | async-start | bytes 4194304 | tf_op jit(solution)/shard_map/all_to_all | solution.py:414
  10.3 4.7 %fusion.15 = (f32[1024,512]{1,0:T(8,128)}, f32[1024,512]{1,0:T(8,128)}) fusion(f32[1024,1024]{1,0:T(8,128)} %bitcast.59), kind=kLoop, calls=%fused_computation.46 | loop fusion | bytes 8388608 | tf_op jit(solution)/shard_map/slice | solution.py:439
  15.0 19.6 %all-to-all-done.refs_0_ = f32[8,2,16,8,256]{4,3,2,1,0:T(8,128)S(1)} async-done(((f32[8,2,16,8,256]{4,3,2,1,0:T(8,128)}), f32[8,2,16,8,256]{4,3,2,1,0:T(8,128)S(1)}, u32[]{:S(2)}, u32[]{:S(2)}) %all-to-all-start) | async-done | bytes 2097184 | tf_op jit(solution)/shard_map/all_to_all | solution.py:414
  34.5 2.5 %collective-permute-start.9 = (f32[1024,512]{1,0:T(8,128)}, f32[1024,512]{1,0:T(8,128)}, u32[]{:S(2)}, u32[]{:S(2)}) collective-permute-start(f32[1024,512]{1,0:T(8,128)} %get-tuple-element.64.a), channel_id=1, source_target_pairs={{0,1},{1,0},{2,3},{3,2},{4,5},{5,4},{6,7},{7,6},{8,9},{9,8},{10,11... | collective-permute-start | bytes 6291464 | tf_op jit(solution)/shard_map/ppermute | solution.py:22
  37.0 1.2 slice_bitcast_fusion
  38.2 2.3 %collective-permute-start.1 = (f32[8,16,8,256]{3,2,1,0:T(8,128)S(1)}, f32[8,16,8,256]{3,2,1,0:T(8,128)S(1)}, u32[]{:S(2)}, u32[]{:S(2)}) collective-permute-start(f32[8,16,8,256]{3,2,1,0:T(8,128)S(1)} %get-tuple-element.115), channel_id=1, source_target_pairs={{0,16},{16,0},{1,17},{17,1},{2,18},{18,2},{3,19},{19,3},{4,20},{20... | collective-permute-start | bytes 3145736 | tf_op jit(solution)/shard_map/ppermute | solution.py:22
  40.5 2.4 %collective-permute-start.3 = (f32[8,2,16,8,256]{4,3,2,1,0:T(8,128)S(1)}, f32[8,2,16,8,256]{4,3,2,1,0:T(8,128)}, u32[]{:S(2)}, u32[]{:S(2)}) collective-permute-start(f32[8,2,16,8,256]{4,3,2,1,0:T(8,128)S(1)} %all-to-all-done.refs_0_), channel_id=1, source_target_pairs={{0,2},{2,0},{1,3},{3,1},{4,6},{6,4},{5,7},{7,5},{8,10},{10,8},{9,1... | collective-permute-start | bytes 6291464 | tf_op jit(solution)/shard_map/ppermute | solution.py:22
  42.9 2.7 %fusion.14 = (f32[1024,512]{1,0:T(8,128)S(1)}, f32[1024,512]{1,0:T(8,128)S(1)}) fusion(f32[1024,1024]{1,0:T(8,128)} %collective-permute-done.2), kind=kLoop, calls=%fused_computation.45 | loop fusion | bytes 8388608 | tf_op jit(solution)/shard_map/slice | solution.py:440
  46.9 1.4 copy-done.11
  48.3 1.3 copy-done.13
  49.7 2.0 shard_map.61
  51.7 1.4 copy-done.15
  53.1 1.3 copy-done.17
  54.4 31.6 %collective-permute-done.1.refs_1_ = f32[8,16,8,256]{3,2,1,0:T(8,128)S(1)} collective-permute-done((f32[8,16,8,256]{3,2,1,0:T(8,128)S(1)}, f32[8,16,8,256]{3,2,1,0:T(8,128)S(1)}, u32[]{:S(2)}, u32[]{:S(2)}) %collective-permute-start.1) | collective-permute-done | bytes 1048608 | tf_op jit(solution)/shard_map/ppermute | solution.py:22
  86.0 1.2 collective-permute-start.10
  88.9 3.7 %collective-permute-done.4.refs_3_ = f32[8,16,8,256]{3,2,1,0:T(8,128)} collective-permute-done((f32[8,16,8,256]{3,2,1,0:T(8,128)S(1)}, f32[8,16,8,256]{3,2,1,0:T(8,128)}, u32[]{:S(2)}, u32[]{:S(2)}) %collective-permute-start.4) | collective-permute-done | bytes 1048608 | tf_op jit(solution)/shard_map/ppermute | solution.py:22
  92.6 4.2 %shard_map.62 = (f32[8,8,2048]{2,1,0:T(8,128)S(1)}, f32[8,8,2048]{2,1,0:T(8,128)}, f32[8,8,2048]{2,1,0:T(8,128)}, f32[8,8,2048]{2,1,0:T(8,128)}) custom-call(s32[4,8]{1,0:T(4,128)S(1)} %get-tuple-element.108.row_at, s32[4,16]{1,0:T(4,128)S(1)} %get-tuple-element.117.col_at, s32[4,16]{1,0:T(4,128)S(1)} %get-tuple-element.116.lane_at, ...), custom_call_target="tpu_custom_call" | custom-call | flops 1 | bytes 1 | tf_op jit(solution)/shard_map/pallas_call | solution.py:101
  97.6 1.2 collective-permute-start.5
  100.3 1.6 copy-done.7
  101.9 1.6 copy-done.9
  103.5 3.4 %shard_map.64 = (bf16[8,512,256]{2,1,0:T(8,128)(2,1)S(1)}, bf16[8,512,256]{2,1,0:T(8,128)(2,1)S(1)}) custom-call(s32[2]{0:T(128)S(1)} %pad_add_fusion.1.flag, f32[8,4,2,2,8,512]{5,4,3,2,1,0:T(8,128)S(1)} %bitcast.39, f32[8,4,2,2,8,512]{5,4,3,2,1,0:T(8,128)S(1)} %bitcast.40, f32[8,4,2,2,8,512]{5,4,3,2,1,0:T(8,128)} %bitcast.10.far, ...), custom_call_target="tpu_custom_call" | custom-call | flops 1 | bytes 1 | tf_op jit(solution)/shard_map/pallas_call | solution.py:197
  106.9 3.5 %shard_map.63 = (bf16[2048,512]{1,0:T(8,128)(2,1)S(1)}, bf16[2048,512]{1,0:T(8,128)(2,1)S(1)}) custom-call(f32[1024,512]{1,0:T(8,128)} %collective-permute-done.9.a, f32[1024,512]{1,0:T(8,128)} %collective-permute-done.10.b), custom_call_target="tpu_custom_call" | custom-call | flops 1 | bytes 1 | tf_op jit(solution)/shard_map/pallas_call | solution.py:146
  110.4 26.0 %collective-permute-done.8.refs_1_ = f32[8,16,8,256]{3,2,1,0:T(8,128)} collective-permute-done((f32[8,16,8,256]{3,2,1,0:T(8,128)}, f32[8,16,8,256]{3,2,1,0:T(8,128)}, u32[]{:S(2)}, u32[]{:S(2)}) %collective-permute-start.8) | collective-permute-done | bytes 1048608 | tf_op jit(solution)/shard_map/ppermute | solution.py:22
  136.4 8.3 %collective-permute-done.7.refs_3_ = f32[8,8,2048]{2,1,0:T(8,128)} collective-permute-done((f32[8,8,2048]{2,1,0:T(8,128)}, f32[8,8,2048]{2,1,0:T(8,128)}, u32[]{:S(2)}, u32[]{:S(2)}) %collective-permute-start.7) | collective-permute-done | bytes 524320 | tf_op jit(solution)/shard_map/ppermute | solution.py:22
  144.7 1.5 collective-permute-start.15
  146.2 1.7 shard_map.65
  148.0 2.6 %shard_map.66 = f32[8,4,8,512]{3,2,1,0:T(8,128)} custom-call(bf16[256,2048]{1,0:T(8,128)(2,1)S(1)} %get-tuple-element.88.refs_0_, bf16[256,2048]{1,0:T(8,128)(2,1)S(1)} %get-tuple-element.89.refs_1_, bf16[2048,512]{1,0:T(8,128)(2,1)S(1)} %get-tuple-element.67.refs_2_, bf16[2048,512]{1,0:T(8,128)(2,1)S(1)} %get-tuple-element.76.refs_3_), custom_call_target="tpu_custom_call" | custom-call | flops 1 | bytes 1 | tf_op jit(solution)/shard_map/pallas_call | solution.py:277
  151.7 4.1 %shard_map.67 = (f32[8,8,2048]{2,1,0:T(8,128)S(1)}, f32[8,8,2048]{2,1,0:T(8,128)}, f32[8,8,2048]{2,1,0:T(8,128)}, f32[8,8,2048]{2,1,0:T(8,128)}) custom-call(s32[4,8]{1,0:T(4,128)S(1)} %get-tuple-element.108.row_at, s32[4,16]{1,0:T(4,128)S(1)} %get-tuple-element.117.col_at, s32[4,16]{1,0:T(4,128)S(1)} %get-tuple-element.116.lane_at, ...), custom_call_target="tpu_custom_call" | custom-call | flops 1 | bytes 1 | tf_op jit(solution)/shard_map/pallas_call | solution.py:101
  155.8 1.2 collective-permute-start.12
  157.0 1.5 collective-permute-start.14
  158.5 2.8 %shard_map.68 = (bf16[2048,512]{1,0:T(8,128)(2,1)S(1)}, bf16[2048,512]{1,0:T(8,128)(2,1)S(1)}) custom-call(f32[1024,512]{1,0:T(8,128)} %collective-permute-done.a, f32[1024,512]{1,0:T(8,128)S(1)} %collective-permute-done.15.b), custom_call_target="tpu_custom_call" | custom-call | flops 1 | bytes 1 | tf_op jit(solution)/shard_map/pallas_call | solution.py:146
  161.4 2.6 %shard_map.69 = f32[8,4,8,512]{3,2,1,0:T(8,128)} custom-call(bf16[256,2048]{1,0:T(8,128)(2,1)S(1)} %get-tuple-element.88.refs_0_, bf16[256,2048]{1,0:T(8,128)(2,1)S(1)} %get-tuple-element.89.refs_1_, bf16[2048,512]{1,0:T(8,128)(2,1)S(1)} %get-tuple-element.84.refs_2_.refs_4_, bf16[2048,512]{1,0:T(8,128)(2,1)S(1)} %get-tuple-element.85.refs_3_.refs_5_), custom_call_target="tpu_custom_call" | custom-call | flops 1 | bytes 1 | tf_op jit(solution)/shard_map/pallas_call | solution.py:277
  165.3 3.7 %shard_map.70 = (bf16[8,512,256]{2,1,0:T(8,128)(2,1)S(1)}, bf16[8,512,256]{2,1,0:T(8,128)(2,1)S(1)}) custom-call(s32[2]{0:T(128)S(1)} %pad_add_fusion.1.flag, f32[8,4,2,2,8,512]{5,4,3,2,1,0:T(8,128)} %bitcast.12.own, f32[8,4,2,2,8,512]{5,4,3,2,1,0:T(8,128)S(1)} %bitcast.38, f32[8,4,2,2,8,512]{5,4,3,2,1,0:T(8,128)} %bitcast.14.far, ...), custom_call_target="tpu_custom_call" | custom-call | flops 1 | bytes 1 | tf_op jit(solution)/shard_map/pallas_call | solution.py:197
  169.0 1.3 copy-done.2
  170.4 3.9 %shard_map.71.refs_0_ = f32[8,4,8,1024]{3,2,1,0:T(8,128)S(1)} custom-call(bf16[256,2048]{1,0:T(8,128)(2,1)S(1)} %get-tuple-element.88.refs_0_, bf16[256,2048]{1,0:T(8,128)(2,1)S(1)} %get-tuple-element.89.refs_1_, bf16[2048,512]{1,0:T(8,128)(2,1)S(1)} %copy-done.12, bf16[2048,512]{1,0:T(8,128)(2,1)S(1)} %copy-done.14, bf16[2048,512]{1,0:T(8,128)(2,1)S(1)} %copy-done.16, ...), custom_call_target="tpu_custom_call" | custom-call | flops 1 | bytes 1 | tf_op jit(solution)/shard_map/pallas_call | solution.py:277
  174.3 7.1 %collective-permute-done.14.refs_3_ = f32[8,8,2048]{2,1,0:T(8,128)} collective-permute-done((f32[8,8,2048]{2,1,0:T(8,128)}, f32[8,8,2048]{2,1,0:T(8,128)}, u32[]{:S(2)}, u32[]{:S(2)}) %collective-permute-start.14) | collective-permute-done | bytes 524320 | tf_op jit(solution)/shard_map/ppermute | solution.py:22
  181.4 2.1 shard_map.72
  183.5 3.7 %shard_map.73 = f32[8,4,8,1024]{3,2,1,0:T(8,128)S(1)} custom-call(bf16[256,2048]{1,0:T(8,128)(2,1)S(1)} %get-tuple-element.98.refs_0_, bf16[256,2048]{1,0:T(8,128)(2,1)S(1)} %get-tuple-element.99.refs_1_, bf16[2048,512]{1,0:T(8,128)(2,1)S(1)} %get-tuple-element.67.refs_2_, bf16[2048,512]{1,0:T(8,128)(2,1)S(1)} %copy-done.20, ...), custom_call_target="tpu_custom_call" | custom-call | flops 1 | bytes 1 | tf_op jit(solution)/shard_map/pallas_call | solution.py:277
  187.2 1.8 shard_map.75.refs_2_
  189.0 1.6 collective-permute-start.21
  191.0 1.8 shard_map.74.refs_1_
  196.6 13.7 %shard_map.78.refs_0_ = f32[1024,1024]{1,0:T(8,128)} custom-call(f32[1024,1024]{1,0:T(8,128)} %bitcast.57, bf16[8,512,256]{2,1,0:T(8,128)(2,1)S(1)} %get-tuple-element.68.refs_1_.refs_6_.refs_11_.refs_17_.refs_23_.refs_29_, bf16[8,512,256]{2,1,0:T(8,128)(2,1)S(1)} %get-tuple-element.100.refs_2_.refs_7_.refs_12_.refs_18_.refs_24_.refs_30_, ...), custom_call_target="tpu_custom_call" | custom-call | flops 1 | bytes 1 | tf_op jit(solution)/shard_map/pallas_call | solution.py:341
  210.3 4.7 %collective-permute-done.18.refs_0_ = f32[8,4,8,1024]{3,2,1,0:T(8,128)S(1)} collective-permute-done((f32[8,4,8,1024]{3,2,1,0:T(8,128)S(1)}, f32[8,4,8,1024]{3,2,1,0:T(8,128)S(1)}, u32[]{:S(2)}, u32[]{:S(2)}) %collective-permute-start.18) | collective-permute-done | bytes 1048608 | tf_op jit(solution)/shard_map/ppermute | solution.py:22
  215.0 1.3 collective-permute-start.24
  216.3 1.7 shard_map.76.refs_1_
  219.9 6.6 %shard_map.79 = f32[1024,1024]{1,0:T(8,128)} custom-call(f32[1024,1024]{1,0:T(8,128)} %shard_map.78.refs_0_, bf16[8,512,256]{2,1,0:T(8,128)(2,1)S(1)} %get-tuple-element.68.refs_1_.refs_6_.refs_11_.refs_17_.refs_23_.refs_29_, ...), custom_call_target="tpu_custom_call", output_to_operand_aliasing={{}: (0, {})} | custom-call | flops 1 | bytes 1 | tf_op jit(solution)/shard_map/pallas_call | solution.py:341
  (96 shorter events, 15.4 us)
Async XLA Ops:
  0.6 86.8 %copy-start = (s32[8,16]{1,0:T(8,128)S(1)}, s32[8,16]{1,0:T(8,128)}, u32[]{:S(2)}) copy-start(s32[8,16]{1,0:T(8,128)} %param.5) | copy-start | bytes 1540
  0.6 1.6 copy-start.27
  4.0 30.5 %all-to-all-start = ((f32[8,2,16,8,256]{4,3,2,1,0:T(8,128)}), f32[8,2,16,8,256]{4,3,2,1,0:T(8,128)S(1)}, u32[]{:S(2)}, u32[]{:S(2)}) async-start(f32[8,2,16,8,256]{4,3,2,1,0:T(8,128)} %copy-done.10), calls=%async_computation | async-start | bytes 4194304 | tf_op jit(solution)/shard_map/all_to_all | solution.py:414
  9.3 33.6 %collective-permute-start.2 = (f32[1024,1024]{1,0:T(8,128)}, f32[1024,1024]{1,0:T(8,128)}, u32[]{:S(2)}, u32[]{:S(2)}) collective-permute-start(f32[1024,1024]{1,0:T(8,128)} %bitcast.58), channel_id=1, source_target_pairs={{0,2},{2,0},{1,3},{3,1},{4,6},{6,4},{5,7},{7,5},{8,10},{10,8},{9,1... | collective-permute-start | bytes 12582920 | tf_op jit(solution)/shard_map/ppermute | solution.py:22
  34.5 51.5 %collective-permute-start.9 = (f32[1024,512]{1,0:T(8,128)}, f32[1024,512]{1,0:T(8,128)}, u32[]{:S(2)}, u32[]{:S(2)}) collective-permute-start(f32[1024,512]{1,0:T(8,128)} %get-tuple-element.64.a), channel_id=1, source_target_pairs={{0,1},{1,0},{2,3},{3,2},{4,5},{5,4},{6,7},{7,6},{8,9},{9,8},{10,11... | collective-permute-start | bytes 6291464 | tf_op jit(solution)/shard_map/ppermute | solution.py:22
  38.2 7.4 %copy-start.6 = (f32[1024,512]{1,0:T(8,128)S(1)}, f32[1024,512]{1,0:T(8,128)}, u32[]{:S(2)}) copy-start(f32[1024,512]{1,0:T(8,128)} %get-tuple-element.64.a) | copy-start | bytes 6291460
  38.2 47.8 %collective-permute-start.1 = (f32[8,16,8,256]{3,2,1,0:T(8,128)S(1)}, f32[8,16,8,256]{3,2,1,0:T(8,128)S(1)}, u32[]{:S(2)}, u32[]{:S(2)}) collective-permute-start(f32[8,16,8,256]{3,2,1,0:T(8,128)S(1)} %get-tuple-element.115), channel_id=1, source_target_pairs={{0,16},{16,0},{1,17},{17,1},{2,18},{18,2},{3,19},{19,3},{4,20},{20... | collective-permute-start | bytes 3145736 | tf_op jit(solution)/shard_map/ppermute | solution.py:22
  40.5 48.4 %collective-permute-start.3 = (f32[8,2,16,8,256]{4,3,2,1,0:T(8,128)S(1)}, f32[8,2,16,8,256]{4,3,2,1,0:T(8,128)}, u32[]{:S(2)}, u32[]{:S(2)}) collective-permute-start(f32[8,2,16,8,256]{4,3,2,1,0:T(8,128)S(1)} %all-to-all-done.refs_0_), channel_id=1, source_target_pairs={{0,2},{2,0},{1,3},{3,1},{4,6},{6,4},{5,7},{7,5},{8,10},{10,8},{9,1... | collective-permute-start | bytes 6291464 | tf_op jit(solution)/shard_map/ppermute | solution.py:22
  45.6 4.1 %copy-start.4 = (f32[1024,512]{1,0:T(8,128)}, f32[1024,512]{1,0:T(8,128)S(1)}, u32[]{:S(2)}) copy-start(f32[1024,512]{1,0:T(8,128)S(1)} %get-tuple-element.110.b) | copy-start | bytes 6291460
  86.0 13.1 %collective-permute-start.10 = (f32[1024,512]{1,0:T(8,128)}, f32[1024,512]{1,0:T(8,128)}, u32[]{:S(2)}, u32[]{:S(2)}) collective-permute-start(f32[1024,512]{1,0:T(8,128)} %collective-permute-done.9.a), channel_id=1, source_target_pairs={{0,2},{2,0},{1,3},{3,1},{4,6},{6,4},{5,7},{7,5},{8,10},{10,8},{9,1... | collective-permute-start | bytes 6291464 | tf_op jit(solution)/shard_map/ppermute | solution.py:22
  87.2 49.2 %collective-permute-start = (f32[1024,512]{1,0:T(8,128)}, f32[1024,512]{1,0:T(8,128)}, u32[]{:S(2)}, u32[]{:S(2)}) collective-permute-start(f32[1024,512]{1,0:T(8,128)} %get-tuple-element.86.a), channel_id=1, source_target_pairs={{0,1},{1,0},{2,3},{3,2},{4,5},{5,4},{6,7},{7,6},{8,9},{9,8},{10,11... | collective-permute-start | bytes 6291464 | tf_op jit(solution)/shard_map/ppermute | solution.py:22
  87.2 5.4 %collective-permute-start.4 = (f32[8,16,8,256]{3,2,1,0:T(8,128)S(1)}, f32[8,16,8,256]{3,2,1,0:T(8,128)}, u32[]{:S(2)}, u32[]{:S(2)}) collective-permute-start(f32[8,16,8,256]{3,2,1,0:T(8,128)S(1)} %collective-permute-done.1.refs_1_), channel_id=1, source_target_pairs={{0,2},{2,0},{1,3},{3,1},{4,6},{6,4},{5,7},{7,5},{8,10},{10,8},{9,1... | collective-permute-start | bytes 3145736 | tf_op jit(solution)/shard_map/ppermute | solution.py:22
  88.0 48.3 %collective-permute-start.8 = (f32[8,16,8,256]{3,2,1,0:T(8,128)}, f32[8,16,8,256]{3,2,1,0:T(8,128)}, u32[]{:S(2)}, u32[]{:S(2)}) collective-permute-start(f32[8,16,8,256]{3,2,1,0:T(8,128)} %get-tuple-element.63), channel_id=1, source_target_pairs={{0,16},{16,0},{1,17},{17,1},{2,18},{18,2},{3,19},{19,3},{4,20},{20... | collective-permute-start | bytes 3145736 | tf_op jit(solution)/shard_map/ppermute | solution.py:22
  97.6 38.8 %collective-permute-start.5 = (f32[8,8,2048]{2,1,0:T(8,128)}, f32[8,8,2048]{2,1,0:T(8,128)S(1)}, u32[]{:S(2)}, u32[]{:S(2)}) collective-permute-start(f32[8,8,2048]{2,1,0:T(8,128)} %get-tuple-element.60), channel_id=1, source_target_pairs={{0,4},{4,0},{8,12},{12,8},{1,5},{5,1},{9,13},{13,9},{2,6},{6,2},{1... | collective-permute-start | bytes 1572872 | tf_op jit(solution)/shard_map/ppermute | solution.py:22
  98.8 37.6 %collective-permute-start.6 = (f32[8,8,2048]{2,1,0:T(8,128)}, f32[8,8,2048]{2,1,0:T(8,128)S(1)}, u32[]{:S(2)}, u32[]{:S(2)}) collective-permute-start(f32[8,8,2048]{2,1,0:T(8,128)} %get-tuple-element.61), channel_id=1, source_target_pairs={{0,8},{4,12},{8,0},{12,4},{1,9},{5,13},{9,1},{13,5},{2,10},{6,14},... | collective-permute-start | bytes 1572872 | tf_op jit(solution)/shard_map/ppermute | solution.py:22
  99.1 45.6 %collective-permute-start.7 = (f32[8,8,2048]{2,1,0:T(8,128)}, f32[8,8,2048]{2,1,0:T(8,128)}, u32[]{:S(2)}, u32[]{:S(2)}) collective-permute-start(f32[8,8,2048]{2,1,0:T(8,128)} %get-tuple-element.62), channel_id=1, source_target_pairs={{0,12},{4,8},{8,4},{12,0},{1,13},{5,9},{9,5},{13,1},{2,14},{6,10},... | collective-permute-start | bytes 1572872 | tf_op jit(solution)/shard_map/ppermute | solution.py:22
  100.3 1.6 copy-start.7
  101.9 1.6 copy-start.9
  106.9 39.3 %copy-start.29 = (f32[8,8,2048]{2,1,0:T(8,128)S(1)}, f32[8,8,2048]{2,1,0:T(8,128)}, u32[]{:S(2)}) copy-start(f32[8,8,2048]{2,1,0:T(8,128)} %copy-done.28) | copy-start | bytes 1572868
  110.4 40.2 %copy-start.19 = (bf16[2048,512]{1,0:T(8,128)(2,1)}, bf16[2048,512]{1,0:T(8,128)(2,1)S(1)}, u32[]{:S(2)}) copy-start(bf16[2048,512]{1,0:T(8,128)(2,1)S(1)} %get-tuple-element.76.refs_3_) | copy-start | bytes 6291460
  144.7 13.8 %collective-permute-start.15 = (f32[1024,512]{1,0:T(8,128)}, f32[1024,512]{1,0:T(8,128)S(1)}, u32[]{:S(2)}, u32[]{:S(2)}) collective-permute-start(f32[1024,512]{1,0:T(8,128)} %collective-permute-done.a), channel_id=1, source_target_pairs={{0,2},{2,0},{1,3},{3,1},{4,6},{6,4},{5,7},{7,5},{8,10},{10,8},{9,1... | collective-permute-start | bytes 6291464 | tf_op jit(solution)/shard_map/ppermute | solution.py:22
  146.2 5.5 %collective-permute-start.11 = (f32[8,16,8,256]{3,2,1,0:T(8,128)}, f32[8,16,8,256]{3,2,1,0:T(8,128)S(1)}, u32[]{:S(2)}, u32[]{:S(2)}) collective-permute-start(f32[8,16,8,256]{3,2,1,0:T(8,128)} %collective-permute-done.8.refs_1_), channel_id=1, source_target_pairs={{0,2},{2,0},{1,3},{3,1},{4,6},{6,4},{5,7},{7,5},{8,10},{10,8},{9,1... | collective-permute-start | bytes 3145736 | tf_op jit(solution)/shard_map/ppermute | solution.py:22
  150.5 23.7 %collective-permute-start.16 = (f32[8,4,8,512]{3,2,1,0:T(8,128)}, f32[8,4,8,512]{3,2,1,0:T(8,128)S(1)}, u32[]{:S(2)}, u32[]{:S(2)}) collective-permute-start(f32[8,4,8,512]{3,2,1,0:T(8,128)} %shard_map.66), channel_id=1, source_target_pairs={{0,1},{1,0},{2,3},{3,2},{4,5},{5,4},{6,7},{7,6},{8,9},{9,8},{10,11... | collective-permute-start | bytes 1572872 | tf_op jit(solution)/shard_map/ppermute | solution.py:22
  155.8 18.5 %collective-permute-start.12 = (f32[8,8,2048]{2,1,0:T(8,128)}, f32[8,8,2048]{2,1,0:T(8,128)}, u32[]{:S(2)}, u32[]{:S(2)}) collective-permute-start(f32[8,8,2048]{2,1,0:T(8,128)} %get-tuple-element.79), channel_id=1, source_target_pairs={{0,4},{4,0},{8,12},{12,8},{1,5},{5,1},{9,13},{13,9},{2,6},{6,2},{1... | collective-permute-start | bytes 1572872 | tf_op jit(solution)/shard_map/ppermute | solution.py:22
  157.0 17.3 %collective-permute-start.13 = (f32[8,8,2048]{2,1,0:T(8,128)}, f32[8,8,2048]{2,1,0:T(8,128)}, u32[]{:S(2)}, u32[]{:S(2)}) collective-permute-start(f32[8,8,2048]{2,1,0:T(8,128)} %get-tuple-element.80), channel_id=1, source_target_pairs={{0,8},{4,12},{8,0},{12,4},{1,9},{5,13},{9,1},{13,5},{2,10},{6,14},... | collective-permute-start | bytes 1572872 | tf_op jit(solution)/shard_map/ppermute | solution.py:22
  157.0 24.4 %collective-permute-start.14 = (f32[8,8,2048]{2,1,0:T(8,128)}, f32[8,8,2048]{2,1,0:T(8,128)}, u32[]{:S(2)}, u32[]{:S(2)}) collective-permute-start(f32[8,8,2048]{2,1,0:T(8,128)} %get-tuple-element.81), channel_id=1, source_target_pairs={{0,12},{4,8},{8,4},{12,0},{1,13},{5,9},{9,5},{13,1},{2,14},{6,10},... | collective-permute-start | bytes 1572872 | tf_op jit(solution)/shard_map/ppermute | solution.py:22
  158.5 2.8 %copy-start.21 = (f32[1024,512]{1,0:T(8,128)}, f32[1024,512]{1,0:T(8,128)S(1)}, u32[]{:S(2)}) copy-start(f32[1024,512]{1,0:T(8,128)S(1)} %collective-permute-done.15.b) | copy-start | bytes 6291460
  161.4 2.6 %copy-start.23 = (bf16[2048,512]{1,0:T(8,128)(2,1)}, bf16[2048,512]{1,0:T(8,128)(2,1)S(1)}, u32[]{:S(2)}) copy-start(bf16[2048,512]{1,0:T(8,128)(2,1)S(1)} %get-tuple-element.84.refs_2_.refs_4_) | copy-start | bytes 6291460
  161.4 2.6 %copy-start.25 = (bf16[2048,512]{1,0:T(8,128)(2,1)}, bf16[2048,512]{1,0:T(8,128)(2,1)S(1)}, u32[]{:S(2)}) copy-start(bf16[2048,512]{1,0:T(8,128)(2,1)S(1)} %get-tuple-element.85.refs_3_.refs_5_) | copy-start | bytes 6291460
  161.4 3.2 %copy-start.5 = (f32[1024,512]{1,0:T(8,128)S(1)}, f32[1024,512]{1,0:T(8,128)}, u32[]{:S(2)}) copy-start(f32[1024,512]{1,0:T(8,128)} %copy-done.4) | copy-start | bytes 6291460
  161.4 3.9 %copy-start.22 = (f32[1024,512]{1,0:T(8,128)S(1)}, f32[1024,512]{1,0:T(8,128)}, u32[]{:S(2)}) copy-start(f32[1024,512]{1,0:T(8,128)} %copy-done.21) | copy-start | bytes 6291460
  164.0 17.4 %collective-permute-start.17 = (f32[8,4,8,512]{3,2,1,0:T(8,128)}, f32[8,4,8,512]{3,2,1,0:T(8,128)S(1)}, u32[]{:S(2)}, u32[]{:S(2)}) collective-permute-start(f32[8,4,8,512]{3,2,1,0:T(8,128)} %shard_map.69), channel_id=1, source_target_pairs={{0,1},{1,0},{2,3},{3,2},{4,5},{5,4},{6,7},{7,6},{8,9},{9,8},{10,11... | collective-permute-start | bytes 1572872 | tf_op jit(solution)/shard_map/ppermute | solution.py:22
  165.3 5.1 %copy-start.12 = (bf16[2048,512]{1,0:T(8,128)(2,1)S(1)}, bf16[2048,512]{1,0:T(8,128)(2,1)}, u32[]{:S(2)}) copy-start(bf16[2048,512]{1,0:T(8,128)(2,1)} %copy-done.11) | copy-start | bytes 6291460
  165.3 5.1 %copy-start.14 = (bf16[2048,512]{1,0:T(8,128)(2,1)S(1)}, bf16[2048,512]{1,0:T(8,128)(2,1)}, u32[]{:S(2)}) copy-start(bf16[2048,512]{1,0:T(8,128)(2,1)} %copy-done.13) | copy-start | bytes 6291460
  165.3 5.1 %copy-start.16 = (bf16[2048,512]{1,0:T(8,128)(2,1)S(1)}, bf16[2048,512]{1,0:T(8,128)(2,1)}, u32[]{:S(2)}) copy-start(bf16[2048,512]{1,0:T(8,128)(2,1)} %copy-done.15) | copy-start | bytes 6291460
  165.3 5.1 %copy-start.18 = (bf16[2048,512]{1,0:T(8,128)(2,1)S(1)}, bf16[2048,512]{1,0:T(8,128)(2,1)}, u32[]{:S(2)}) copy-start(bf16[2048,512]{1,0:T(8,128)(2,1)} %copy-done.17) | copy-start | bytes 6291460
  170.4 13.1 %copy-start.24 = (bf16[2048,512]{1,0:T(8,128)(2,1)S(1)}, bf16[2048,512]{1,0:T(8,128)(2,1)}, u32[]{:S(2)}) copy-start(bf16[2048,512]{1,0:T(8,128)(2,1)} %copy-done.23) | copy-start | bytes 6291460
  170.4 13.1 %copy-start.26 = (bf16[2048,512]{1,0:T(8,128)(2,1)S(1)}, bf16[2048,512]{1,0:T(8,128)(2,1)}, u32[]{:S(2)}) copy-start(bf16[2048,512]{1,0:T(8,128)(2,1)} %copy-done.25) | copy-start | bytes 6291460
  174.3 9.3 %copy-start.20 = (bf16[2048,512]{1,0:T(8,128)(2,1)S(1)}, bf16[2048,512]{1,0:T(8,128)(2,1)}, u32[]{:S(2)}) copy-start(bf16[2048,512]{1,0:T(8,128)(2,1)} %copy-done.19) | copy-start | bytes 6291460
  189.0 4.6 %collective-permute-start.21 = (f32[8,4,8,512]{3,2,1,0:T(8,128)S(1)}, f32[8,4,8,512]{3,2,1,0:T(8,128)S(1)}, u32[]{:S(2)}, u32[]{:S(2)}) collective-permute-start(f32[8,4,8,512]{3,2,1,0:T(8,128)S(1)} %shard_map.75.refs_2_), channel_id=1, source_target_pairs={{0,2},{2,0},{1,3},{3,1},{4,6},{6,4},{5,7},{7,5},{8,10},{10,8},{9,1... | collective-permute-start | bytes 1572872 | tf_op jit(solution)/shard_map/ppermute | solution.py:22
  190.6 6.0 %collective-permute-start.19 = (f32[8,4,8,1024]{3,2,1,0:T(8,128)S(1)}, f32[8,4,8,1024]{3,2,1,0:T(8,128)S(1)}, u32[]{:S(2)}, u32[]{:S(2)}) collective-permute-start(f32[8,4,8,1024]{3,2,1,0:T(8,128)S(1)} %shard_map.71.refs_0_), channel_id=1, source_target_pairs={{0,2},{2,0},{1,3},{3,1},{4,6},{6,4},{5,7},{7,5},{8,10},{10,8},{9,1... | collective-permute-start | bytes 3145736 | tf_op jit(solution)/shard_map/ppermute | solution.py:22
  190.7 24.3 %collective-permute-start.18 = (f32[8,4,8,1024]{3,2,1,0:T(8,128)S(1)}, f32[8,4,8,1024]{3,2,1,0:T(8,128)S(1)}, u32[]{:S(2)}, u32[]{:S(2)}) collective-permute-start(f32[8,4,8,1024]{3,2,1,0:T(8,128)S(1)} %shard_map.73), channel_id=1, source_target_pairs={{0,1},{1,0},{2,3},{3,2},{4,5},{5,4},{6,7},{7,6},{8,9},{9,8},{10,11... | collective-permute-start | bytes 3145736 | tf_op jit(solution)/shard_map/ppermute | solution.py:22
  192.8 2.3 %collective-permute-start.20 = (f32[8,4,8,512]{3,2,1,0:T(8,128)S(1)}, f32[8,4,8,512]{3,2,1,0:T(8,128)S(1)}, u32[]{:S(2)}, u32[]{:S(2)}) collective-permute-start(f32[8,4,8,512]{3,2,1,0:T(8,128)S(1)} %shard_map.74.refs_1_), channel_id=1, source_target_pairs={{0,2},{2,0},{1,3},{3,1},{4,6},{6,4},{5,7},{7,5},{8,10},{10,8},{9,1... | collective-permute-start | bytes 1572872 | tf_op jit(solution)/shard_map/ppermute | solution.py:22
  193.6 2.3 %collective-permute-start.22 = (f32[8,4,8,512]{3,2,1,0:T(8,128)S(1)}, f32[8,4,8,512]{3,2,1,0:T(8,128)S(1)}, u32[]{:S(2)}, u32[]{:S(2)}) collective-permute-start(f32[8,4,8,512]{3,2,1,0:T(8,128)S(1)} %collective-permute-done.16.refs_3_), channel_id=1, source_target_pairs={{0,2},{2,0},{1,3},{3,1},{4,6},{6,4},{5,7},{7,5},{8,10},{10,8},{9,1... | collective-permute-start | bytes 1572872 | tf_op jit(solution)/shard_map/ppermute | solution.py:22
  193.6 3.0 %collective-permute-start.23 = (f32[8,4,8,512]{3,2,1,0:T(8,128)S(1)}, f32[8,4,8,512]{3,2,1,0:T(8,128)S(1)}, u32[]{:S(2)}, u32[]{:S(2)}) collective-permute-start(f32[8,4,8,512]{3,2,1,0:T(8,128)S(1)} %collective-permute-done.17.refs_4_), channel_id=1, source_target_pairs={{0,2},{2,0},{1,3},{3,1},{4,6},{6,4},{5,7},{7,5},{8,10},{10,8},{9,1... | collective-permute-start | bytes 1572872 | tf_op jit(solution)/shard_map/ppermute | solution.py:22
  215.0 4.0 %collective-permute-start.24 = (f32[8,4,8,1024]{3,2,1,0:T(8,128)S(1)}, f32[8,4,8,1024]{3,2,1,0:T(8,128)S(1)}, u32[]{:S(2)}, u32[]{:S(2)}) collective-permute-start(f32[8,4,8,1024]{3,2,1,0:T(8,128)S(1)} %collective-permute-done.18.refs_0_), channel_id=1, source_target_pairs={{0,2},{2,0},{1,3},{3,1},{4,6},{6,4},{5,7},{7,5},{8,10},{10,8},{9,1... | collective-permute-start | bytes 3145736 | tf_op jit(solution)/shard_map/ppermute | solution.py:22
  218.0 2.0 copy-start.3
  219.9 6.6 %copy-start.1 = (s32[8,16]{1,0:T(8,128)S(1)}, s32[8,16]{1,0:T(8,128)}, u32[]{:S(2)}) copy-start(s32[8,16]{1,0:T(8,128)} %param.5) | copy-start | bytes 1540
  (8 other events, 10.2 us)
